TPU v7x, 256 devices: a whole 4x4x8 slice. The times are simulated.
256 devices in a mesh: tm: 8 (over y, x_hi), dp: 32 (over x_lo, z, core).
Axes of the slice: x: 4 (x_hi: 2, x_lo: 2; x = x_hi * 2 + x_lo), y: 4, z: 8, core: 2. Of those that a mesh axis runs over, the one named last changes fastest.
Arguments:
- history: bfloat16 [32, 16384, 256], P('dp', 'tm'), may hold values from -6 to 6
- now_weight: bfloat16 [256, 1024], replicated, may hold values from -0.25 to 0.25
- past_weight: bfloat16 [256, 1024], replicated, may hold values from -0.25 to 0.25
- gate_bias: float32 [1024], replicated, may hold values from -1 to 1
- residual_weight: bfloat16 [512, 256], replicated, may hold values from -0.25 to 0.25
- skip_weight: bfloat16 [512, 256], replicated, may hold values from -0.25 to 0.25
- out_cotangent: bfloat16 [32, 16384, 256], P('dp', 'tm'), may hold values from -6 to 6
- skip_cotangent: bfloat16 [32, 16384, 256], P('dp', 'tm'), may hold values from -6 to 6
Outputs:
- residual_out: bfloat16 [32, 16384, 256], P('dp', 'tm')
- skip_out: bfloat16 [32, 16384, 256], P('dp', 'tm')
- grad_input: bfloat16 [32, 16384, 256], P('dp', 'tm')
- grad_now: float32 [256, 1024], P('dp')
- grad_past: float32 [256, 1024], P('dp')
- grad_bias: float32 [1024], P('dp')
- grad_residual: float32 [512, 256], P('dp')
- skip_grad: float32 [512, 256], P('dp')
All inputs are finite; a program needn't handle non-finite values.
Results may differ from a plain program's by a relative error of at most 0.0048.
Values may be sent and summed in bfloat16 or wider, within the bound.
No kernel may reach another device: no remote copies, remote signals or barrier semaphores. Data moves between devices by JAX's collectives and lax.ppermute only.
A program may use at most 64 MiB of HBM per device.

v0:
```python
import jax
import jax.numpy as jnp
from jax import lax
from jax.sharding import PartitionSpec as P

DILATION_STEPS = 2048


def passed_along(value, axis, steps):
    count = lax.axis_size(axis)
    leading, last = (max(0, -steps), min(count, count - steps))
    return lax.ppermute(value, axis, [(source, source + steps) for source in range(leading, last)])


def contract_rows(left, right):
    return lax.dot_general(
        left, right, (((0,), (0,)), ((), ())), preferred_element_type=jnp.float32
    )


def shards(
    history,
    now_weight,
    past_weight,
    gate_bias,
    residual_weight,
    skip_weight,
    out_cotangent,
    skip_cotangent,
):
    histories, series_length, channels = history.shape
    gated_width = residual_weight.shape[0]
    total_rows = histories * series_length
    received_rows = passed_along(history, "tm", 1)
    lagged_input = jnp.concatenate(
        [received_rows, history[:, : series_length - DILATION_STEPS, :]], axis=1
    )
    power_series = history.reshape(total_rows, channels)
    delayed_flat = lagged_input.reshape(total_rows, channels)
    out_cot = out_cotangent.reshape(total_rows, channels)
    skip_cot = skip_cotangent.reshape(total_rows, channels)
    zeta = jnp.dot(power_series, now_weight, preferred_element_type=jnp.float32)
    zeta = zeta + jnp.dot(delayed_flat, past_weight, preferred_element_type=jnp.float32) + gate_bias
    tanh_part = jnp.tanh(zeta[:, :gated_width])
    sigm_part = jax.nn.sigmoid(zeta[:, gated_width:])
    gated = (tanh_part * sigm_part).astype(jnp.bfloat16)
    resid = (
        power_series.astype(jnp.float32)
        + jnp.dot(gated, residual_weight, preferred_element_type=jnp.float32)
    ).astype(jnp.bfloat16)
    skipped = jnp.dot(gated, skip_weight, preferred_element_type=jnp.float32).astype(jnp.bfloat16)
    dgated = jnp.dot(out_cot, residual_weight.T, preferred_element_type=jnp.float32)
    dgated = dgated + jnp.dot(skip_cot, skip_weight.T, preferred_element_type=jnp.float32)
    dzeta = jnp.concatenate(
        [
            dgated * sigm_part * (1.0 - tanh_part * tanh_part),
            dgated * tanh_part * sigm_part * (1.0 - sigm_part),
        ],
        axis=1,
    ).astype(jnp.bfloat16)
    dzeta_seq = dzeta.reshape(histories, series_length, 2 * gated_width)
    reverse_pass = jnp.einsum(
        "btk,ck->btc", dzeta_seq, past_weight, preferred_element_type=jnp.float32
    ).astype(jnp.bfloat16)
    came = passed_along(reverse_pass, "tm", -1)
    local_slice = reverse_pass[:, DILATION_STEPS:, :]
    shifted_rows = jnp.concatenate([local_slice, came], axis=1).reshape(total_rows, channels)
    shifted_rows = lax.optimization_barrier(shifted_rows).astype(jnp.float32)
    grad_in = (
        out_cot.astype(jnp.float32)
        + jnp.dot(dzeta, now_weight.T, preferred_element_type=jnp.float32)
        + shifted_rows
    )
    grad_in = grad_in.astype(jnp.bfloat16)
    partials = (
        contract_rows(power_series, dzeta),
        contract_rows(delayed_flat, dzeta),
        jnp.sum(dzeta.astype(jnp.float32), axis=0),
        contract_rows(gated, out_cot),
        contract_rows(gated, skip_cot),
    )
    summed = lax.psum((partials[0], partials[1], partials[2], partials[3], partials[4]), "tm")
    totals = (
        lax.psum_scatter(summed[0], "dp", scatter_dimension=0, tiled=True),
        lax.psum_scatter(summed[1], "dp", scatter_dimension=0, tiled=True),
        lax.psum_scatter(summed[2], "dp", scatter_dimension=0, tiled=True),
        lax.psum_scatter(summed[3], "dp", scatter_dimension=0, tiled=True),
        lax.psum_scatter(summed[4], "dp", scatter_dimension=0, tiled=True),
    )
    shape_out = (histories, series_length, channels)
    return (
        resid.reshape(shape_out),
        skipped.reshape(shape_out),
        grad_in.reshape(shape_out),
        totals[0],
        totals[1],
        totals[2],
        totals[3],
        totals[4],
    )


def solution(mesh):
    in_specs = (
        P("dp", "tm", None),
        P(),
        P(),
        P(),
        P(),
        P(),
        P("dp", "tm", None),
        P("dp", "tm", None),
    )
    out_specs = (
        P("dp", "tm", None),
        P("dp", "tm", None),
        P("dp", "tm", None),
        P("dp", None),
        P("dp", None),
        P("dp"),
        P("dp", None),
        P("dp", None),
    )
    return jax.shard_map(shards, mesh=mesh, in_specs=in_specs, out_specs=out_specs, check_vma=False)
```

profile of v0, /device:TPU:64, one launch (start us, length us, event | category | flops | bytes accessed | tf_op | source)
XLA Modules:
  0.0 621.9 jit_solution(12741490128602185852)
XLA Ops:
  7.2 0.0 copy-start
  7.2 0.0 copy-start.7
  7.2 0.0 copy-start.10
  7.2 0.0 reduce-scatter.15.cloned.1.call-start
  7.3 5.1 collective-permute-start
  12.4 2.0 fusion.13
  14.4 0.0 copy-done.7
  14.4 0.0 copy-done.10
  14.4 0.0 copy-start.9
  14.4 0.0 copy-start.13
  14.4 1.3 fusion.18
  15.7 0.0 copy-start.14
  15.8 19.3 %collective-permute-done = bf16[1,2048,256]{2,1,0:T(8,128)(2,1)S(1)} collective-permute-done((bf16[1,2048,256]{2,1,0:T(8,128)(2,1)}, bf16[1,2048,256]{2,1,0:T(8,128)(2,1)S(1)}, u32[]{:S(2)}, u32[]{:S(2)}) %collective-permute-start) | collective-permute-done | bytes 1048608 | tf_op jit(solution)/shard_map/ppermute | solution.py:12
  35.0 0.0 copy-done.9
  35.0 0.0 copy-done.13
  35.0 1.5 add_add_fusion
  36.5 0.0 copy-done
  36.5 0.0 copy-done.14
  36.5 3.9 multiply_convert_fusion.1
  40.5 1.3 copy-done.4
  41.8 2.2 convolution_bitcast_fusion
  44.1 2.6 copy.22
  46.7 0.0 reduce-scatter.15.cloned.1.call-update
  46.7 0.0 reduce-scatter.13.cloned.1.call-start
  46.7 4.1 convolution_bitcast_fusion.1
  50.8 2.6 copy.20
  53.5 0.0 reduce-scatter.13.cloned.1.call-update
  53.5 0.0 reduce-scatter.11.cloned.1.call-start
  53.5 3.1 fusion.8
  56.6 0.0 reduce-scatter.11.cloned.1.call-update
  56.7 0.0 reduce-scatter.9.cloned.1.call-start
  56.7 0.6 dynamic-slice
  58.0 4.1 fusion.4
  62.1 1.4 collective-permute-start.1
  63.5 2.2 convert_reduce_fusion
  65.8 48.9 %all-reduce = f32[1024]{0:T(1024)S(1)} all-reduce(f32[1024]{0:T(1024)S(1)} %convert_reduce_fusion), channel_id=4, replica_groups=mesh['tm'=8,'dp'=32] {'dp'}, use_global_device_ids=true, to_apply=%region_6.0.clone | all-reduce | flops 1024 | bytes 8192
  114.6 0.6 dynamic-slice.1
  115.2 3.1 fusion.11
  118.4 0.0 reduce-scatter.9.cloned.1.call-update
  118.4 0.2 all-reduce.4.cloned.1.call-start
  118.6 3.5 fusion.5
  122.1 0.0 copy-done.16
  122.1 0.0 copy-start.3
  122.1 0.0 copy-start.6
  122.1 0.0 copy-start.11
  122.2 1.8 fusion.6
  123.9 0.8 copy-done.6
  124.7 0.1 copy-done.11
  124.8 2.7 convolution_add_fusion.2
  127.5 0.0 collective-permute-done.1
  127.5 31.1 %reduce-scatter.15.cloned.1.call-done = f32[8,1024]{1,0:T(8,128)} async-done(((f32[256,1024]{1,0:T(8,128)}), f32[8,1024]{1,0:T(8,128)}) %reduce-scatter.15.cloned.1.call-update) | async-done | bytes 32784
  158.7 1.8 copy.23
  160.5 114.8 %reduce-scatter.13.cloned.1.call-done = f32[8,1024]{1,0:T(8,128)} async-done(((f32[256,1024]{1,0:T(8,128)}), f32[8,1024]{1,0:T(8,128)}) %reduce-scatter.13.cloned.1.call-update) | async-done | bytes 32784
  275.3 1.8 copy.21
  277.0 112.5 %reduce-scatter.11.cloned.1.call-done = f32[16,256]{1,0:T(8,128)} async-done(((f32[512,256]{1,0:T(8,128)}), f32[16,256]{1,0:T(8,128)}) %reduce-scatter.11.cloned.1.call-update) | async-done | bytes 16400 | tf_op jit(solution)/shard_map/reduce_scatter | solution.py:88
  389.6 113.9 %reduce-scatter.9.cloned.1.call-done = f32[16,256]{1,0:T(8,128)} async-done(((f32[512,256]{1,0:T(8,128)}), f32[16,256]{1,0:T(8,128)}) %reduce-scatter.9.cloned.1.call-update) | async-done | bytes 16400 | tf_op jit(solution)/shard_map/reduce_scatter | solution.py:87
  503.5 0.0 all-reduce.4.cloned.1.call-update
  503.5 3.1 fusion.7
  506.6 101.3 %all-reduce.4.cloned.1.call-done = (f32[8,1024]{0,1:T(8,128)}, f32[8,1024]{0,1:T(8,128)}, f32[32]{0:T(128)}, f32[16,256]{1,0:T(8,128)}, f32[16,256]{1,0:T(8,128)}) async-done(((f32[8,1024]{0,1:T(8,128)}, f32[8,1024]{0,1:T(8,128)}, f32[32]{0:T(128)}, f32[16,256]{1,0:T(8,128)}, f32[16,256]{1,0:T(8,128)}), (f32[8,1024]{0,1:T(8,128)}, f32[8,1024]{0,1:T(8,128)}, f32[32]{0:T(128)}, f32[16,256]{1,0:T(8,128)}, ...) | async-done | bytes 98448 | tf_op jit(solution)/shard_map/psum | solution.py:82
  607.9 1.8 copy.18
  609.7 1.8 copy.19
  611.6 1.1 copy.29
  612.7 1.3 copy.30
  614.0 1.3 copy.31
  (15 shorter events, 0.0 us)
Async XLA Ops:
  7.2 29.4 %copy-start = (bf16[1,2048,256]{2,1,0:T(8,128)(2,1)S(1)}, bf16[1,2048,256]{2,1,0:T(8,128)(2,1)}, u32[]{:S(2)}) copy-start(bf16[1,2048,256]{2,1,0:T(8,128)(2,1)} %param.15) | copy-start | bytes 3145732
  7.2 7.2 %copy-start.7 = (bf16[1,2048,256]{2,1,0:T(8,128)(2,1)S(1)}, bf16[1,2048,256]{2,1,0:T(8,128)(2,1)}, u32[]{:S(2)}) copy-start(bf16[1,2048,256]{2,1,0:T(8,128)(2,1)} %param.8) | copy-start | bytes 3145732
  7.2 7.2 %copy-start.10 = (bf16[256,1024]{1,0:T(8,128)(2,1)S(1)}, bf16[256,1024]{1,0:T(8,128)(2,1)}, u32[]{:S(2)}) copy-start(bf16[256,1024]{1,0:T(8,128)(2,1)} %param.9) | copy-start | bytes 1572868
  7.2 151.5 %reduce-scatter.15.cloned.1.call-start = ((), (), s32[]{:S(2)}) async-start(), calls=%async_computation.7 | async-start | bytes 1081344
  7.3 27.8 %collective-permute-start = (bf16[1,2048,256]{2,1,0:T(8,128)(2,1)}, bf16[1,2048,256]{2,1,0:T(8,128)(2,1)S(1)}, u32[]{:S(2)}, u32[]{:S(2)}) collective-permute-start(bf16[1,2048,256]{2,1,0:T(8,128)(2,1)} %param.8), channel_id=1, source_target_pairs={{0,32},{32,64},{64,96},{96,128},{128,160},{160,192},{192,224},{1,3... | collective-permute-start | bytes 3145736 | tf_op jit(solution)/shard_map/ppermute | solution.py:12
  14.4 20.6 %copy-start.9 = (bf16[256,1024]{1,0:T(8,128)(2,1)S(1)}, bf16[256,1024]{1,0:T(8,128)(2,1)}, u32[]{:S(2)}) copy-start(bf16[256,1024]{1,0:T(8,128)(2,1)} %param.10) | copy-start | bytes 1572868
  14.4 20.6 %copy-start.13 = (f32[1024]{0:T(1024)S(1)}, f32[1024]{0:T(1024)}, u32[]{:S(2)}) copy-start(f32[1024]{0:T(1024)} %param.11) | copy-start | bytes 12292
  15.7 20.8 %copy-start.14 = (bf16[512,256]{1,0:T(8,128)(2,1)S(1)}, bf16[512,256]{1,0:T(8,128)(2,1)}, u32[]{:S(2)}) copy-start(bf16[512,256]{1,0:T(8,128)(2,1)} %param.13) | copy-start | bytes 786436
  40.5 1.3 copy-start.4
  40.5 17.5 %copy-start.2 = (bf16[2048,512]{0,1:T(8,128)(2,1)}, bf16[2048,512]{0,1:T(8,128)(2,1)S(1)}, u32[]{:S(2)}) copy-start(bf16[2048,512]{0,1:T(8,128)(2,1)S(1)} %get-tuple-element.29) | copy-start | bytes 6291460
  46.7 228.6 %reduce-scatter.13.cloned.1.call-start = ((), (), s32[]{:S(2)}) async-start(), calls=%async_computation.6 | async-start | bytes 1081344
  50.8 5.9 copy-start.15
  53.5 336.1 %reduce-scatter.11.cloned.1.call-start = ((), (), s32[]{:S(2)}) async-start(), calls=%async_computation.5 | async-start | bytes 540672 | tf_op jit(solution)/shard_map/reduce_scatter | solution.py:88
  56.7 446.8 %reduce-scatter.9.cloned.1.call-start = ((), (), s32[]{:S(2)}) async-start(), calls=%async_computation.4 | async-start | bytes 540672 | tf_op jit(solution)/shard_map/reduce_scatter | solution.py:87
  58.0 5.6 copy-start.5
  62.1 53.1 %copy-start.1 = (bf16[1,2048,256]{2,1,0:T(8,128)(2,1)S(1)}, bf16[1,2048,256]{2,1,0:T(8,128)(2,1)}, u32[]{:S(2)}) copy-start(bf16[1,2048,256]{2,1,0:T(8,128)(2,1)} %param.14) | copy-start | bytes 3145732
  62.1 65.4 %collective-permute-start.1 = (bf16[1,2048,256]{2,1,0:T(8,128)(2,1)}, bf16[1,2048,256]{2,1,0:T(8,128)(2,1)}, u32[]{:S(2)}, u32[]{:S(2)}) collective-permute-start(bf16[1,2048,256]{2,1,0:T(8,128)(2,1)} %fusion.4), channel_id=1, source_target_pairs={{32,0},{64,32},{96,64},{128,96},{160,128},{192,160},{224,192},{33,... | collective-permute-start | bytes 3145736 | tf_op jit(solution)/shard_map/ppermute | solution.py:12
  118.4 3.8 copy-start.8
  118.4 3.8 copy-start.12
  118.4 489.5 %all-reduce.4.cloned.1.call-start = ((), (), s32[]{:S(2)}) async-start(), calls=%async_computation.8 | async-start | bytes 2163712 | tf_op jit(solution)/shard_map/psum | solution.py:82
  118.6 3.5 copy-start.16
  122.1 1.8 copy-start.3
  122.1 2.6 copy-start.6
  122.1 2.7 copy-start.11
Sparse Core Ops, SparseCore 0:
  46.8 111.8 reduce-scatter.14
  161.3 113.9 reduce-scatter.12
  277.8 111.7 reduce-scatter.10
  392.1 111.3 reduce-scatter.8
  506.9 100.9 all-reduce.3
where the time goes:
time: 623 us; the launch traced here: 622 us
  waiting for transfers between devices  493 us (79%)
  blocking collectives  48.9 us (8%)
  matrix products  33.4 us (5%)
  local copies, waits for them, and re-layouts  19.7 us (3%)
  between operations  14.6 us (2%)
  starting transfers between devices  6.92 us (1%)
    unnamed x7, waiting for transfers between devices  146 us
    reduce_scatter x1, waiting for transfers between devices, shards(): lax.psum_scatter(summed[3], 'dp', scatter_dimension=0, tiled=True)  114 us
    reduce_scatter x1, waiting for transfers between devices, shards(): lax.psum_scatter(summed[4], 'dp', scatter_dimension=0, tiled=True)  113 us
    psum x1, waiting for transfers between devices, shards(): lax.psum((partials[0], partials[1], partials[2], partials[3], partials[4]...  101 us
    unnamed x1, blocking collectives  48.9 us
    unnamed x45, local copies, waits for them, and re-layouts  19.7 us
    ppermute x2, waiting for transfers between devices, passed_along(): lax.ppermute(value, axis, [(source, source + steps) for source in range(l...  19.3 us
    dot_general x4, matrix products, contract_rows(): lax.dot_general(left, right, (((0,), (0,)), ((), ())), preferred_element_...  12.6 us
  transfers between devices with their start and end apart: 7, of which 6 were waited for; matrix products, arithmetic and copies ran while one was open for 6% of the time, Pallas kernels for 0%

commit v1 on v0

v1 whole, which is shorter than its diff:
```python
import functools

import jax
import jax.numpy as jnp
from jax import lax
from jax.experimental import pallas as pl
from jax.experimental.pallas import tpu as pltpu
from jax.sharding import PartitionSpec as P

BF16, F32 = jnp.bfloat16, jnp.float32
TILE = 512
CHUNKS = (1024, 1024)
LANES = 128
CHIP_GROUPS = [[chip * 2 + core for chip in range(16)] for core in range(2)]


def dot(a, b):
    return jnp.dot(a, b, preferred_element_type=F32)


def rows_dot(a, b):
    return lax.dot_general(a, b, (((0,), (0,)), ((), ())), preferred_element_type=F32)


def layer_kernel(first, last, core, h, d, oc, sk, taps, bias, heads, heads_t, taps_t, *rest):
    n_in = 2 if first else 5
    outs = rest if first else rest[n_in:]
    if first:
        res, skip, part, back, g_taps, g_heads, g_bias = rest
    elif last:
        in_taps, in_heads, in_bias, _, _ = rest[:5]
        res, skip, part, back, send, keep, g_taps, g_heads, g_bias = rest[5:]
    width = h.shape[1]
    gated_width = 2 * width
    step = pl.program_id(0)

    @pl.when(step == 0)
    def _():
        if first:
            g_taps[...] = jnp.zeros_like(g_taps)
            g_heads[...] = jnp.zeros_like(g_heads)
            g_bias[...] = jnp.zeros_like(g_bias)
        else:
            g_taps[...] = in_taps[...]
            g_heads[...] = in_heads[...]
            g_bias[...] = in_bias[...]

    both = jnp.concatenate([h[...], d[...]], axis=1)
    cots = jnp.concatenate([oc[...], sk[...]], axis=1)
    z = dot(both, taps[...]) + bias[...]
    th = jnp.tanh(z[:, :gated_width])
    sg = 0.5 * jnp.tanh(0.5 * z[:, gated_width:]) + 0.5
    ts = th * sg
    gated = ts.astype(BF16)
    heads_out = dot(gated, heads[...])
    res[...] = (h[...].astype(F32) + heads_out[:, :width]).astype(BF16)
    skip[...] = heads_out[:, width:].astype(BF16)
    dg = dot(cots, heads_t[...])
    dza = dg * (sg - ts * th)
    dzb = dg * (ts - ts * sg)
    dz = jnp.concatenate([dza.astype(BF16), dzb.astype(BF16)], axis=1)
    down = dot(dz, taps_t[...])
    part[...] = oc[...].astype(F32) + down[:, :width]
    back[...] = down[:, width:].astype(BF16)
    g_taps[...] += rows_dot(both, dz)
    g_heads[...] += rows_dot(gated, cots)
    g_bias[...] += jnp.sum(dz.astype(F32).reshape(-1, 8, 2 * gated_width), axis=0)

    if last:

        @pl.when(step == pl.num_programs(0) - 1)
        def _():
            mine = core[0]
            for out, side in ((send, 1 - mine), (keep, mine)):
                for j in range(16):
                    r = pl.multiple_of((2 * j + side) * 8, 8)
                    rr = pl.multiple_of((2 * j + side) * 16, 16)
                    pieces = (
                        g_taps[pl.ds(r, 8), :],
                        g_taps[pl.ds(width + r, 8), :],
                        g_heads[pl.ds(rr, 8), :width],
                        g_heads[pl.ds(rr + 8, 8), :width],
                        g_heads[pl.ds(rr, 8), width:],
                        g_heads[pl.ds(rr + 8, 8), width:],
                        g_bias[:, (j // 2) * LANES : (j // 2 + 1) * LANES],
                    )
                    at = 0
                    for piece in pieces:
                        out[j, :, at : at + piece.shape[1]] = piece.astype(out.dtype)
                        at += piece.shape[1]


def layer(core, h, d, oc, sk, weights, base, rows, total, carry):
    first, last = base == 0, base + rows == total
    width = h.shape[1]
    tile = min(TILE, rows)
    off = base // tile
    taps, bias, heads, heads_t, taps_t = weights
    whole = pl.BlockSpec((tile, width), lambda i: (off + i, 0))
    own = pl.BlockSpec((tile, width), lambda i: (i, 0))
    const = lambda a: pl.BlockSpec(a.shape, lambda i: (0,) * len(a.shape))
    shape = lambda s, t: jax.ShapeDtypeStruct(s, t)
    ins = [core, h, d, oc, sk, taps, bias, heads, heads_t, taps_t]
    in_specs = [pl.BlockSpec(memory_space=pltpu.SMEM), whole, own, whole, whole]
    in_specs += [const(a) for a in ins[5:]]
    out_shape = [
        shape((total, width), BF16),
        shape((total, width), BF16),
        shape((rows, width), F32),
        shape((rows, width), BF16),
    ]
    out_specs = [whole, whole, own, own]
    sums = [shape((2 * width, 4 * width), F32), shape((2 * width, 2 * width), F32), shape((8, 4 * width), F32)]
    scratch, aliases = [], {}
    if first:
        out_shape += sums
        out_specs += [const(s) for s in sums]
    else:
        ins += list(carry)
        in_specs += [const(s) for s in sums] + [pl.BlockSpec(memory_space=pl.ANY)] * 2
        aliases = {13: 0, 14: 1}
        packed = (16, 8, 12 * width + LANES)
        out_shape += [shape(packed, BF16), shape(packed, F32)]
        out_specs += [const(s) for s in out_shape[4:]]
        scratch = [pltpu.VMEM(s.shape, F32) for s in sums]
    flops = 2 * rows * width * width * 36
    return pl.pallas_call(
        functools.partial(layer_kernel, first, last),
        out_shape=out_shape,
        grid=(rows // tile,),
        in_specs=in_specs,
        out_specs=out_specs,
        scratch_shapes=scratch,
        input_output_aliases=aliases,
        compiler_params=pltpu.CompilerParams(
            dimension_semantics=("arbitrary",), vmem_limit_bytes=50 << 20
        ),
        cost_estimate=pl.CostEstimate(
            flops=flops, bytes_accessed=rows * width * 20 + (6 << 20), transcendentals=4 * rows * width
        ),
        name="layer_rows",
    )(*ins)


def shift(value, steps):
    n = lax.axis_size("tm")
    return lax.ppermute(
        value, "tm", [(s, s + steps) for s in range(max(0, -steps), min(n, n - steps))]
    )


def shards(history, now_w, past_w, gate_bias, res_w, skip_w, out_cot, skip_cot):
    _, total, width = history.shape
    h, oc, sk = history[0], out_cot[0], skip_cot[0]
    dp = lax.axis_index("dp")
    core = jnp.reshape(dp % 2, (1,)).astype(jnp.int32)
    taps = jnp.concatenate([now_w, past_w], axis=0)
    heads = jnp.concatenate([res_w, skip_w], axis=1)
    weights = (taps, gate_bias[None, :], heads, heads.T, taps.T)

    bases = [sum(CHUNKS[:k]) for k in range(len(CHUNKS))]
    delayed = [shift(h[b : b + r], 1) for b, r in zip(bases, CHUNKS)]
    carry, parts, backs = None, [], []
    for b, r, d in zip(bases, CHUNKS, delayed):
        out = layer(core, h, d, oc, sk, weights, b, r, total, carry)
        res, skip, part, back = out[:4]
        parts.append(part)
        backs.append(shift(back, -1))
        carry = (*out[4:], res, skip)
    send, keep = out[4:]

    came = lax.ppermute(send, "dp", [(i, i ^ 1) for i in range(32)])
    pair = (keep + came.astype(F32)).astype(BF16)
    spread = lax.all_to_all(pair, "dp", 0, 0, axis_index_groups=CHIP_GROUPS)
    mine = jnp.sum(spread.astype(F32), axis=0)
    for k in (1, 2, 4):
        mine = mine + lax.ppermute(mine, "tm", [(i, i ^ k) for i in range(8)])

    grad_in = jnp.concatenate([p + b.astype(F32) for p, b in zip(parts, backs)], axis=0)
    g_now, g_past = mine[:, : 4 * width], mine[:, 4 * width : 8 * width]
    at = [8 * width + k * width for k in range(5)]
    tops = [mine[:, a : a + width] for a in at[:4]]
    g_res = jnp.concatenate(tops[:2], axis=0)
    g_skip = jnp.concatenate(tops[2:], axis=0)
    bias_sum = jnp.sum(mine[:, at[4] :], axis=0)
    g_bias = lax.dynamic_slice(bias_sum, ((dp % 4) * 32,), (32,))
    return (
        res[None],
        skip[None],
        grad_in.astype(BF16)[None],
        g_now,
        g_past,
        g_bias,
        g_res,
        g_skip,
    )


def solution(mesh):
    rows, whole = P("dp", "tm", None), P()
    return jax.shard_map(
        shards,
        mesh=mesh,
        in_specs=(rows, whole, whole, whole, whole, whole, rows, rows),
        out_specs=(rows, rows, rows, P("dp", None), P("dp", None), P("dp"), P("dp", None), P("dp", None)),
        check_vma=False,
    )
```

time: 623 us -> 114 us (0.18)
  waiting for transfers between devices: 493 us -> 38.1 us
  blocking collectives: 48.9 us -> 0 us
  matrix products: 33.4 us -> 0 us
  starting transfers between devices: 6.92 us -> 29.7 us
  Pallas kernels: 0 us -> 20.1 us
  between operations: 14.6 us -> 0.84 us
  local copies, waits for them, and re-layouts: 19.7 us -> 12.9 us
    reduce_scatter x2 -> x0, waiting for transfers between devices: 226 us -> none  [the longest x1 114 us: shards(): lax.psum_scatter(summed[3], 'dp', scatter_dimension=0, tiled=True)]
    unnamed x7 -> x0, waiting for transfers between devices: 146 us -> none
    psum x1 -> x0, waiting for transfers between devices: 101 us -> none  [shards(): lax.psum((partials[0], partials[1], partials[2], partials[3], partials[4]...]
    unnamed x1 -> x0, blocking collectives: 48.9 us -> none
    dot_general x12 -> x0, matrix products: 33.4 us -> none  [the longest x4 12.6 us: contract_rows(): lax.dot_general(left, right, (((0,), (0,)), ((), ())), preferred_element_...]
    pallas_call x0 -> x2, Pallas kernels: none -> 20.1 us  [layer(): pl.pallas_call(functools.partial(layer_kernel, first, last), out_shape=ou...]
    all_to_all x0 -> x1, waiting for transfers between devices: none -> 17.7 us  [shards(): spread = lax.all_to_all(pair, 'dp', 0, 0, axis_index_groups=CHIP_GROUPS)]
    ppermute x2 -> x8, starting transfers between devices: 6.54 us -> 21.6 us  [the longest x4 11 us: shift(): lax.ppermute(value, 'tm', [(s, s + steps) for s in range(max(0, -steps),...]
  transfers between devices with their start and end apart: 7 -> 9, of which waited for: 6 -> 6; matrix products, arithmetic and copies ran while one was open for 6% -> 10% of each run, Pallas kernels for 0% -> 9%
where the time goes in v1:
time: 114 us; the launch traced here: 112 us
  waiting for transfers between devices  38.1 us (33%)
  starting transfers between devices  29.7 us (26%)
  Pallas kernels  20.1 us (18%)
  local copies, waits for them, and re-layouts  12.9 us (11%)
  other arithmetic  9.86 us (9%)
    pallas_call x2, Pallas kernels, layer(): pl.pallas_call(functools.partial(layer_kernel, first, last), out_shape=ou...  20.1 us
    all_to_all x1, waiting for transfers between devices, shards(): spread = lax.all_to_all(pair, 'dp', 0, 0, axis_index_groups=CHIP_GROUPS)  17.7 us
    ppermute x3, waiting for transfers between devices, shards(): mine = mine + lax.ppermute(mine, 'tm', [(i, i ^ k) for i in range(8)])  14.9 us
    ppermute x4, starting transfers between devices, shift(): lax.ppermute(value, 'tm', [(s, s + steps) for s in range(max(0, -steps),...  11 us
    ppermute x3, starting transfers between devices, shards(): mine = mine + lax.ppermute(mine, 'tm', [(i, i ^ k) for i in range(8)])  10.6 us
    all_to_all x1, starting transfers between devices, shards(): spread = lax.all_to_all(pair, 'dp', 0, 0, axis_index_groups=CHIP_GROUPS)  8.17 us
    unnamed x32, local copies, waits for them, and re-layouts  6.71 us
    concatenate x3, other arithmetic, shards(): jnp.concatenate([p + b.astype(F32) for p, b in zip(parts, backs)], axis=0)  3.35 us
  transfers between devices with their start and end apart: 9, of which 6 were waited for; matrix products, arithmetic and copies ran while one was open for 10% of the time, Pallas kernels for 9%

profile of v1, /device:TPU:64, one launch (start us, length us, event | category | flops | bytes accessed | tf_op | source)
XLA Modules:
  0.0 111.5 jit_solution(5264368925630513991)
XLA Ops:
  0.6 0.0 copy-start.12
  0.6 0.0 copy-start.13
  0.7 0.0 copy-start.10
  0.7 0.0 copy-start.11
  0.7 2.4 %slice_bitcast_fusion = (bf16[1024,256]{1,0:T(8,128)(2,1)}, bf16[1024,256]{1,0:T(8,128)(2,1)}) fusion(bf16[1,2048,256]{2,1,0:T(8,128)(2,1)} %param.8), kind=kLoop, calls=%fused_computation.9 | loop fusion | bytes 2097152 | tf_op jit(solution)/shard_map/slice | solution.py:162
  3.0 4.9 %collective-permute-start.1 = (bf16[1024,256]{1,0:T(8,128)(2,1)}, bf16[1024,256]{1,0:T(8,128)(2,1)S(1)}, u32[]{:S(2)}, u32[]{:S(2)}) collective-permute-start(bf16[1024,256]{1,0:T(8,128)(2,1)} %get-tuple-element.34), channel_id=1, source_target_pairs={{0,32},{32,64},{64,96},{96,128},{128,160},{160,192},{192,224},{1,3... | collective-permute-start | bytes 1572872 | tf_op jit(solution)/shard_map/ppermute | solution.py:147
  8.0 3.4 %collective-permute-start = (bf16[1024,256]{1,0:T(8,128)(2,1)}, bf16[1024,256]{1,0:T(8,128)(2,1)S(1)}, u32[]{:S(2)}, u32[]{:S(2)}) collective-permute-start(bf16[1024,256]{1,0:T(8,128)(2,1)} %get-tuple-element.35), channel_id=1, source_target_pairs={{0,32},{32,64},{64,96},{96,128},{128,160},{160,192},{192,224},{1,3... | collective-permute-start | bytes 1572872 | tf_op jit(solution)/shard_map/ppermute | solution.py:147
  11.4 0.0 copy-done.12
  11.4 0.1 copy.20
  11.6 0.0 copy-done.13
  11.6 0.8 copy.21
  12.4 0.0 copy-done.10
  12.4 0.2 copy.18
  12.7 0.0 copy-done.11
  12.7 0.2 copy.19
  12.9 0.0 copy-start.9
  12.9 1.1 fusion.3
  14.0 0.0 copy-done.9
  14.0 0.0 copy-start.8
  14.0 0.9 fusion.2
  14.9 1.3 %copy.25.heads = bf16[512,512]{1,0:T(8,128)(2,1)S(1)} copy(bf16[512,512]{0,1:T(8,128)(2,1)} %get-tuple-element.39) | data formatting | bytes 1048576 | tf_op jit(solution)/shard_map/concatenate | solution.py:158
  16.1 1.3 %copy.24.taps = bf16[512,1024]{1,0:T(8,128)(2,1)} copy(bf16[512,1024]{0,1:T(8,128)(2,1)S(1)} %get-tuple-element.37) | data formatting | bytes 2097152 | tf_op jit(solution)/shard_map/concatenate | solution.py:157
  17.5 3.1 %collective-permute-done.1.d = bf16[1024,256]{1,0:T(8,128)(2,1)S(1)} collective-permute-done((bf16[1024,256]{1,0:T(8,128)(2,1)}, bf16[1024,256]{1,0:T(8,128)(2,1)S(1)}, u32[]{:S(2)}, u32[]{:S(2)}) %collective-permute-start.1) | collective-permute-done | bytes 524320 | tf_op jit(solution)/shard_map/ppermute | solution.py:147
  20.6 0.0 copy-start.6
  20.6 0.8 copy-done.6
  21.4 0.0 copy-done.8
  21.4 0.0 copy-start.7
  21.4 1.0 copy-done.7
  22.4 9.6 %layer_rows.2 = (bf16[2048,256]{1,0:T(8,128)(2,1)}, bf16[2048,256]{1,0:T(8,128)(2,1)}, f32[1024,256]{1,0:T(8,128)S(1)}, bf16[1024,256]{1,0:T(8,128)(2,1)S(1)}, f...) custom-call(s32[1]{0:T(128)} %bitcast.core, bf16[2048,256]{1,0:T(8,128)(2,1)} %bitcast.21, ...), custom_call_target="tpu_custom_call" | custom-call | flops 4831838208 | bytes 11534336 | tf_op jit(solution)/shard_map/layer_rows/pallas_call | solution.py:127
  32.0 0.0 copy-start
  32.0 0.8 copy-done
  32.8 0.0 collective-permute-done.d
  32.8 0.0 copy-start.4
  32.8 0.8 copy-done.4
  33.6 0.0 copy-start.5
  33.6 1.0 copy-done.5
  34.7 10.5 %layer_rows.3 = (bf16[2048,256]{1,0:T(8,128)(2,1)}, bf16[2048,256]{1,0:T(8,128)(2,1)}, f32[1024,256]{1,0:T(8,128)S(1)}, bf16[1024,256]{1,0:T(8,128)(2,1)S(1)}, b...) custom-call(s32[1]{0:T(128)} %bitcast.core, ...), custom_call_target="tpu_custom_call", output_to_operand_aliasing={{0}: (13, {}), {1}: (14, {})} | custom-call | flops 4831838208 | bytes 11534336 | tf_op jit(solution)/shard_map/layer_rows/pallas_call | solution.py:127
  45.2 0.0 copy-start.2
  45.2 0.8 copy-done.2
  46.0 0.0 collective-permute-start.4
  46.0 2.3 %collective-permute-done.4 = bf16[16,8,3200]{2,1,0:T(8,128)(2,1)S(1)} collective-permute-done((bf16[16,8,3200]{2,1,0:T(8,128)(2,1)S(1)}, bf16[16,8,3200]{2,1,0:T(8,128)(2,1)S(1)}, u32[]{:S(2)}, u32[]{:S(2)}) %collective-permute-start.4) | collective-permute-done | bytes 819232 | tf_op jit(solution)/shard_map/ppermute | solution.py:172
  48.4 0.0 copy-start.3
  48.4 2.6 %add_convert_fusion = bf16[16,8,3200]{2,1,0:T(8,128)(2,1)} fusion(f32[16,8,3200]{2,1,0:T(8,128)} %get-tuple-element.32, bf16[16,8,3200]{2,1,0:T(8,128)(2,1)S(1)} %collective-permute-done.4), kind=kLoop, calls=%fused_computation.1 | loop fusion | flops 1228800 | bytes 3276800 | tf_op jit(solution)/shard_map/convert_element_type | solution.py:173
  51.0 8.2 %all-to-all-start = ((bf16[16,8,3200]{2,1,0:T(8,128)(2,1)}), bf16[16,8,3200]{2,1,0:T(8,128)(2,1)}, u32[]{:S(2)}, u32[]{:S(2)}) async-start(bf16[16,8,3200]{2,1,0:T(8,128)(2,1)} %add_convert_fusion), calls=%async_computation | async-start | bytes 1638400 | tf_op jit(solution)/shard_map/all_to_all | solution.py:174
  59.1 0.0 copy-done.3
  59.1 1.3 %collective-permute-start.3 = (bf16[1024,256]{1,0:T(8,128)(2,1)S(1)}, bf16[1024,256]{1,0:T(8,128)(2,1)}, u32[]{:S(2)}, u32[]{:S(2)}) collective-permute-start(bf16[1024,256]{1,0:T(8,128)(2,1)S(1)} %copy-done.3), channel_id=1, source_target_pairs={{32,0},{64,32},{96,64},{128,96},{160,128},{192,160},{224,192},{33,... | collective-permute-start | bytes 1572872 | tf_op jit(solution)/shard_map/ppermute | solution.py:147
  60.4 0.0 copy-done.1
  60.4 1.3 %collective-permute-start.2 = (bf16[1024,256]{1,0:T(8,128)(2,1)S(1)}, bf16[1024,256]{1,0:T(8,128)(2,1)}, u32[]{:S(2)}, u32[]{:S(2)}) collective-permute-start(bf16[1024,256]{1,0:T(8,128)(2,1)S(1)} %copy-done.1), channel_id=1, source_target_pairs={{32,0},{64,32},{96,64},{128,96},{160,128},{192,160},{224,192},{33,... | collective-permute-start | bytes 1572872 | tf_op jit(solution)/shard_map/ppermute | solution.py:147
  61.8 17.7 %all-to-all-done = bf16[16,8,3200]{2,1,0:T(8,128)(2,1)} async-done(((bf16[16,8,3200]{2,1,0:T(8,128)(2,1)}), bf16[16,8,3200]{2,1,0:T(8,128)(2,1)}, u32[]{:S(2)}, u32[]{:S(2)}) %all-to-all-start) | async-done | bytes 819232 | tf_op jit(solution)/shard_map/all_to_all | solution.py:174
  79.4 1.3 %convert_reduce_fusion = f32[8,3200]{1,0:T(8,128)S(1)} fusion(bf16[16,8,3200]{2,1,0:T(8,128)(2,1)} %all-to-all-done), kind=kLoop, calls=%fused_computation | loop fusion | flops 793600 | bytes 921600 | tf_op jit(solution)/shard_map/reduce_sum | solution.py:175
  80.7 4.6 %collective-permute-start.5 = (f32[8,3200]{1,0:T(8,128)S(1)}, f32[8,3200]{1,0:T(8,128)S(1)}, u32[]{:S(2)}, u32[]{:S(2)}) collective-permute-start(f32[8,3200]{1,0:T(8,128)S(1)} %convert_reduce_fusion), channel_id=1, source_target_pairs={{0,32},{32,0},{64,96},{96,64},{128,160},{160,128},{192,224},{224,1... | collective-permute-start | bytes 307208 | tf_op jit(solution)/shard_map/ppermute | solution.py:177
  85.3 0.0 collective-permute-done.3
  85.3 1.2 %fusion.1 = bf16[1,1024,256]{2,1,0:T(8,128)(2,1)S(1)} fusion(f32[1024,256]{1,0:T(8,128)S(1)} %get-tuple-element.30, bf16[1024,256]{1,0:T(8,128)(2,1)} %collective-permute-done.3), kind=kLoop, calls=%fused_computation.7 | loop fusion | flops 786432 | bytes 2097152 | tf_op jit(solution)/shard_map/concatenate | solution.py:179
  86.4 11.3 %collective-permute-done.5 = f32[8,3200]{1,0:T(8,128)S(1)} collective-permute-done((f32[8,3200]{1,0:T(8,128)S(1)}, f32[8,3200]{1,0:T(8,128)S(1)}, u32[]{:S(2)}, u32[]{:S(2)}) %collective-permute-start.5) | collective-permute-done | bytes 102432 | tf_op jit(solution)/shard_map/ppermute | solution.py:177
  97.8 2.6 %collective-permute-start.6 = (f32[8,3200]{1,0:T(8,128)S(1)}, f32[8,3200]{1,0:T(8,128)S(1)}, u32[]{:S(2)}, u32[]{:S(2)}) collective-permute-start(f32[8,3200]{1,0:T(8,128)S(1)} %add.32), channel_id=1, source_target_pairs={{0,64},{32,96},{64,0},{96,32},{128,192},{160,224},{192,128},{224,1... | collective-permute-start | bytes 307208 | tf_op jit(solution)/shard_map/ppermute | solution.py:177
  100.4 0.0 collective-permute-done.2
  100.4 1.2 %fusion = bf16[1,1024,256]{2,1,0:T(8,128)(2,1)S(1)} fusion(f32[1024,256]{1,0:T(8,128)S(1)} %get-tuple-element.28, bf16[1024,256]{1,0:T(8,128)(2,1)} %collective-permute-done.2), kind=kLoop, calls=%fused_computation.6 | loop fusion | flops 786432 | bytes 2097152 | tf_op jit(solution)/shard_map/concatenate | solution.py:179
  101.5 1.9 %collective-permute-done.6 = f32[8,3200]{1,0:T(8,128)S(1)} collective-permute-done((f32[8,3200]{1,0:T(8,128)S(1)}, f32[8,3200]{1,0:T(8,128)S(1)}, u32[]{:S(2)}, u32[]{:S(2)}) %collective-permute-start.6) | collective-permute-done | bytes 102432 | tf_op jit(solution)/shard_map/ppermute | solution.py:177
  103.4 3.4 %collective-permute-start.7 = (f32[8,3200]{1,0:T(8,128)S(1)}, f32[8,3200]{1,0:T(8,128)S(1)}, u32[]{:S(2)}, u32[]{:S(2)}) collective-permute-start(f32[8,3200]{1,0:T(8,128)S(1)} %add.33), channel_id=1, source_target_pairs={{0,128},{32,160},{64,192},{96,224},{128,0},{160,32},{192,64},{224,... | collective-permute-start | bytes 307208 | tf_op jit(solution)/shard_map/ppermute | solution.py:177
  106.9 1.0 pad_maximum_fusion.1
  107.9 1.8 %collective-permute-done.7 = f32[8,3200]{1,0:T(8,128)S(1)} collective-permute-done((f32[8,3200]{1,0:T(8,128)S(1)}, f32[8,3200]{1,0:T(8,128)S(1)}, u32[]{:S(2)}, u32[]{:S(2)}) %collective-permute-start.7) | collective-permute-done | bytes 102432 | tf_op jit(solution)/shard_map/ppermute | solution.py:177
  109.7 0.6 fusion.5
  110.3 0.6 dynamic_slice.3
  110.9 0.6 pad_maximum_fusion.3
  (6 shorter events, 0.1 us)
Async XLA Ops:
  0.6 10.8 %copy-start.12 = (bf16[512,256]{1,0:T(8,128)(2,1)S(1)}, bf16[512,256]{1,0:T(8,128)(2,1)}, u32[]{:S(2)}) copy-start(bf16[512,256]{1,0:T(8,128)(2,1)} %param.12) | copy-start | bytes 786436
  0.6 10.9 %copy-start.13 = (bf16[512,256]{1,0:T(8,128)(2,1)S(1)}, bf16[512,256]{1,0:T(8,128)(2,1)}, u32[]{:S(2)}) copy-start(bf16[512,256]{1,0:T(8,128)(2,1)} %param.13) | copy-start | bytes 786436
  0.7 11.8 %copy-start.10 = (bf16[256,1024]{1,0:T(8,128)(2,1)S(1)}, bf16[256,1024]{1,0:T(8,128)(2,1)}, u32[]{:S(2)}) copy-start(bf16[256,1024]{1,0:T(8,128)(2,1)} %param.9) | copy-start | bytes 1572868
  0.7 12.0 %copy-start.11 = (bf16[256,1024]{1,0:T(8,128)(2,1)S(1)}, bf16[256,1024]{1,0:T(8,128)(2,1)}, u32[]{:S(2)}) copy-start(bf16[256,1024]{1,0:T(8,128)(2,1)} %param.10) | copy-start | bytes 1572868
  3.0 17.5 %collective-permute-start.1 = (bf16[1024,256]{1,0:T(8,128)(2,1)}, bf16[1024,256]{1,0:T(8,128)(2,1)S(1)}, u32[]{:S(2)}, u32[]{:S(2)}) collective-permute-start(bf16[1024,256]{1,0:T(8,128)(2,1)} %get-tuple-element.34), channel_id=1, source_target_pairs={{0,32},{32,64},{64,96},{96,128},{128,160},{160,192},{192,224},{1,3... | collective-permute-start | bytes 1572872 | tf_op jit(solution)/shard_map/ppermute | solution.py:147
  8.0 24.8 %collective-permute-start = (bf16[1024,256]{1,0:T(8,128)(2,1)}, bf16[1024,256]{1,0:T(8,128)(2,1)S(1)}, u32[]{:S(2)}, u32[]{:S(2)}) collective-permute-start(bf16[1024,256]{1,0:T(8,128)(2,1)} %get-tuple-element.35), channel_id=1, source_target_pairs={{0,32},{32,64},{64,96},{96,128},{128,160},{160,192},{192,224},{1,3... | collective-permute-start | bytes 1572872 | tf_op jit(solution)/shard_map/ppermute | solution.py:147
  12.9 1.1 %copy-start.9 = (bf16[512,256]{0,1:T(8,128)(2,1)S(1)}, bf16[512,256]{0,1:T(8,128)(2,1)}, u32[]{:S(2)}) copy-start(bf16[512,256]{0,1:T(8,128)(2,1)} %copy.21) | copy-start | bytes 786436
  14.0 7.4 %copy-start.8 = (f32[1024]{0:T(1024)S(1)}, f32[1024]{0:T(1024)}, u32[]{:S(2)}) copy-start(f32[1024]{0:T(1024)} %param.11) | copy-start | bytes 12292
  20.6 0.8 copy-start.6
  21.4 1.0 copy-start.7
  32.0 0.8 copy-start
  32.8 0.8 copy-start.4
  33.6 1.0 copy-start.5
  45.2 0.8 copy-start.2
  46.0 2.3 %collective-permute-start.4 = (bf16[16,8,3200]{2,1,0:T(8,128)(2,1)S(1)}, bf16[16,8,3200]{2,1,0:T(8,128)(2,1)S(1)}, u32[]{:S(2)}, u32[]{:S(2)}) collective-permute-start(bf16[16,8,3200]{2,1,0:T(8,128)(2,1)S(1)} %get-tuple-element.33), channel_id=1, source_target_pairs={{0,1},{1,0},{2,3},{3,2},{4,5},{5,4},{6,7},{7,6},{8,9},{9,8},{10,11... | collective-permute-start | bytes 2457608 | tf_op jit(solution)/shard_map/ppermute | solution.py:172
  48.4 10.8 %copy-start.3 = (bf16[1024,256]{1,0:T(8,128)(2,1)S(1)}, bf16[1024,256]{1,0:T(8,128)(2,1)}, u32[]{:S(2)}) copy-start(bf16[1024,256]{1,0:T(8,128)(2,1)} %copy-done.2) | copy-start | bytes 1572868
  48.4 12.1 %copy-start.1 = (bf16[1024,256]{1,0:T(8,128)(2,1)S(1)}, bf16[1024,256]{1,0:T(8,128)(2,1)}, u32[]{:S(2)}) copy-start(bf16[1024,256]{1,0:T(8,128)(2,1)} %copy-done) | copy-start | bytes 1572868
  51.0 28.5 %all-to-all-start = ((bf16[16,8,3200]{2,1,0:T(8,128)(2,1)}), bf16[16,8,3200]{2,1,0:T(8,128)(2,1)}, u32[]{:S(2)}, u32[]{:S(2)}) async-start(bf16[16,8,3200]{2,1,0:T(8,128)(2,1)} %add_convert_fusion), calls=%async_computation | async-start | bytes 1638400 | tf_op jit(solution)/shard_map/all_to_all | solution.py:174
  59.1 26.1 %collective-permute-start.3 = (bf16[1024,256]{1,0:T(8,128)(2,1)S(1)}, bf16[1024,256]{1,0:T(8,128)(2,1)}, u32[]{:S(2)}, u32[]{:S(2)}) collective-permute-start(bf16[1024,256]{1,0:T(8,128)(2,1)S(1)} %copy-done.3), channel_id=1, source_target_pairs={{32,0},{64,32},{96,64},{128,96},{160,128},{192,160},{224,192},{33,... | collective-permute-start | bytes 1572872 | tf_op jit(solution)/shard_map/ppermute | solution.py:147
  60.4 39.9 %collective-permute-start.2 = (bf16[1024,256]{1,0:T(8,128)(2,1)S(1)}, bf16[1024,256]{1,0:T(8,128)(2,1)}, u32[]{:S(2)}, u32[]{:S(2)}) collective-permute-start(bf16[1024,256]{1,0:T(8,128)(2,1)S(1)} %copy-done.1), channel_id=1, source_target_pairs={{32,0},{64,32},{96,64},{128,96},{160,128},{192,160},{224,192},{33,... | collective-permute-start | bytes 1572872 | tf_op jit(solution)/shard_map/ppermute | solution.py:147
  80.7 17.0 %collective-permute-start.5 = (f32[8,3200]{1,0:T(8,128)S(1)}, f32[8,3200]{1,0:T(8,128)S(1)}, u32[]{:S(2)}, u32[]{:S(2)}) collective-permute-start(f32[8,3200]{1,0:T(8,128)S(1)} %convert_reduce_fusion), channel_id=1, source_target_pairs={{0,32},{32,0},{64,96},{96,64},{128,160},{160,128},{192,224},{224,1... | collective-permute-start | bytes 307208 | tf_op jit(solution)/shard_map/ppermute | solution.py:177
  97.8 5.6 %collective-permute-start.6 = (f32[8,3200]{1,0:T(8,128)S(1)}, f32[8,3200]{1,0:T(8,128)S(1)}, u32[]{:S(2)}, u32[]{:S(2)}) collective-permute-start(f32[8,3200]{1,0:T(8,128)S(1)} %add.32), channel_id=1, source_target_pairs={{0,64},{32,96},{64,0},{96,32},{128,192},{160,224},{192,128},{224,1... | collective-permute-start | bytes 307208 | tf_op jit(solution)/shard_map/ppermute | solution.py:177
  103.4 6.3 %collective-permute-start.7 = (f32[8,3200]{1,0:T(8,128)S(1)}, f32[8,3200]{1,0:T(8,128)S(1)}, u32[]{:S(2)}, u32[]{:S(2)}) collective-permute-start(f32[8,3200]{1,0:T(8,128)S(1)} %add.33), channel_id=1, source_target_pairs={{0,128},{32,160},{64,192},{96,224},{128,0},{160,32},{192,64},{224,... | collective-permute-start | bytes 307208 | tf_op jit(solution)/shard_map/ppermute | solution.py:177

commit v2 on v0

v2 whole, which is shorter than its diff:
```python
import functools

import jax
import jax.numpy as jnp
from jax import lax
from jax.experimental import pallas as pl
from jax.experimental.pallas import tpu as pltpu
from jax.sharding import PartitionSpec as P

BF16, F32 = jnp.bfloat16, jnp.float32
TILE = 512
CHUNKS = (1024, 1024)
LANES = 128
VMEM = pl.BlockSpec(memory_space=pltpu.VMEM)


def dot(a, b):
    return jnp.dot(a, b, preferred_element_type=F32)


def dot_t(a, b):
    return lax.dot_general(a, b, (((1,), (1,)), ((), ())), preferred_element_type=F32)


def dot_rows(a, b):
    return lax.dot_general(a, b, (((0,), (0,)), ((), ())), preferred_element_type=F32)


def tile_rows(base=0):
    return pl.ds(pl.multiple_of(base + pl.program_id(0) * TILE, TILE), TILE)


def before_kernel(h, oc, sk, now_w, bias, res_w, skip_w, z_now, dg):
    rows = tile_rows()
    z_now[rows, :] = dot(h[rows, :], now_w[...]) + bias[...]
    dg[rows, :] = dot_t(oc[rows, :], res_w[...]) + dot_t(sk[rows, :], skip_w[...])


def gates(base, h, d, oc, sk, z_now, dg, past_w, g_taps, g_heads, g_bias):
    rows = tile_rows(base)
    delayed = d[tile_rows(), :]
    z = z_now[rows, :] + dot(delayed, past_w[...])
    half = z.shape[1] // 2
    th = jnp.tanh(z[:, :half])
    sg = 0.5 * jnp.tanh(0.5 * z[:, half:]) + 0.5
    ts = th * sg
    gated = ts.astype(BF16)
    dgated = dg[rows, :]
    dza = dgated * (sg - ts * th)
    dzb = dgated * (ts - ts * sg)
    dz = jnp.concatenate([dza.astype(BF16), dzb.astype(BF16)], axis=1)
    g_taps[...] += dot_rows(jnp.concatenate([h[rows, :], delayed], axis=1), dz)
    g_heads[...] += dot_rows(gated, jnp.concatenate([oc[rows, :], sk[rows, :]], axis=1))
    g_bias[...] += jnp.sum(dz.astype(F32).reshape(-1, 8, 2 * half), axis=0)
    return gated, dz


def results(base, gated, dz, h, oc, now_w, past_w, res_w, skip_w, res, skip, part, back):
    rows = tile_rows(base)
    res[...] = (h[rows, :].astype(F32) + dot(gated, res_w[...])).astype(BF16)
    skip[...] = dot(gated, skip_w[...]).astype(BF16)
    part[...] = oc[rows, :].astype(F32) + dot_t(dz, now_w[...])
    back[...] = dot_t(dz, past_w[...]).astype(BF16)


def first_kernel(h, d, oc, sk, z_now, dg, now_w, past_w, res_w, skip_w, *outs):
    res, skip, part, back, g_taps, g_heads, g_bias = outs

    @pl.when(pl.program_id(0) == 0)
    def _():
        for g in (g_taps, g_heads, g_bias):
            g[...] = jnp.zeros_like(g)

    gated, dz = gates(0, h, d, oc, sk, z_now, dg, past_w, g_taps, g_heads, g_bias)
    results(0, gated, dz, h, oc, now_w, past_w, res_w, skip_w, res, skip, part, back)


def last_kernel(base, place, h, d, oc, sk, z_now, dg, past_w, *rest):
    gated, dz, send, keep, g_taps, g_heads, g_bias = rest[3:]
    rows = tile_rows()
    gated[rows, :], dz[rows, :] = gates(
        base, h, d, oc, sk, z_now, dg, past_w, g_taps, g_heads, g_bias
    )
    width = h.shape[1]

    @pl.when(pl.program_id(0) == pl.num_programs(0) - 1)
    def _():
        mine = place[0]
        for out, side in ((send, 1 - mine), (keep, mine)):
            for chip in range(16):
                x_lo, z = divmod(chip, 8)
                r = pl.multiple_of((2 * chip + side) * 8, 8)
                rr = pl.multiple_of((2 * chip + side) * 16, 16)
                pieces = (
                    g_taps[pl.ds(r, 8), :],
                    g_taps[pl.ds(width + r, 8), :],
                    g_heads[pl.ds(rr, 8), :width],
                    g_heads[pl.ds(rr + 8, 8), :width],
                    g_heads[pl.ds(rr, 8), width:],
                    g_heads[pl.ds(rr + 8, 8), width:],
                    g_bias[:, (chip // 2) * LANES : (chip // 2 + 1) * LANES],
                )
                at = 0
                for piece in pieces:
                    out[z % 2, z // 2, x_lo, :, at : at + piece.shape[1]] = piece.astype(out.dtype)
                    at += piece.shape[1]


def by_core_kernel(place, keep, came, keep_next, send_next):
    for out, odd in ((keep_next, place[1]), (send_next, 1 - place[1])):
        out[...] = (keep[odd] + came[odd].astype(F32)).astype(out.dtype)


def by_pair_kernel(place, keep, came, *outs):
    for k, out in enumerate(outs):
        at = lax.rem(place[2] + k, 4)
        out[...] = (keep[at] + came[at].astype(F32)).astype(out.dtype)


def total_of(own, one, two, three):
    return (own.astype(F32) + two.astype(F32)) + (one.astype(F32) + three.astype(F32))


def by_z_kernel(place, own, one, two, three, same, other):
    for out, at in ((same, place[3]), (other, 1 - place[3])):
        out[...] = total_of(own[at], one[at], two[at], three[at])


def by_x_kernel(own, one, two, three, out):
    out[...] = total_of(own[...], one[...], two[...], three[...])


def owner_kernel(place, own, one, two, three, g_now, g_past, g_res, g_skip, g_bias):
    width = g_res.shape[1]
    total = lambda at, n: total_of(*(a[:, at : at + n] for a in (own, one, two, three)))
    g_now[...] = total(0, 4 * width)
    g_past[...] = total(4 * width, 4 * width)
    for k in range(2):
        g_res[8 * k : 8 * k + 8, :] = total((8 + k) * width, width)
        g_skip[8 * k : 8 * k + 8, :] = total((10 + k) * width, width)
    sums = jnp.sum(total(12 * width, LANES), axis=0, keepdims=True)
    for m in range(4):

        @pl.when(place[4] == m)
        def _():
            g_bias[...] = sums[:, m * 32 : (m + 1) * 32]


def after_kernel(base, gated, dz, h, oc, now_w, past_w, res_w, skip_w, *rest):
    rows = tile_rows()
    results(base, gated[rows, :], dz[rows, :], h, oc, now_w, past_w, res_w, skip_w, *rest[4:])


def finish_kernel(part, came, out):
    out[...] = (part[...] + came[...].astype(F32)).astype(BF16)


def call(body, name, steps, ins, in_specs, outs, out_specs, flops, aliases={}):
    return pl.pallas_call(
        body,
        out_shape=[kind(s, t) for s, t, *_ in outs for kind in [pltpu.HBM if _ else jax.ShapeDtypeStruct]],
        grid=(steps,),
        in_specs=in_specs,
        out_specs=out_specs,
        input_output_aliases=aliases,
        compiler_params=pltpu.CompilerParams(
            dimension_semantics=("arbitrary",), vmem_limit_bytes=24 << 20
        ),
        cost_estimate=pl.CostEstimate(flops=flops, bytes_accessed=flops >> 9, transcendentals=0),
        name=name,
    )(*ins)


def in_hbm(value):
    return pltpu.with_memory_space_constraint(value, pltpu.HBM)


def shift(value, steps):
    n = lax.axis_size("tm")
    return lax.ppermute(
        value, "tm", [(s, s + steps) for s in range(max(0, -steps), min(n, n - steps))]
    )


def exchange(value, axis, partner):
    return lax.ppermute(value, axis, [(i, partner(i)) for i in range(lax.axis_size(axis))])


def along_z(value, target):
    return exchange(value, "dp", lambda i: i // 16 * 16 + target(i // 2 % 8) * 2 + i % 2)


def along_y(value, k):
    return exchange(value, "tm", lambda i: (i + 2 * k) % 8)


def along_x(value, k):
    def target(i):
        x = (i // 32 % 2 * 2 + i % 32 // 16 + k) % 4
        return i // 64 * 64 + x // 2 * 32 + x % 2 * 16 + i % 16

    return lax.ppermute(value, ("tm", "dp"), [(i, target(i)) for i in range(256)])


def shards(history, now_w, past_w, gate_bias, res_w, skip_w, out_cot, skip_cot):
    _, total, width = history.shape
    h, oc, sk = history[0], out_cot[0], skip_cot[0]
    dp = lax.axis_index("dp")
    z = (dp // 2) % 8
    place = jnp.stack([dp % 2, z % 2, z // 2, dp // 16, dp % 4]).astype(jnp.int32)
    first, last = CHUNKS
    macs = 2 * total * width * width

    h_first = h[:first]
    h, h_first = lax.optimization_barrier((h, h_first))
    d_first = shift(h_first, 1)
    d_last = shift(h[first:], 1)

    z_now, dg = call(
        before_kernel,
        "before",
        total // TILE,
        (h, oc, sk, now_w, gate_bias[None, :], res_w, skip_w),
        [VMEM] * 7,
        [((total, 4 * width), F32), ((total, 2 * width), F32)],
        [VMEM] * 2,
        macs * 8,
    )
    sums = [((2 * width, 4 * width), F32), ((2 * width, 2 * width), F32), ((8, 4 * width), F32)]
    rows_out = [
        ((total, width), BF16),
        ((total, width), BF16),
        ((total, width), F32, 1),
        ((total, width), BF16, 1),
    ]
    block = lambda base: pl.BlockSpec((TILE, width), lambda i: (base // TILE + i, 0))
    *outs, g_taps, g_heads, g_bias = call(
        first_kernel,
        "first",
        first // TILE,
        (h, d_first, oc, sk, z_now, dg, now_w, past_w, res_w, skip_w),
        [VMEM] * 10,
        rows_out + sums,
        [block(0)] * 4 + [VMEM] * 3,
        macs * 28 * first // total,
    )
    block_shape = (8, 12 * width + LANES)
    packed = (2, 4, 2, *block_shape)
    gated, dz, send, keep, *_ = call(
        functools.partial(last_kernel, first),
        "last",
        last // TILE,
        (place, h, d_last, oc, sk, z_now, dg, past_w, g_taps, g_heads, g_bias),
        [pl.BlockSpec(memory_space=pltpu.SMEM)] + [VMEM] * 10,
        [((last, 2 * width), BF16), ((last, 4 * width), BF16), (packed, BF16), (packed, F32)] + sums,
        [VMEM] * 7,
        macs * 16 * last // total,
        {8: 4, 9: 5, 10: 6},
    )
    came = exchange(send, "dp", lambda i: i ^ 1)
    res, skip, part, back = call(
        functools.partial(after_kernel, first),
        "after",
        last // TILE,
        (gated, dz, h, oc, now_w, past_w, res_w, skip_w, *outs),
        [VMEM] * 8 + [pl.BlockSpec(memory_space=pl.ANY)] * 4,
        rows_out,
        [block(first)] * 4,
        macs * 12 * last // total,
        {8: 0, 9: 1, 10: 2, 11: 3},
    )
    came, back = lax.optimization_barrier((came, back))
    smem = pl.BlockSpec(memory_space=pltpu.SMEM)
    step = lambda body, name, ins, outs: call(
        body, name, 1, ins, [smem] * (ins[0] is place) + [VMEM] * (len(ins) - (ins[0] is place)), outs,
        [VMEM] * len(outs), 1 << 20,
    )
    keep, send = step(by_core_kernel, "by_core", (place, keep, came), [(packed[1:], F32), (packed[1:], BF16)])
    came = along_z(send, lambda z: z ^ 1)
    own, *others = step(
        by_pair_kernel, "by_pair", (place, keep, came), [(packed[2:], F32)] + [(packed[2:], BF16)] * 3
    )
    one, two, three = (along_z(v, lambda z, k=k: (z + 2 * k) % 8) for k, v in enumerate(others, 1))
    (grad_in,) = call(
        finish_kernel,
        "finish",
        total // TILE,
        (part, shift(back, -1)),
        [block(0)] * 2,
        [((total, width), BF16)],
        [block(0)],
        macs * 1000,
    )
    own, one, two, three, grad_in = lax.optimization_barrier((own, one, two, three, grad_in))
    same, other = step(
        by_z_kernel, "by_z", (place, own, one, two, three), [(block_shape, F32)] * 2
    )
    (mine,) = step(
        by_x_kernel, "by_x", (same, along_x(other, 1), along_x(same, 2), along_x(other, 3)), [(block_shape, F32)]
    )
    g_now, g_past, g_res, g_skip, g_bias = step(
        owner_kernel,
        "owner",
        (place, mine, *(along_y(mine, k) for k in (1, 2, 3))),
        [((8, 4 * width), F32)] * 2 + [((16, width), F32)] * 2 + [((1, 32), F32)],
    )
    return res[None], skip[None], grad_in[None], g_now, g_past, g_bias[0], g_res, g_skip


def solution(mesh):
    rows, whole = P("dp", "tm", None), P()
    return jax.shard_map(
        shards,
        mesh=mesh,
        in_specs=(rows, whole, whole, whole, whole, whole, rows, rows),
        out_specs=(rows, rows, rows, P("dp", None), P("dp", None), P("dp"), P("dp", None), P("dp", None)),
        check_vma=False,
    )
```

time: 623 us -> 97 us (0.16)
  waiting for transfers between devices: 493 us -> 31.1 us
  blocking collectives: 48.9 us -> 0 us
  matrix products: 33.4 us -> 0 us
  starting transfers between devices: 6.92 us -> 34 us
  Pallas kernels: 0 us -> 22.5 us
  between operations: 14.6 us -> 0.82 us
  local copies, waits for them, and re-layouts: 19.7 us -> 8.17 us
    reduce_scatter x2 -> x0, waiting for transfers between devices: 226 us -> none  [the longest x1 114 us: shards(): lax.psum_scatter(summed[3], 'dp', scatter_dimension=0, tiled=True)]
    unnamed x7 -> x0, waiting for transfers between devices: 146 us -> none
    psum x1 -> x0, waiting for transfers between devices: 101 us -> none  [shards(): lax.psum((partials[0], partials[1], partials[2], partials[3], partials[4]...]
    unnamed x1 -> x0, blocking collectives: 48.9 us -> none
    dot_general x12 -> x0, matrix products: 33.4 us -> none  [the longest x4 12.6 us: contract_rows(): lax.dot_general(left, right, (((0,), (0,)), ((), ())), preferred_element_...]
    ppermute x2 -> x14, starting transfers between devices: 6.54 us -> 34 us  [the longest x8 17.6 us: exchange(): lax.ppermute(value, axis, [(i, partner(i)) for i in range(lax.axis_size(a...]
    pallas_call x0 -> x10, Pallas kernels: none -> 22.5 us  [call(): pl.pallas_call(body, out_shape=[kind(s, t) for s, t, *_ in outs for kind...]
    unnamed x45 -> x20, local copies, waits for them, and re-layouts: 19.7 us -> 4.19 us
  transfers between devices with their start and end apart: 7 -> 14, of which waited for: 6 -> 11; matrix products, arithmetic and copies ran while one was open for 6% -> 2% of each run, Pallas kernels for 0% -> 16%
where the time goes in v2:
time: 97 us; the launch traced here: 96.6 us
  starting transfers between devices  34 us (35%)
  waiting for transfers between devices  31.1 us (32%)
  Pallas kernels  22.5 us (23%)
  local copies, waits for them, and re-layouts  8.17 us (8%)
    pallas_call x10, Pallas kernels, call(): pl.pallas_call(body, out_shape=[kind(s, t) for s, t, *_ in outs for kind...  22.5 us
    ppermute x8, starting transfers between devices, exchange(): lax.ppermute(value, axis, [(i, partner(i)) for i in range(lax.axis_size(a...  17.6 us
    ppermute x8, waiting for transfers between devices, exchange(): lax.ppermute(value, axis, [(i, partner(i)) for i in range(lax.axis_size(a...  17.3 us
    ppermute x3, waiting for transfers between devices, shift(): lax.ppermute(value, 'tm', [(s, s + steps) for s in range(max(0, -steps),...  10 us
    ppermute x3, starting transfers between devices, shift(): lax.ppermute(value, 'tm', [(s, s + steps) for s in range(max(0, -steps),...  9.78 us
    ppermute x3, starting transfers between devices, along_x(): lax.ppermute(value, ('tm', 'dp'), [(i, target(i)) for i in range(256)])  6.62 us
    unnamed x20, local copies, waits for them, and re-layouts  4.19 us
    ppermute x3, waiting for transfers between devices, along_x(): lax.ppermute(value, ('tm', 'dp'), [(i, target(i)) for i in range(256)])  3.85 us
  transfers between devices with their start and end apart: 14, of which 11 were waited for; matrix products, arithmetic and copies ran while one was open for 2% of the time, Pallas kernels for 16%

profile of v2, /device:TPU:64, one launch (start us, length us, event | category | flops | bytes accessed | tf_op | source)
XLA Modules:
  0.0 96.6 jit_solution(15031597112754717302)
XLA Ops:
  0.6 0.0 copy-start
  0.6 0.0 copy-start.1
  0.7 0.0 copy-start.9
  0.7 2.0 %slice_bitcast_fusion = bf16[1024,256]{1,0:T(8,128)(2,1)} fusion(bf16[1,2048,256]{2,1,0:T(8,128)(2,1)} %param.8), kind=kLoop, calls=%fused_computation | loop fusion | bytes 1048576 | tf_op jit(solution)/shard_map/slice | solution.py:214
  2.7 4.9 %collective-permute-start.1 = (bf16[1024,256]{1,0:T(8,128)(2,1)}, bf16[1024,256]{1,0:T(8,128)(2,1)S(1)}, u32[]{:S(2)}, u32[]{:S(2)}) collective-permute-start(bf16[1024,256]{1,0:T(8,128)(2,1)} %slice_bitcast_fusion), channel_id=1, source_target_pairs={{0,32},{32,64},{64,96},{96,128},{128,160},{160,192},{192,224},{1,3... | collective-permute-start | bytes 1572872 | tf_op jit(solution)/shard_map/ppermute | solution.py:180
  7.6 1.9 %slice.11 = bf16[1024,256]{1,0:T(8,128)(2,1)} slice(bf16[2048,256]{1,0:T(8,128)(2,1)} %bitcast.15), slice={[1024:2048], [0:256]} | slice | bytes 1048576 | tf_op jit(solution)/shard_map/slice | solution.py:217
  9.5 3.4 %collective-permute-start = (bf16[1024,256]{1,0:T(8,128)(2,1)}, bf16[1024,256]{1,0:T(8,128)(2,1)S(1)}, u32[]{:S(2)}, u32[]{:S(2)}) collective-permute-start(bf16[1024,256]{1,0:T(8,128)(2,1)} %slice.11), channel_id=1, source_target_pairs={{0,32},{32,64},{64,96},{96,128},{128,160},{160,192},{192,224},{1,3... | collective-permute-start | bytes 1572872 | tf_op jit(solution)/shard_map/ppermute | solution.py:180
  13.0 0.1 stack.23.place
  13.1 0.0 copy-done
  13.1 0.0 copy-done.1
  13.1 0.0 copy-done.9
  13.1 0.0 copy-start.3
  13.1 1.2 %copy-done.3 = bf16[1,2048,256]{2,1,0:T(8,128)(2,1)S(1)} copy-done((bf16[1,2048,256]{2,1,0:T(8,128)(2,1)S(1)}, bf16[1,2048,256]{2,1,0:T(8,128)(2,1)}, u32[]{:S(2)}) %copy-start.3) | copy-done | bytes 1048600
  14.3 0.0 copy-start.4
  14.3 1.0 %copy-done.4 = bf16[256,1024]{1,0:T(8,128)(2,1)S(1)} copy-done((bf16[256,1024]{1,0:T(8,128)(2,1)S(1)}, bf16[256,1024]{1,0:T(8,128)(2,1)}, u32[]{:S(2)}) %copy-start.4) | copy-done | bytes 524312
  15.4 0.0 copy-start.6
  15.4 0.9 copy-done.6
  16.3 0.0 copy-start.8
  16.3 0.9 copy-done.8
  17.3 0.0 copy-start.2
  17.3 0.0 copy-start.7
  17.3 2.9 %before.1 = (f32[2048,1024]{1,0:T(8,128)S(1)}, f32[2048,512]{1,0:T(8,128)S(1)}) custom-call(bf16[2048,256]{1,0:T(8,128)(2,1)S(1)} %bitcast.16, bf16[2048,256]{1,0:T(8,128)(2,1)S(1)} %bitcast.20, bf16[2048,256]{1,0:T(8,128)(2,1)S(1)} %bitcast.24, bf16[256,1024]{1,0:T(8,128)(2,1)S(1)} %copy-done.4, f32[1,1024]{1,0:T(1,128)S(1)} %bitcast.27, ...), custom_call_target="tpu_custom_call" | custom-call | flops 2147483648 | bytes 4194304 | tf_op jit(solution)/shard_map/before/pallas_call | solution.py:159
  20.2 0.1 collective-permute-done.1.d
  20.2 0.0 copy-done.2
  20.2 0.0 copy-done.7
  20.2 6.4 %first.1 = (bf16[2048,256]{1,0:T(8,128)(2,1)}, bf16[2048,256]{1,0:T(8,128)(2,1)}, f32[2048,256]{1,0:T(8,128)}, bf16[2048,256]{1,0:T(8,128)(2,1)}, f32[512,1024]{...) custom-call(bf16[2048,256]{1,0:T(8,128)(2,1)S(1)} %bitcast.17, ...), custom_call_target="tpu_custom_call" | custom-call | flops 3758096384 | bytes 7340032 | tf_op jit(solution)/shard_map/first/pallas_call | solution.py:159
  26.6 3.7 %collective-permute-done.d = bf16[1024,256]{1,0:T(8,128)(2,1)S(1)} collective-permute-done((bf16[1024,256]{1,0:T(8,128)(2,1)}, bf16[1024,256]{1,0:T(8,128)(2,1)S(1)}, u32[]{:S(2)}, u32[]{:S(2)}) %collective-permute-start) | collective-permute-done | bytes 524320 | tf_op jit(solution)/shard_map/ppermute | solution.py:180
  30.3 4.4 %last.1 = (bf16[1024,512]{1,0:T(8,128)(2,1)S(1)}, bf16[1024,1024]{1,0:T(8,128)(2,1)S(1)}, bf16[2,4,2,8,3200]{4,3,2,1,0:T(8,128)(2,1)S(1)}, f32[2,4,2,8,3200]{4,3...) custom-call(s32[5]{0:T(128)S(1)} %stack.23.place, ...), custom_call_target="tpu_custom_call", output_to_operand_aliasing={{4}: (8, {}), {5}: (9, {}), {6}: (10, {})} | custom-call | flops 2147483648 | bytes 4194304 | tf_op jit(solution)/shard_map/last/pallas_call | solution.py:159
  34.7 0.1 collective-permute-start.2
  34.8 3.0 %after.1 = (bf16[2048,256]{1,0:T(8,128)(2,1)}, bf16[2048,256]{1,0:T(8,128)(2,1)}, f32[2048,256]{1,0:T(8,128)}, bf16[2048,256]{1,0:T(8,128)(2,1)}) custom-call(bf16[1024,512]{1,0:T(8,128)(2,1)S(1)} %get-tuple-element.54.gated, bf16[1024,1024]{1,0:T(8,128)(2,1)S(1)} %get-tuple-element.55.dz, ...), custom_call_target="tpu_custom_call", output_to_operand_aliasing={{0}: (8, {}), {1}: (9, {}), {2}: (10, {}), {3}: (11, {})} | custom-call | flops 1610612736 | bytes 3145728 | tf_op jit(solution)/shard_map/after/pallas_call | solution.py:159
  37.8 0.0 copy-start.5
  37.8 0.0 collective-permute-done.2.came
  37.8 1.4 %collective-permute-start.7 = (bf16[2048,256]{1,0:T(8,128)(2,1)}, bf16[2048,256]{1,0:T(8,128)(2,1)S(1)}, u32[]{:S(2)}, u32[]{:S(2)}) collective-permute-start(bf16[2048,256]{1,0:T(8,128)(2,1)} %get-tuple-element.73), channel_id=1, source_target_pairs={{32,0},{64,32},{96,64},{128,96},{160,128},{192,160},{224,192},{33,... | collective-permute-start | bytes 3145736 | tf_op jit(solution)/shard_map/ppermute | solution.py:180
  39.2 0.7 by_core.1
  39.9 2.0 %collective-permute-start.3 = (bf16[4,2,8,3200]{3,2,1,0:T(8,128)(2,1)S(1)}, bf16[4,2,8,3200]{3,2,1,0:T(8,128)(2,1)S(1)}, u32[]{:S(2)}, u32[]{:S(2)}) collective-permute-start(bf16[4,2,8,3200]{3,2,1,0:T(8,128)(2,1)S(1)} %get-tuple-element.67), channel_id=1, source_target_pairs={{0,2},{1,3},{2,0},{3,1},{4,6},{5,7},{6,4},{7,5},{8,10},{9,11},{10,... | collective-permute-start | bytes 1228808 | tf_op jit(solution)/shard_map/ppermute | solution.py:186
  41.9 10.1 %collective-permute-done.3.came = bf16[4,2,8,3200]{3,2,1,0:T(8,128)(2,1)S(1)} collective-permute-done((bf16[4,2,8,3200]{3,2,1,0:T(8,128)(2,1)S(1)}, bf16[4,2,8,3200]{3,2,1,0:T(8,128)(2,1)S(1)}, u32[]{:S(2)}, u32[]{:S(2)}) %collective-permute-start.3) | collective-permute-done | bytes 409632 | tf_op jit(solution)/shard_map/ppermute | solution.py:186
  52.0 1.3 %by_pair.1 = (f32[2,8,3200]{2,1,0:T(8,128)S(1)}, bf16[2,8,3200]{2,1,0:T(8,128)(2,1)}, bf16[2,8,3200]{2,1,0:T(8,128)(2,1)}, bf16[2,8,3200]{2,1,0:T(8,128)(2,1)}) custom-call(s32[5]{0:T(128)S(1)} %stack.23.place, f32[4,2,8,3200]{3,2,1,0:T(8,128)S(1)} %get-tuple-element.66.keep, bf16[4,2,8,3200]{3,2,1,0:T(8,128)(2,1)S(1)} %collective-permute-done.3.came), custom_call_target="tpu_custom_call" | custom-call | flops 1048576 | bytes 2048 | tf_op jit(solution)/shard_map/by_pair/pallas_call | solution.py:159
  53.3 4.3 %collective-permute-start.4 = (bf16[2,8,3200]{2,1,0:T(8,128)(2,1)}, bf16[2,8,3200]{2,1,0:T(8,128)(2,1)}, u32[]{:S(2)}, u32[]{:S(2)}) collective-permute-start(bf16[2,8,3200]{2,1,0:T(8,128)(2,1)} %get-tuple-element.69), channel_id=1, source_target_pairs={{0,4},{1,5},{2,6},{3,7},{4,8},{5,9},{6,10},{7,11},{8,12},{9,13},{1... | collective-permute-start | bytes 307208 | tf_op jit(solution)/shard_map/ppermute | solution.py:186
  57.6 0.9 collective-permute-start.5
  58.5 2.9 %collective-permute-start.6 = (bf16[2,8,3200]{2,1,0:T(8,128)(2,1)}, bf16[2,8,3200]{2,1,0:T(8,128)(2,1)}, u32[]{:S(2)}, u32[]{:S(2)}) collective-permute-start(bf16[2,8,3200]{2,1,0:T(8,128)(2,1)} %get-tuple-element.71), channel_id=1, source_target_pairs={{0,12},{1,13},{2,14},{3,15},{4,0},{5,1},{6,2},{7,3},{8,4},{9,5},{1... | collective-permute-start | bytes 307208 | tf_op jit(solution)/shard_map/ppermute | solution.py:186
  61.5 6.2 %collective-permute-done.7.came = bf16[2048,256]{1,0:T(8,128)(2,1)S(1)} collective-permute-done((bf16[2048,256]{1,0:T(8,128)(2,1)}, bf16[2048,256]{1,0:T(8,128)(2,1)S(1)}, u32[]{:S(2)}, u32[]{:S(2)}) %collective-permute-start.7) | collective-permute-done | bytes 1048608 | tf_op jit(solution)/shard_map/ppermute | solution.py:180
  67.7 0.0 copy-done.5
  67.7 1.6 %finish.1 = bf16[2048,256]{1,0:T(8,128)(2,1)} custom-call(f32[2048,256]{1,0:T(8,128)S(1)} %copy-done.5, bf16[2048,256]{1,0:T(8,128)(2,1)S(1)} %collective-permute-done.7.came), custom_call_target="tpu_custom_call" | custom-call | flops 268435456000 | bytes 524288000 | tf_op jit(solution)/shard_map/finish/pallas_call | solution.py:159
  69.3 0.0 collective-permute-done.4.one
  69.3 0.0 collective-permute-done.5.two
  69.3 1.3 %collective-permute-done.6.three = bf16[2,8,3200]{2,1,0:T(8,128)(2,1)} collective-permute-done((bf16[2,8,3200]{2,1,0:T(8,128)(2,1)}, bf16[2,8,3200]{2,1,0:T(8,128)(2,1)}, u32[]{:S(2)}, u32[]{:S(2)}) %collective-permute-start.6) | collective-permute-done | bytes 102432 | tf_op jit(solution)/shard_map/ppermute | solution.py:186
  70.5 1.1 %by_z.1 = (f32[8,3200]{1,0:T(8,128)S(1)}, f32[8,3200]{1,0:T(8,128)S(1)}) custom-call(s32[5]{0:T(128)S(1)} %stack.23.place, f32[2,8,3200]{2,1,0:T(8,128)S(1)} %get-tuple-element.75.own, bf16[2,8,3200]{2,1,0:T(8,128)(2,1)} %collective-permute-done.4.one, bf16[2,8,3200]{2,1,0:T(8,128)(2,1)} %collective-permute-done.5.two, ...), custom_call_target="tpu_custom_call" | custom-call | flops 1048576 | bytes 2048 | tf_op jit(solution)/shard_map/by_z/pallas_call | solution.py:159
  71.6 4.6 %collective-permute-start.9 = (f32[8,3200]{1,0:T(8,128)S(1)}, f32[8,3200]{1,0:T(8,128)S(1)}, u32[]{:S(2)}, u32[]{:S(2)}) collective-permute-start(f32[8,3200]{1,0:T(8,128)S(1)} %get-tuple-element.79.own), channel_id=1, source_target_pairs={{0,32},{1,33},{2,34},{3,35},{4,36},{5,37},{6,38},{7,39},{8,40},{9,... | collective-permute-start | bytes 307208 | tf_op jit(solution)/shard_map/ppermute | solution.py:202
  76.2 0.0 collective-permute-start.10
  76.2 2.0 %collective-permute-start.8 = (f32[8,3200]{1,0:T(8,128)S(1)}, f32[8,3200]{1,0:T(8,128)S(1)}, u32[]{:S(2)}, u32[]{:S(2)}) collective-permute-start(f32[8,3200]{1,0:T(8,128)S(1)} %get-tuple-element.80), channel_id=1, source_target_pairs={{0,16},{1,17},{2,18},{3,19},{4,20},{5,21},{6,22},{7,23},{8,24},{9,... | collective-permute-start | bytes 307208 | tf_op jit(solution)/shard_map/ppermute | solution.py:202
  78.2 1.4 %collective-permute-done.9.two = f32[8,3200]{1,0:T(8,128)S(1)} collective-permute-done((f32[8,3200]{1,0:T(8,128)S(1)}, f32[8,3200]{1,0:T(8,128)S(1)}, u32[]{:S(2)}, u32[]{:S(2)}) %collective-permute-start.9) | collective-permute-done | bytes 102432 | tf_op jit(solution)/shard_map/ppermute | solution.py:202
  79.7 1.2 %collective-permute-done.10.three = f32[8,3200]{1,0:T(8,128)S(1)} collective-permute-done((f32[8,3200]{1,0:T(8,128)S(1)}, f32[8,3200]{1,0:T(8,128)S(1)}, u32[]{:S(2)}, u32[]{:S(2)}) %collective-permute-start.10) | collective-permute-done | bytes 102432 | tf_op jit(solution)/shard_map/ppermute | solution.py:202
  80.9 1.2 %collective-permute-done.8.one = f32[8,3200]{1,0:T(8,128)S(1)} collective-permute-done((f32[8,3200]{1,0:T(8,128)S(1)}, f32[8,3200]{1,0:T(8,128)S(1)}, u32[]{:S(2)}, u32[]{:S(2)}) %collective-permute-start.8) | collective-permute-done | bytes 102432 | tf_op jit(solution)/shard_map/ppermute | solution.py:202
  82.1 6.0 %collective-permute-start.13 = (f32[8,3200]{1,0:T(8,128)S(1)}, f32[8,3200]{1,0:T(8,128)S(1)}, u32[]{:S(2)}, u32[]{:S(2)}) collective-permute-start(f32[8,3200]{1,0:T(8,128)S(1)} %by_x.1.own), channel_id=1, source_target_pairs={{0,192},{32,224},{64,0},{96,32},{128,64},{160,96},{192,128},{224,1... | collective-permute-start | bytes 307208 | tf_op jit(solution)/shard_map/ppermute | solution.py:186
  88.1 0.3 collective-permute-start.12
  88.5 1.0 %collective-permute-start.11 = (f32[8,3200]{1,0:T(8,128)S(1)}, f32[8,3200]{1,0:T(8,128)S(1)}, u32[]{:S(2)}, u32[]{:S(2)}) collective-permute-start(f32[8,3200]{1,0:T(8,128)S(1)} %by_x.1.own), channel_id=1, source_target_pairs={{0,64},{32,96},{64,128},{96,160},{128,192},{160,224},{192,0},{224,... | collective-permute-start | bytes 307208 | tf_op jit(solution)/shard_map/ppermute | solution.py:186
  89.4 2.0 %collective-permute-done.13.three = f32[8,3200]{1,0:T(8,128)S(1)} collective-permute-done((f32[8,3200]{1,0:T(8,128)S(1)}, f32[8,3200]{1,0:T(8,128)S(1)}, u32[]{:S(2)}, u32[]{:S(2)}) %collective-permute-start.13) | collective-permute-done | bytes 102432 | tf_op jit(solution)/shard_map/ppermute | solution.py:186
  91.4 3.0 %collective-permute-done.12.two = f32[8,3200]{1,0:T(8,128)S(1)} collective-permute-done((f32[8,3200]{1,0:T(8,128)S(1)}, f32[8,3200]{1,0:T(8,128)S(1)}, u32[]{:S(2)}, u32[]{:S(2)}) %collective-permute-start.12) | collective-permute-done | bytes 102432 | tf_op jit(solution)/shard_map/ppermute | solution.py:186
  94.4 1.0 %collective-permute-done.11.one = f32[8,3200]{1,0:T(8,128)S(1)} collective-permute-done((f32[8,3200]{1,0:T(8,128)S(1)}, f32[8,3200]{1,0:T(8,128)S(1)}, u32[]{:S(2)}, u32[]{:S(2)}) %collective-permute-start.11) | collective-permute-done | bytes 102432 | tf_op jit(solution)/shard_map/ppermute | solution.py:186
  95.4 1.2 %owner.1 = (f32[8,1024]{1,0:T(8,128)}, f32[8,1024]{1,0:T(8,128)}, f32[16,256]{1,0:T(8,128)}, f32[16,256]{1,0:T(8,128)}, f32[1,32]{1,0:T(1,128)}) custom-call(s32[5]{0:T(128)S(1)} %stack.23.place, f32[8,3200]{1,0:T(8,128)S(1)} %by_x.1.own, f32[8,3200]{1,0:T(8,128)S(1)} %collective-permute-done.11.one, f32[8,3200]{1,0:T(8,128)S(1)} %collective-permute-done.12.two, ...), custom_call_target="tpu_custom_call" | custom-call | flops 1048576 | bytes 2048 | tf_op jit(solution)/shard_map/owner/pallas_call | solution.py:159
  (1 shorter events, 0.0 us)
Async XLA Ops:
  0.6 12.5 %copy-start = (bf16[1,2048,256]{2,1,0:T(8,128)(2,1)S(1)}, bf16[1,2048,256]{2,1,0:T(8,128)(2,1)}, u32[]{:S(2)}) copy-start(bf16[1,2048,256]{2,1,0:T(8,128)(2,1)} %param.8) | copy-start | bytes 3145732
  0.6 12.5 %copy-start.1 = (bf16[1,2048,256]{2,1,0:T(8,128)(2,1)S(1)}, bf16[1,2048,256]{2,1,0:T(8,128)(2,1)}, u32[]{:S(2)}) copy-start(bf16[1,2048,256]{2,1,0:T(8,128)(2,1)} %param.14) | copy-start | bytes 3145732
  0.7 12.5 %copy-start.9 = (f32[1024]{0:T(1024)S(1)}, f32[1024]{0:T(1024)}, u32[]{:S(2)}) copy-start(f32[1024]{0:T(1024)} %param.11) | copy-start | bytes 12292
  2.7 17.5 %collective-permute-start.1 = (bf16[1024,256]{1,0:T(8,128)(2,1)}, bf16[1024,256]{1,0:T(8,128)(2,1)S(1)}, u32[]{:S(2)}, u32[]{:S(2)}) collective-permute-start(bf16[1024,256]{1,0:T(8,128)(2,1)} %slice_bitcast_fusion), channel_id=1, source_target_pairs={{0,32},{32,64},{64,96},{96,128},{128,160},{160,192},{192,224},{1,3... | collective-permute-start | bytes 1572872 | tf_op jit(solution)/shard_map/ppermute | solution.py:180
  9.5 20.8 %collective-permute-start = (bf16[1024,256]{1,0:T(8,128)(2,1)}, bf16[1024,256]{1,0:T(8,128)(2,1)S(1)}, u32[]{:S(2)}, u32[]{:S(2)}) collective-permute-start(bf16[1024,256]{1,0:T(8,128)(2,1)} %slice.11), channel_id=1, source_target_pairs={{0,32},{32,64},{64,96},{96,128},{128,160},{160,192},{192,224},{1,3... | collective-permute-start | bytes 1572872 | tf_op jit(solution)/shard_map/ppermute | solution.py:180
  13.1 1.2 %copy-start.3 = (bf16[1,2048,256]{2,1,0:T(8,128)(2,1)S(1)}, bf16[1,2048,256]{2,1,0:T(8,128)(2,1)}, u32[]{:S(2)}) copy-start(bf16[1,2048,256]{2,1,0:T(8,128)(2,1)} %param.15) | copy-start | bytes 3145732
  14.3 1.0 %copy-start.4 = (bf16[256,1024]{1,0:T(8,128)(2,1)S(1)}, bf16[256,1024]{1,0:T(8,128)(2,1)}, u32[]{:S(2)}) copy-start(bf16[256,1024]{1,0:T(8,128)(2,1)} %now_w.5) | copy-start | bytes 1572868
  15.4 0.9 copy-start.6
  16.3 0.9 copy-start.8
  17.3 2.9 %copy-start.2 = (bf16[256,1024]{1,0:T(8,128)(2,1)S(1)}, bf16[256,1024]{1,0:T(8,128)(2,1)}, u32[]{:S(2)}) copy-start(bf16[256,1024]{1,0:T(8,128)(2,1)} %past_w.5) | copy-start | bytes 1572868
  17.3 2.9 %copy-start.7 = (bf16[512,256]{1,0:T(8,128)(2,1)S(1)}, bf16[512,256]{1,0:T(8,128)(2,1)}, u32[]{:S(2)}) copy-start(bf16[512,256]{1,0:T(8,128)(2,1)} %res_w.5) | copy-start | bytes 786436
  34.7 3.1 %collective-permute-start.2 = (bf16[2,4,2,8,3200]{4,3,2,1,0:T(8,128)(2,1)S(1)}, bf16[2,4,2,8,3200]{4,3,2,1,0:T(8,128)(2,1)S(1)}, u32[]{:S(2)}, u32[]{:S(2)}) collective-permute-start(bf16[2,4,2,8,3200]{4,3,2,1,0:T(8,128)(2,1)S(1)} %get-tuple-element.63), channel_id=1, source_target_pairs={{0,1},{1,0},{2,3},{3,2},{4,5},{5,4},{6,7},{7,6},{8,9},{9,8},{10,11... | collective-permute-start | bytes 2457608 | tf_op jit(solution)/shard_map/ppermute | solution.py:186
  37.8 29.9 %copy-start.5 = (f32[2048,256]{1,0:T(8,128)S(1)}, f32[2048,256]{1,0:T(8,128)}, u32[]{:S(2)}) copy-start(f32[2048,256]{1,0:T(8,128)} %get-tuple-element.72.part) | copy-start | bytes 6291460
  37.8 29.9 %collective-permute-start.7 = (bf16[2048,256]{1,0:T(8,128)(2,1)}, bf16[2048,256]{1,0:T(8,128)(2,1)S(1)}, u32[]{:S(2)}, u32[]{:S(2)}) collective-permute-start(bf16[2048,256]{1,0:T(8,128)(2,1)} %get-tuple-element.73), channel_id=1, source_target_pairs={{32,0},{64,32},{96,64},{128,96},{160,128},{192,160},{224,192},{33,... | collective-permute-start | bytes 3145736 | tf_op jit(solution)/shard_map/ppermute | solution.py:180
  39.9 12.1 %collective-permute-start.3 = (bf16[4,2,8,3200]{3,2,1,0:T(8,128)(2,1)S(1)}, bf16[4,2,8,3200]{3,2,1,0:T(8,128)(2,1)S(1)}, u32[]{:S(2)}, u32[]{:S(2)}) collective-permute-start(bf16[4,2,8,3200]{3,2,1,0:T(8,128)(2,1)S(1)} %get-tuple-element.67), channel_id=1, source_target_pairs={{0,2},{1,3},{2,0},{3,1},{4,6},{5,7},{6,4},{7,5},{8,10},{9,11},{10,... | collective-permute-start | bytes 1228808 | tf_op jit(solution)/shard_map/ppermute | solution.py:186
  53.3 15.9 %collective-permute-start.4 = (bf16[2,8,3200]{2,1,0:T(8,128)(2,1)}, bf16[2,8,3200]{2,1,0:T(8,128)(2,1)}, u32[]{:S(2)}, u32[]{:S(2)}) collective-permute-start(bf16[2,8,3200]{2,1,0:T(8,128)(2,1)} %get-tuple-element.69), channel_id=1, source_target_pairs={{0,4},{1,5},{2,6},{3,7},{4,8},{5,9},{6,10},{7,11},{8,12},{9,13},{1... | collective-permute-start | bytes 307208 | tf_op jit(solution)/shard_map/ppermute | solution.py:186
  57.6 11.6 %collective-permute-start.5 = (bf16[2,8,3200]{2,1,0:T(8,128)(2,1)}, bf16[2,8,3200]{2,1,0:T(8,128)(2,1)}, u32[]{:S(2)}, u32[]{:S(2)}) collective-permute-start(bf16[2,8,3200]{2,1,0:T(8,128)(2,1)} %get-tuple-element.70), channel_id=1, source_target_pairs={{0,8},{1,9},{2,10},{3,11},{4,12},{5,13},{6,14},{7,15},{8,0},{9,1},... | collective-permute-start | bytes 307208 | tf_op jit(solution)/shard_map/ppermute | solution.py:186
  58.5 12.0 %collective-permute-start.6 = (bf16[2,8,3200]{2,1,0:T(8,128)(2,1)}, bf16[2,8,3200]{2,1,0:T(8,128)(2,1)}, u32[]{:S(2)}, u32[]{:S(2)}) collective-permute-start(bf16[2,8,3200]{2,1,0:T(8,128)(2,1)} %get-tuple-element.71), channel_id=1, source_target_pairs={{0,12},{1,13},{2,14},{3,15},{4,0},{5,1},{6,2},{7,3},{8,4},{9,5},{1... | collective-permute-start | bytes 307208 | tf_op jit(solution)/shard_map/ppermute | solution.py:186
  71.6 8.1 %collective-permute-start.9 = (f32[8,3200]{1,0:T(8,128)S(1)}, f32[8,3200]{1,0:T(8,128)S(1)}, u32[]{:S(2)}, u32[]{:S(2)}) collective-permute-start(f32[8,3200]{1,0:T(8,128)S(1)} %get-tuple-element.79.own), channel_id=1, source_target_pairs={{0,32},{1,33},{2,34},{3,35},{4,36},{5,37},{6,38},{7,39},{8,40},{9,... | collective-permute-start | bytes 307208 | tf_op jit(solution)/shard_map/ppermute | solution.py:202
  76.2 4.7 %collective-permute-start.10 = (f32[8,3200]{1,0:T(8,128)S(1)}, f32[8,3200]{1,0:T(8,128)S(1)}, u32[]{:S(2)}, u32[]{:S(2)}) collective-permute-start(f32[8,3200]{1,0:T(8,128)S(1)} %get-tuple-element.80), channel_id=1, source_target_pairs={{0,48},{1,49},{2,50},{3,51},{4,52},{5,53},{6,54},{7,55},{8,56},{9,... | collective-permute-start | bytes 307208 | tf_op jit(solution)/shard_map/ppermute | solution.py:202
  76.2 5.9 %collective-permute-start.8 = (f32[8,3200]{1,0:T(8,128)S(1)}, f32[8,3200]{1,0:T(8,128)S(1)}, u32[]{:S(2)}, u32[]{:S(2)}) collective-permute-start(f32[8,3200]{1,0:T(8,128)S(1)} %get-tuple-element.80), channel_id=1, source_target_pairs={{0,16},{1,17},{2,18},{3,19},{4,20},{5,21},{6,22},{7,23},{8,24},{9,... | collective-permute-start | bytes 307208 | tf_op jit(solution)/shard_map/ppermute | solution.py:202
  82.1 9.3 %collective-permute-start.13 = (f32[8,3200]{1,0:T(8,128)S(1)}, f32[8,3200]{1,0:T(8,128)S(1)}, u32[]{:S(2)}, u32[]{:S(2)}) collective-permute-start(f32[8,3200]{1,0:T(8,128)S(1)} %by_x.1.own), channel_id=1, source_target_pairs={{0,192},{32,224},{64,0},{96,32},{128,64},{160,96},{192,128},{224,1... | collective-permute-start | bytes 307208 | tf_op jit(solution)/shard_map/ppermute | solution.py:186
  88.1 6.3 %collective-permute-start.12 = (f32[8,3200]{1,0:T(8,128)S(1)}, f32[8,3200]{1,0:T(8,128)S(1)}, u32[]{:S(2)}, u32[]{:S(2)}) collective-permute-start(f32[8,3200]{1,0:T(8,128)S(1)} %by_x.1.own), channel_id=1, source_target_pairs={{0,128},{32,160},{64,192},{96,224},{128,0},{160,32},{192,64},{224,... | collective-permute-start | bytes 307208 | tf_op jit(solution)/shard_map/ppermute | solution.py:186
  88.5 6.9 %collective-permute-start.11 = (f32[8,3200]{1,0:T(8,128)S(1)}, f32[8,3200]{1,0:T(8,128)S(1)}, u32[]{:S(2)}, u32[]{:S(2)}) collective-permute-start(f32[8,3200]{1,0:T(8,128)S(1)} %by_x.1.own), channel_id=1, source_target_pairs={{0,64},{32,96},{64,128},{96,160},{128,192},{160,224},{192,0},{224,... | collective-permute-start | bytes 307208 | tf_op jit(solution)/shard_map/ppermute | solution.py:186

commit v3 on v2

--- a/solution.py
+++ b/solution.py
@@ -32,8 +32,8 @@
 
 def before_kernel(h, oc, sk, now_w, bias, res_w, skip_w, z_now, dg):
     rows = tile_rows()
-    z_now[rows, :] = dot(h[rows, :], now_w[...]) + bias[...]
-    dg[rows, :] = dot_t(oc[rows, :], res_w[...]) + dot_t(sk[rows, :], skip_w[...])
+    z_now[rows, :] = dot(h[...], now_w[...]) + bias[...]
+    dg[rows, :] = dot_t(oc[...], res_w[...]) + dot_t(sk[...], skip_w[...])
 
 
 def gates(base, h, d, oc, sk, z_now, dg, past_w, g_taps, g_heads, g_bias):
@@ -76,7 +76,7 @@
 
 
 def last_kernel(base, place, h, d, oc, sk, z_now, dg, past_w, *rest):
-    gated, dz, send, keep, g_taps, g_heads, g_bias = rest[3:]
+    gated, dz, send0, send1, keep, g_taps, g_heads, g_bias = rest[3:]
     rows = tile_rows()
     gated[rows, :], dz[rows, :] = gates(
         base, h, d, oc, sk, z_now, dg, past_w, g_taps, g_heads, g_bias
@@ -86,7 +86,7 @@
     @pl.when(pl.program_id(0) == pl.num_programs(0) - 1)
     def _():
         mine = place[0]
-        for out, side in ((send, 1 - mine), (keep, mine)):
+        for outs, side in (((send0, send1), 1 - mine), ((keep.at[0], keep.at[1]), mine)):
             for chip in range(16):
                 x_lo, z = divmod(chip, 8)
                 r = pl.multiple_of((2 * chip + side) * 8, 8)
@@ -102,13 +102,17 @@
                 )
                 at = 0
                 for piece in pieces:
-                    out[z % 2, z // 2, x_lo, :, at : at + piece.shape[1]] = piece.astype(out.dtype)
+                    outs[z % 2][z // 2, x_lo, :, at : at + piece.shape[1]] = piece.astype(outs[0].dtype)
                     at += piece.shape[1]
 
 
-def by_core_kernel(place, keep, came, keep_next, send_next):
-    for out, odd in ((keep_next, place[1]), (send_next, 1 - place[1])):
-        out[...] = (keep[odd] + came[odd].astype(F32)).astype(out.dtype)
+def by_core_kernel(place, keep, came0, came1, keep_next, send_next):
+    for odd, (near, far) in enumerate(((came0, came1), (came1, came0))):
+
+        @pl.when(place[1] == odd)
+        def _():
+            keep_next[...] = keep[odd] + near[...].astype(F32)
+            send_next[...] = (keep[1 - odd] + far[...].astype(F32)).astype(BF16)
 
 
 def by_pair_kernel(place, keep, came, *outs):
@@ -123,11 +127,11 @@
 
 def by_z_kernel(place, own, one, two, three, same, other):
     for out, at in ((same, place[3]), (other, 1 - place[3])):
-        out[...] = total_of(own[at], one[at], two[at], three[at])
+        out[...] = total_of(own[at], one[at], two[at], three[at]).astype(out.dtype)
 
 
 def by_x_kernel(own, one, two, three, out):
-    out[...] = total_of(own[...], one[...], two[...], three[...])
+    out[...] = total_of(own[...], one[...], two[...], three[...]).astype(out.dtype)
 
 
 def owner_kernel(place, own, one, two, three, g_now, g_past, g_res, g_skip, g_bias):
@@ -148,11 +152,11 @@
 
 def after_kernel(base, gated, dz, h, oc, now_w, past_w, res_w, skip_w, *rest):
     rows = tile_rows()
-    results(base, gated[rows, :], dz[rows, :], h, oc, now_w, past_w, res_w, skip_w, *rest[4:])
-
-
-def finish_kernel(part, came, out):
-    out[...] = (part[...] + came[...].astype(F32)).astype(BF16)
+    results(base, gated[rows, :], dz[rows, :], h, oc, now_w, past_w, res_w, skip_w, *rest[2:])
+
+
+def finish_kernel(part, came, *refs):
+    refs[-1][...] = (part[...] + came[...].astype(F32)).astype(BF16)
 
 
 def call(body, name, steps, ins, in_specs, outs, out_specs, flops, aliases={}):
@@ -175,6 +179,24 @@
     return pltpu.with_memory_space_constraint(value, pltpu.HBM)
 
 
+def copy_rows_kernel(base, src, dst, sem):
+    copy = pltpu.make_async_copy(src.at[pl.ds(base, dst.shape[0]), :], dst, sem)
+    copy.start()
+    copy.wait()
+
+
+def copy_rows(value, base, rows):
+    return pl.pallas_call(
+        functools.partial(copy_rows_kernel, base),
+        out_shape=jax.ShapeDtypeStruct((rows, value.shape[1]), value.dtype),
+        in_specs=[pl.BlockSpec(memory_space=pl.ANY)],
+        out_specs=VMEM,
+        scratch_shapes=[pltpu.SemaphoreType.DMA],
+        cost_estimate=pl.CostEstimate(flops=0, bytes_accessed=1 << 20, transcendentals=0),
+        name="copy_rows",
+    )(in_hbm(value))
+
+
 def shift(value, steps):
     n = lax.axis_size("tm")
     return lax.ppermute(
@@ -208,20 +230,20 @@
     dp = lax.axis_index("dp")
     z = (dp // 2) % 8
     place = jnp.stack([dp % 2, z % 2, z // 2, dp // 16, dp % 4]).astype(jnp.int32)
+    place, gate_bias = lax.optimization_barrier((place, gate_bias))
     first, last = CHUNKS
     macs = 2 * total * width * width
 
-    h_first = h[:first]
-    h, h_first = lax.optimization_barrier((h, h_first))
-    d_first = shift(h_first, 1)
-    d_last = shift(h[first:], 1)
+    d_first = shift(copy_rows(h, 0, first), 1)
+    d_last = shift(copy_rows(h, first, last), 1)
 
     z_now, dg = call(
         before_kernel,
         "before",
         total // TILE,
-        (h, oc, sk, now_w, gate_bias[None, :], res_w, skip_w),
-        [VMEM] * 7,
+        tuple(in_hbm(a) for a in (h, oc, sk, now_w, gate_bias[None, :], res_w, skip_w)),
+        [pl.BlockSpec((TILE, width), lambda i: (i, 0))] * 3
+        + [pl.BlockSpec(s, lambda i: (0, 0)) for s in (now_w.shape, (1, 4 * width), res_w.shape, skip_w.shape)],
         [((total, 4 * width), F32), ((total, 2 * width), F32)],
         [VMEM] * 2,
         macs * 8,
@@ -230,78 +252,81 @@
     rows_out = [
         ((total, width), BF16),
         ((total, width), BF16),
-        ((total, width), F32, 1),
-        ((total, width), BF16, 1),
     ]
+    tail_out = lambda n: [((n, width), F32, 1), ((n, width), BF16)]
     block = lambda base: pl.BlockSpec((TILE, width), lambda i: (base // TILE + i, 0))
-    *outs, g_taps, g_heads, g_bias = call(
+    res, skip, part0, back0, g_taps, g_heads, g_bias = call(
         first_kernel,
         "first",
         first // TILE,
         (h, d_first, oc, sk, z_now, dg, now_w, past_w, res_w, skip_w),
         [VMEM] * 10,
-        rows_out + sums,
+        rows_out + tail_out(first) + sums,
         [block(0)] * 4 + [VMEM] * 3,
         macs * 28 * first // total,
     )
     block_shape = (8, 12 * width + LANES)
     packed = (2, 4, 2, *block_shape)
-    gated, dz, send, keep, *_ = call(
+    came0 = shift(back0, -1)
+    gated, dz, send0, send1, keep, *_ = call(
         functools.partial(last_kernel, first),
         "last",
         last // TILE,
         (place, h, d_last, oc, sk, z_now, dg, past_w, g_taps, g_heads, g_bias),
         [pl.BlockSpec(memory_space=pltpu.SMEM)] + [VMEM] * 10,
-        [((last, 2 * width), BF16), ((last, 4 * width), BF16), (packed, BF16), (packed, F32)] + sums,
-        [VMEM] * 7,
-        macs * 16 * last // total,
-        {8: 4, 9: 5, 10: 6},
-    )
-    came = exchange(send, "dp", lambda i: i ^ 1)
-    res, skip, part, back = call(
+        [((last, 2 * width), BF16), ((last, 4 * width), BF16), (packed[1:], BF16), (packed[1:], BF16), (packed, F32)]
+        + sums,
+        [VMEM] * 8,
+        1 << 20,
+        {8: 5, 9: 6, 10: 7},
+    )
+    halves = [exchange(v, "dp", lambda i: i ^ 1) for v in (send0, send1)]
+    *halves, came0 = lax.optimization_barrier((*halves, came0))
+    smem = pl.BlockSpec(memory_space=pltpu.SMEM)
+    step = lambda body, name, ins, outs, flops=1 << 20: call(
+        body, name, 1, ins, [smem] * (ins[0] is place) + [VMEM] * (len(ins) - (ins[0] is place)), outs,
+        [VMEM] * len(outs), flops,
+    )
+    keep, send = step(by_core_kernel, "by_core", (place, keep, *halves), [(packed[1:], F32), (packed[1:], BF16)])
+    came = along_z(send, lambda z: z ^ 1)
+    gated, dz, _ = lax.optimization_barrier((gated, dz, send))
+    res, skip, part1, back1 = call(
         functools.partial(after_kernel, first),
         "after",
         last // TILE,
-        (gated, dz, h, oc, now_w, past_w, res_w, skip_w, *outs),
-        [VMEM] * 8 + [pl.BlockSpec(memory_space=pl.ANY)] * 4,
-        rows_out,
-        [block(first)] * 4,
+        (gated, dz, h, oc, now_w, past_w, res_w, skip_w, res, skip),
+        [VMEM] * 8 + [pl.BlockSpec(memory_space=pl.ANY)] * 2,
+        rows_out + tail_out(last),
+        [block(first)] * 2 + [block(0)] * 2,
         macs * 12 * last // total,
-        {8: 0, 9: 1, 10: 2, 11: 3},
-    )
-    came, back = lax.optimization_barrier((came, back))
-    smem = pl.BlockSpec(memory_space=pltpu.SMEM)
-    step = lambda body, name, ins, outs: call(
-        body, name, 1, ins, [smem] * (ins[0] is place) + [VMEM] * (len(ins) - (ins[0] is place)), outs,
-        [VMEM] * len(outs), 1 << 20,
-    )
-    keep, send = step(by_core_kernel, "by_core", (place, keep, came), [(packed[1:], F32), (packed[1:], BF16)])
-    came = along_z(send, lambda z: z ^ 1)
+        {8: 0, 9: 1},
+    )
+
     own, *others = step(
-        by_pair_kernel, "by_pair", (place, keep, came), [(packed[2:], F32)] + [(packed[2:], BF16)] * 3
+        by_pair_kernel, "by_pair", (place, keep, came), [(packed[2:], F32)] + [(packed[2:], BF16)] * 3,
+        macs * 1000,
     )
     one, two, three = (along_z(v, lambda z, k=k: (z + 2 * k) % 8) for k, v in enumerate(others, 1))
-    (grad_in,) = call(
-        finish_kernel,
-        "finish",
-        total // TILE,
-        (part, shift(back, -1)),
-        [block(0)] * 2,
-        [((total, width), BF16)],
-        [block(0)],
-        macs * 1000,
-    )
+    finish = lambda base, rows, ins, aliases: call(
+        finish_kernel, "finish", rows // TILE, ins,
+        [block(0)] * 2 + [pl.BlockSpec(memory_space=pl.ANY)] * len(aliases),
+        [((total, width), BF16)], [block(base)], macs, aliases,
+    )[0]
+    grad_in = finish(0, first, (part0, came0), {})
     own, one, two, three, grad_in = lax.optimization_barrier((own, one, two, three, grad_in))
+    grad_in = finish(first, last, (part1, shift(back1, -1), grad_in), {2: 0})
     same, other = step(
-        by_z_kernel, "by_z", (place, own, one, two, three), [(block_shape, F32)] * 2
+        by_z_kernel, "by_z", (place, own, one, two, three), [(block_shape, BF16)] * 2
     )
     (mine,) = step(
-        by_x_kernel, "by_x", (same, along_x(other, 1), along_x(same, 2), along_x(other, 3)), [(block_shape, F32)]
-    )
+        by_x_kernel, "by_x", (same, along_x(other, 1), along_x(same, 2), along_x(other, 3)), [(block_shape, BF16)]
+    )
+    others = [along_y(mine, k) for k in (1, 2, 3)]
+    *others, grad_in = lax.optimization_barrier((*others, grad_in))
     g_now, g_past, g_res, g_skip, g_bias = step(
         owner_kernel,
         "owner",
-        (place, mine, *(along_y(mine, k) for k in (1, 2, 3))),
+        (place, mine, *others),
         [((8, 4 * width), F32)] * 2 + [((16, width), F32)] * 2 + [((1, 32), F32)],
     )
     return res[None], skip[None], grad_in[None], g_now, g_past, g_bias[0], g_res, g_skip

time: 97 us -> 89.6 us (0.924)
  local copies, waits for them, and re-layouts: 8.17 us -> 0.24 us
  starting transfers between devices: 34 us -> 28.7 us
  Pallas kernels: 22.5 us -> 27.6 us
    ppermute x8 -> x9, starting transfers between devices: 17.6 us -> 12.8 us  [exchange(): lax.ppermute(value, axis, [(i, partner(i)) for i in range(lax.axis_size(a...]
    unnamed x20 -> x22, local copies, waits for them, and re-layouts: 4.19 us -> 0.15 us
    slice x2 -> x0, local copies, waits for them, and re-layouts: 3.9 us -> none  [the longest x1 2.01 us: shards(): h_first = h[:first]]
    pallas_call x0 -> x2, Pallas kernels: none -> 3.69 us  [copy_rows(): pl.pallas_call(functools.partial(copy_rows_kernel, base), out_shape=jax.S...]
    ppermute x8 -> x9, waiting for transfers between devices: 17.3 us -> 14.9 us  [exchange(): lax.ppermute(value, axis, [(i, partner(i)) for i in range(lax.axis_size(a...]
    ppermute x3, starting transfers between devices: 6.62 us -> 4.98 us  [along_x(): lax.ppermute(value, ('tm', 'dp'), [(i, target(i)) for i in range(256)])]
    ppermute x3, waiting for transfers between devices: 3.85 us -> 5.32 us  [along_x(): lax.ppermute(value, ('tm', 'dp'), [(i, target(i)) for i in range(256)])]
    pallas_call x10 -> x11, Pallas kernels: 22.5 us -> 23.9 us  [call(): pl.pallas_call(body, out_shape=[kind(s, t) for s, t, *_ in outs for kind...]
  transfers between devices with their start and end apart: 14 -> 16, of which waited for: 11 -> 14; matrix products, arithmetic and copies ran while one was open for 2% -> 0% of each run, Pallas kernels for 16% -> 27%
where the time goes in v3:
time: 89.6 us; the launch traced here: 89.1 us
  waiting for transfers between devices  31.6 us (35%)
  starting transfers between devices  28.7 us (32%)
  Pallas kernels  27.6 us (31%)
    pallas_call x11, Pallas kernels, call(): pl.pallas_call(body, out_shape=[kind(s, t) for s, t, *_ in outs for kind...  23.9 us
    ppermute x9, waiting for transfers between devices, exchange(): lax.ppermute(value, axis, [(i, partner(i)) for i in range(lax.axis_size(a...  14.9 us
    ppermute x9, starting transfers between devices, exchange(): lax.ppermute(value, axis, [(i, partner(i)) for i in range(lax.axis_size(a...  12.8 us
    ppermute x4, waiting for transfers between devices, shift(): lax.ppermute(value, 'tm', [(s, s + steps) for s in range(max(0, -steps),...  11.3 us
    ppermute x4, starting transfers between devices, shift(): lax.ppermute(value, 'tm', [(s, s + steps) for s in range(max(0, -steps),...  10.9 us
    ppermute x3, waiting for transfers between devices, along_x(): lax.ppermute(value, ('tm', 'dp'), [(i, target(i)) for i in range(256)])  5.32 us
    ppermute x3, starting transfers between devices, along_x(): lax.ppermute(value, ('tm', 'dp'), [(i, target(i)) for i in range(256)])  4.98 us
    pallas_call x2, Pallas kernels, copy_rows(): pl.pallas_call(functools.partial(copy_rows_kernel, base), out_shape=jax.S...  3.69 us
  transfers between devices with their start and end apart: 16, of which 14 were waited for; matrix products, arithmetic and copies ran while one was open for 0% of the time, Pallas kernels for 27%

profile of v3, /device:TPU:64, one launch (start us, length us, event | category | flops | bytes accessed | tf_op | source)
XLA Modules:
  0.0 89.1 jit_solution(2990398475898473929)
XLA Ops:
  0.6 1.8 %copy_rows.3 = bf16[1024,256]{1,0:T(8,128)(2,1)} custom-call(bf16[2048,256]{1,0:T(8,128)(2,1)} %bitcast.13), custom_call_target="tpu_custom_call" | custom-call | bytes 1048576 | tf_op jit(solution)/shard_map/copy_rows/pallas_call | solution.py:189
  2.5 5.0 %collective-permute-start.1 = (bf16[1024,256]{1,0:T(8,128)(2,1)}, bf16[1024,256]{1,0:T(8,128)(2,1)S(1)}, u32[]{:S(2)}, u32[]{:S(2)}) collective-permute-start(bf16[1024,256]{1,0:T(8,128)(2,1)} %copy_rows.3), channel_id=1, source_target_pairs={{0,32},{32,64},{64,96},{96,128},{128,160},{160,192},{192,224},{1,3... | collective-permute-start | bytes 1572872 | tf_op jit(solution)/shard_map/ppermute | solution.py:202
  7.5 1.8 %copy_rows.2 = bf16[1024,256]{1,0:T(8,128)(2,1)} custom-call(bf16[2048,256]{1,0:T(8,128)(2,1)} %bitcast.14), custom_call_target="tpu_custom_call" | custom-call | bytes 1048576 | tf_op jit(solution)/shard_map/copy_rows/pallas_call | solution.py:189
  9.3 3.4 %collective-permute-start = (bf16[1024,256]{1,0:T(8,128)(2,1)}, bf16[1024,256]{1,0:T(8,128)(2,1)S(1)}, u32[]{:S(2)}, u32[]{:S(2)}) collective-permute-start(bf16[1024,256]{1,0:T(8,128)(2,1)} %copy_rows.2), channel_id=1, source_target_pairs={{0,32},{32,64},{64,96},{96,128},{128,160},{160,192},{192,224},{1,3... | collective-permute-start | bytes 1572872 | tf_op jit(solution)/shard_map/ppermute | solution.py:202
  12.8 0.1 stack.23.place
  12.9 0.0 copy-start
  12.9 0.0 copy-start.1
  12.9 0.0 copy-start.2
  12.9 0.0 copy-start.3
  12.9 0.0 copy-start.4
  12.9 0.0 copy-start.5
  12.9 0.0 copy-start.6
  13.0 5.0 %before.1 = (f32[2048,1024]{1,0:T(8,128)S(1)}, f32[2048,512]{1,0:T(8,128)S(1)}) custom-call(bf16[2048,256]{1,0:T(8,128)(2,1)} %bitcast.15, bf16[2048,256]{1,0:T(8,128)(2,1)} %bitcast.19, bf16[2048,256]{1,0:T(8,128)(2,1)} %bitcast.23, bf16[256,1024]{1,0:T(8,128)(2,1)} %now_w.5, f32[1,1024]{1,0:T(1,128)} %bitcast.29, bf16[512,256]{1,0:T(8,128)(2,1)} %res_w.5, ...), custom_call_target="tpu_custom_call" | custom-call | flops 2147483648 | bytes 4194304 | tf_op jit(solution)/shard_map/before/pallas_call | solution.py:163
  18.0 2.0 %collective-permute-done.1.d = bf16[1024,256]{1,0:T(8,128)(2,1)S(1)} collective-permute-done((bf16[1024,256]{1,0:T(8,128)(2,1)}, bf16[1024,256]{1,0:T(8,128)(2,1)S(1)}, u32[]{:S(2)}, u32[]{:S(2)}) %collective-permute-start.1) | collective-permute-done | bytes 524320 | tf_op jit(solution)/shard_map/ppermute | solution.py:202
  20.0 0.0 copy-done
  20.0 0.0 copy-done.1
  20.1 0.0 copy-done.2
  20.1 0.0 copy-done.3
  20.1 0.0 copy-done.4
  20.1 0.0 copy-done.5
  20.1 0.0 copy-done.6
  20.1 6.0 %first.1 = (bf16[2048,256]{1,0:T(8,128)(2,1)}, bf16[2048,256]{1,0:T(8,128)(2,1)}, f32[1024,256]{1,0:T(8,128)}, bf16[1024,256]{1,0:T(8,128)(2,1)S(1)}, f32[512,10...) custom-call(bf16[2048,256]{1,0:T(8,128)(2,1)S(1)} %bitcast.16, ...), custom_call_target="tpu_custom_call" | custom-call | flops 3758096384 | bytes 7340032 | tf_op jit(solution)/shard_map/first/pallas_call | solution.py:163
  26.1 1.3 %collective-permute-start.4 = (bf16[1024,256]{1,0:T(8,128)(2,1)S(1)}, bf16[1024,256]{1,0:T(8,128)(2,1)S(1)}, u32[]{:S(2)}, u32[]{:S(2)}) collective-permute-start(bf16[1024,256]{1,0:T(8,128)(2,1)S(1)} %get-tuple-element.67), channel_id=1, source_target_pairs={{32,0},{64,32},{96,64},{128,96},{160,128},{192,160},{224,192},{33,... | collective-permute-start | bytes 1572872 | tf_op jit(solution)/shard_map/ppermute | solution.py:202
  27.4 2.7 %collective-permute-done.d = bf16[1024,256]{1,0:T(8,128)(2,1)S(1)} collective-permute-done((bf16[1024,256]{1,0:T(8,128)(2,1)}, bf16[1024,256]{1,0:T(8,128)(2,1)S(1)}, u32[]{:S(2)}, u32[]{:S(2)}) %collective-permute-start) | collective-permute-done | bytes 524320 | tf_op jit(solution)/shard_map/ppermute | solution.py:202
  30.1 4.1 %last.1 = (bf16[1024,512]{1,0:T(8,128)(2,1)S(1)}, bf16[1024,1024]{1,0:T(8,128)(2,1)S(1)}, bf16[4,2,8,3200]{3,2,1,0:T(8,128)(2,1)S(1)}, bf16[4,2,8,3200]{3,2,1,0:...) custom-call(s32[5]{0:T(128)S(1)} %stack.23.place, ...), custom_call_target="tpu_custom_call", output_to_operand_aliasing={{5}: (8, {}), {6}: (9, {}), {7}: (10, {})} | custom-call | flops 1048576 | bytes 2048 | tf_op jit(solution)/shard_map/last/pallas_call | solution.py:163
  34.3 0.1 collective-permute-start.2
  34.4 0.5 collective-permute-start.3
  34.9 1.2 %collective-permute-done.2.came0 = bf16[4,2,8,3200]{3,2,1,0:T(8,128)(2,1)S(1)} collective-permute-done((bf16[4,2,8,3200]{3,2,1,0:T(8,128)(2,1)S(1)}, bf16[4,2,8,3200]{3,2,1,0:T(8,128)(2,1)S(1)}, u32[]{:S(2)}, u32[]{:S(2)}) %collective-permute-start.2) | collective-permute-done | bytes 409632 | tf_op jit(solution)/shard_map/ppermute | solution.py:208
  36.1 0.6 collective-permute-done.3.came1
  36.7 6.6 %collective-permute-done.4.came = bf16[1024,256]{1,0:T(8,128)(2,1)S(1)} collective-permute-done((bf16[1024,256]{1,0:T(8,128)(2,1)S(1)}, bf16[1024,256]{1,0:T(8,128)(2,1)S(1)}, u32[]{:S(2)}, u32[]{:S(2)}) %collective-permute-start.4) | collective-permute-done | bytes 524320 | tf_op jit(solution)/shard_map/ppermute | solution.py:202
  43.2 0.7 by_core.1
  43.9 0.1 copy-done.9
  44.0 1.9 %collective-permute-start.5 = (bf16[4,2,8,3200]{3,2,1,0:T(8,128)(2,1)S(1)}, bf16[4,2,8,3200]{3,2,1,0:T(8,128)(2,1)S(1)}, u32[]{:S(2)}, u32[]{:S(2)}) collective-permute-start(bf16[4,2,8,3200]{3,2,1,0:T(8,128)(2,1)S(1)} %get-tuple-element.70), channel_id=1, source_target_pairs={{0,2},{1,3},{2,0},{3,1},{4,6},{5,7},{6,4},{7,5},{8,10},{9,11},{10,... | collective-permute-start | bytes 1228808 | tf_op jit(solution)/shard_map/ppermute | solution.py:208
  46.0 2.9 %after.1 = (bf16[2048,256]{1,0:T(8,128)(2,1)}, bf16[2048,256]{1,0:T(8,128)(2,1)}, f32[1024,256]{1,0:T(8,128)}, bf16[1024,256]{1,0:T(8,128)(2,1)}) custom-call(bf16[1024,512]{1,0:T(8,128)(2,1)S(1)} %get-tuple-element.71.gated, bf16[1024,1024]{1,0:T(8,128)(2,1)S(1)} %get-tuple-element.72.dz, ...), custom_call_target="tpu_custom_call", output_to_operand_aliasing={{0}: (8, {}), {1}: (9, {})} | custom-call | flops 1610612736 | bytes 3145728 | tf_op jit(solution)/shard_map/after/pallas_call | solution.py:163
  48.9 1.3 %collective-permute-start.15 = (bf16[1024,256]{1,0:T(8,128)(2,1)}, bf16[1024,256]{1,0:T(8,128)(2,1)}, u32[]{:S(2)}, u32[]{:S(2)}) collective-permute-start(bf16[1024,256]{1,0:T(8,128)(2,1)} %get-tuple-element.91), channel_id=1, source_target_pairs={{32,0},{64,32},{96,64},{128,96},{160,128},{192,160},{224,192},{33,... | collective-permute-start | bytes 1572872 | tf_op jit(solution)/shard_map/ppermute | solution.py:202
  50.1 4.0 %collective-permute-done.5.came = bf16[4,2,8,3200]{3,2,1,0:T(8,128)(2,1)S(1)} collective-permute-done((bf16[4,2,8,3200]{3,2,1,0:T(8,128)(2,1)S(1)}, bf16[4,2,8,3200]{3,2,1,0:T(8,128)(2,1)S(1)}, u32[]{:S(2)}, u32[]{:S(2)}) %collective-permute-start.5) | collective-permute-done | bytes 409632 | tf_op jit(solution)/shard_map/ppermute | solution.py:208
  54.2 0.6 by_pair.1
  54.8 0.0 copy-start.7
  54.8 4.4 %collective-permute-start.6 = (bf16[2,8,3200]{2,1,0:T(8,128)(2,1)S(1)}, bf16[2,8,3200]{2,1,0:T(8,128)(2,1)S(1)}, u32[]{:S(2)}, u32[]{:S(2)}) collective-permute-start(bf16[2,8,3200]{2,1,0:T(8,128)(2,1)S(1)} %get-tuple-element.79), channel_id=1, source_target_pairs={{0,4},{1,5},{2,6},{3,7},{4,8},{5,9},{6,10},{7,11},{8,12},{9,13},{1... | collective-permute-start | bytes 307208 | tf_op jit(solution)/shard_map/ppermute | solution.py:208
  59.2 1.0 %collective-permute-start.7 = (bf16[2,8,3200]{2,1,0:T(8,128)(2,1)S(1)}, bf16[2,8,3200]{2,1,0:T(8,128)(2,1)S(1)}, u32[]{:S(2)}, u32[]{:S(2)}) collective-permute-start(bf16[2,8,3200]{2,1,0:T(8,128)(2,1)S(1)} %get-tuple-element.80), channel_id=1, source_target_pairs={{0,8},{1,9},{2,10},{3,11},{4,12},{5,13},{6,14},{7,15},{8,0},{9,1},... | collective-permute-start | bytes 307208 | tf_op jit(solution)/shard_map/ppermute | solution.py:208
  60.2 2.8 %collective-permute-start.8 = (bf16[2,8,3200]{2,1,0:T(8,128)(2,1)S(1)}, bf16[2,8,3200]{2,1,0:T(8,128)(2,1)S(1)}, u32[]{:S(2)}, u32[]{:S(2)}) collective-permute-start(bf16[2,8,3200]{2,1,0:T(8,128)(2,1)S(1)} %get-tuple-element.81), channel_id=1, source_target_pairs={{0,12},{1,13},{2,14},{3,15},{4,0},{5,1},{6,2},{7,3},{8,4},{9,5},{1... | collective-permute-start | bytes 307208 | tf_op jit(solution)/shard_map/ppermute | solution.py:208
  63.1 0.0 copy-done.8
  63.1 0.0 copy-done.10
  63.1 0.8 finish.2.refs_0_
  63.9 0.0 collective-permute-done.6.one
  63.9 5.3 %collective-permute-done.7.two = bf16[2,8,3200]{2,1,0:T(8,128)(2,1)S(1)} collective-permute-done((bf16[2,8,3200]{2,1,0:T(8,128)(2,1)S(1)}, bf16[2,8,3200]{2,1,0:T(8,128)(2,1)S(1)}, u32[]{:S(2)}, u32[]{:S(2)}) %collective-permute-start.7) | collective-permute-done | bytes 102432 | tf_op jit(solution)/shard_map/ppermute | solution.py:208
  69.2 0.8 collective-permute-done.8.three
  70.0 0.6 by_z.1
  70.6 0.4 collective-permute-start.10
  71.0 4.6 %collective-permute-start.11 = (bf16[8,3200]{1,0:T(8,128)(2,1)S(1)}, bf16[8,3200]{1,0:T(8,128)(2,1)S(1)}, u32[]{:S(2)}, u32[]{:S(2)}) collective-permute-start(bf16[8,3200]{1,0:T(8,128)(2,1)S(1)} %get-tuple-element.89), channel_id=1, source_target_pairs={{0,48},{1,49},{2,50},{3,51},{4,52},{5,53},{6,54},{7,55},{8,56},{9,... | collective-permute-start | bytes 153608 | tf_op jit(solution)/shard_map/ppermute | solution.py:224
  75.6 0.0 collective-permute-start.9
  75.6 0.8 collective-permute-done.10.two
  76.4 0.9 %collective-permute-done.11.three = bf16[8,3200]{1,0:T(8,128)(2,1)S(1)} collective-permute-done((bf16[8,3200]{1,0:T(8,128)(2,1)S(1)}, bf16[8,3200]{1,0:T(8,128)(2,1)S(1)}, u32[]{:S(2)}, u32[]{:S(2)}) %collective-permute-start.11) | collective-permute-done | bytes 51232 | tf_op jit(solution)/shard_map/ppermute | solution.py:224
  77.4 3.6 %collective-permute-done.9.one = bf16[8,3200]{1,0:T(8,128)(2,1)S(1)} collective-permute-done((bf16[8,3200]{1,0:T(8,128)(2,1)S(1)}, bf16[8,3200]{1,0:T(8,128)(2,1)S(1)}, u32[]{:S(2)}, u32[]{:S(2)}) %collective-permute-start.9) | collective-permute-done | bytes 51232 | tf_op jit(solution)/shard_map/ppermute | solution.py:224
  81.0 0.1 collective-permute-start.14
  81.0 0.2 collective-permute-start.13
  81.2 1.8 %collective-permute-start.12 = (bf16[8,3200]{1,0:T(8,128)(2,1)S(1)}, bf16[8,3200]{1,0:T(8,128)(2,1)S(1)}, u32[]{:S(2)}, u32[]{:S(2)}) collective-permute-start(bf16[8,3200]{1,0:T(8,128)(2,1)S(1)} %by_x.1.own), channel_id=1, source_target_pairs={{0,64},{32,96},{64,128},{96,160},{128,192},{160,224},{192,0},{224,... | collective-permute-start | bytes 153608 | tf_op jit(solution)/shard_map/ppermute | solution.py:208
  83.1 0.0 collective-permute-done.15.came
  83.1 0.0 copy-done.7
  83.1 1.8 %finish.3 = bf16[2048,256]{1,0:T(8,128)(2,1)} custom-call(f32[1024,256]{1,0:T(8,128)S(1)} %copy-done.7, bf16[1024,256]{1,0:T(8,128)(2,1)} %collective-permute-done.15.came, bf16[2048,256]{1,0:T(8,128)(2,1)} %finish.2.refs_0_), custom_call_target="tpu_custom_call", output_to_operand_aliasing={{}: (2, {})} | custom-call | flops 268435456 | bytes 524288 | tf_op jit(solution)/shard_map/finish/pallas_call | solution.py:163
  84.9 0.3 collective-permute-done.14.three
  85.1 1.6 %collective-permute-done.13.two = bf16[8,3200]{1,0:T(8,128)(2,1)S(1)} collective-permute-done((bf16[8,3200]{1,0:T(8,128)(2,1)S(1)}, bf16[8,3200]{1,0:T(8,128)(2,1)S(1)}, u32[]{:S(2)}, u32[]{:S(2)}) %collective-permute-start.13) | collective-permute-done | bytes 51232 | tf_op jit(solution)/shard_map/ppermute | solution.py:208
  86.7 1.1 %collective-permute-done.12.one = bf16[8,3200]{1,0:T(8,128)(2,1)S(1)} collective-permute-done((bf16[8,3200]{1,0:T(8,128)(2,1)S(1)}, bf16[8,3200]{1,0:T(8,128)(2,1)S(1)}, u32[]{:S(2)}, u32[]{:S(2)}) %collective-permute-start.12) | collective-permute-done | bytes 51232 | tf_op jit(solution)/shard_map/ppermute | solution.py:208
  87.8 1.2 %owner.1 = (f32[8,1024]{1,0:T(8,128)}, f32[8,1024]{1,0:T(8,128)}, f32[16,256]{1,0:T(8,128)}, f32[16,256]{1,0:T(8,128)}, f32[1,32]{1,0:T(1,128)}) custom-call(s32[5]{0:T(128)S(1)} %stack.23.place, bf16[8,3200]{1,0:T(8,128)(2,1)S(1)} %by_x.1.own, bf16[8,3200]{1,0:T(8,128)(2,1)S(1)} %collective-permute-done.12.one, ...), custom_call_target="tpu_custom_call" | custom-call | flops 1048576 | bytes 2048 | tf_op jit(solution)/shard_map/owner/pallas_call | solution.py:163
  (4 shorter events, 0.0 us)
Async XLA Ops:
  2.5 17.6 %collective-permute-start.1 = (bf16[1024,256]{1,0:T(8,128)(2,1)}, bf16[1024,256]{1,0:T(8,128)(2,1)S(1)}, u32[]{:S(2)}, u32[]{:S(2)}) collective-permute-start(bf16[1024,256]{1,0:T(8,128)(2,1)} %copy_rows.3), channel_id=1, source_target_pairs={{0,32},{32,64},{64,96},{96,128},{128,160},{160,192},{192,224},{1,3... | collective-permute-start | bytes 1572872 | tf_op jit(solution)/shard_map/ppermute | solution.py:202
  9.3 20.8 %collective-permute-start = (bf16[1024,256]{1,0:T(8,128)(2,1)}, bf16[1024,256]{1,0:T(8,128)(2,1)S(1)}, u32[]{:S(2)}, u32[]{:S(2)}) collective-permute-start(bf16[1024,256]{1,0:T(8,128)(2,1)} %copy_rows.2), channel_id=1, source_target_pairs={{0,32},{32,64},{64,96},{96,128},{128,160},{160,192},{192,224},{1,3... | collective-permute-start | bytes 1572872 | tf_op jit(solution)/shard_map/ppermute | solution.py:202
  12.9 7.1 %copy-start = (bf16[1,2048,256]{2,1,0:T(8,128)(2,1)S(1)}, bf16[1,2048,256]{2,1,0:T(8,128)(2,1)}, u32[]{:S(2)}) copy-start(bf16[1,2048,256]{2,1,0:T(8,128)(2,1)} %param.8) | copy-start | bytes 3145732
  12.9 7.1 %copy-start.1 = (bf16[1,2048,256]{2,1,0:T(8,128)(2,1)S(1)}, bf16[1,2048,256]{2,1,0:T(8,128)(2,1)}, u32[]{:S(2)}) copy-start(bf16[1,2048,256]{2,1,0:T(8,128)(2,1)} %param.14) | copy-start | bytes 3145732
  12.9 7.1 %copy-start.2 = (bf16[256,1024]{1,0:T(8,128)(2,1)S(1)}, bf16[256,1024]{1,0:T(8,128)(2,1)}, u32[]{:S(2)}) copy-start(bf16[256,1024]{1,0:T(8,128)(2,1)} %past_w.5) | copy-start | bytes 1572868
  12.9 7.1 %copy-start.3 = (bf16[1,2048,256]{2,1,0:T(8,128)(2,1)S(1)}, bf16[1,2048,256]{2,1,0:T(8,128)(2,1)}, u32[]{:S(2)}) copy-start(bf16[1,2048,256]{2,1,0:T(8,128)(2,1)} %param.15) | copy-start | bytes 3145732
  12.9 7.1 %copy-start.4 = (bf16[256,1024]{1,0:T(8,128)(2,1)S(1)}, bf16[256,1024]{1,0:T(8,128)(2,1)}, u32[]{:S(2)}) copy-start(bf16[256,1024]{1,0:T(8,128)(2,1)} %now_w.5) | copy-start | bytes 1572868
  12.9 7.1 %copy-start.5 = (bf16[512,256]{1,0:T(8,128)(2,1)S(1)}, bf16[512,256]{1,0:T(8,128)(2,1)}, u32[]{:S(2)}) copy-start(bf16[512,256]{1,0:T(8,128)(2,1)} %res_w.5) | copy-start | bytes 786436
  12.9 7.1 %copy-start.6 = (bf16[512,256]{1,0:T(8,128)(2,1)S(1)}, bf16[512,256]{1,0:T(8,128)(2,1)}, u32[]{:S(2)}) copy-start(bf16[512,256]{1,0:T(8,128)(2,1)} %skip_w.5) | copy-start | bytes 786436
  26.1 17.1 %collective-permute-start.4 = (bf16[1024,256]{1,0:T(8,128)(2,1)S(1)}, bf16[1024,256]{1,0:T(8,128)(2,1)S(1)}, u32[]{:S(2)}, u32[]{:S(2)}) collective-permute-start(bf16[1024,256]{1,0:T(8,128)(2,1)S(1)} %get-tuple-element.67), channel_id=1, source_target_pairs={{32,0},{64,32},{96,64},{128,96},{160,128},{192,160},{224,192},{33,... | collective-permute-start | bytes 1572872 | tf_op jit(solution)/shard_map/ppermute | solution.py:202
  34.3 1.8 %collective-permute-start.2 = (bf16[4,2,8,3200]{3,2,1,0:T(8,128)(2,1)S(1)}, bf16[4,2,8,3200]{3,2,1,0:T(8,128)(2,1)S(1)}, u32[]{:S(2)}, u32[]{:S(2)}) collective-permute-start(bf16[4,2,8,3200]{3,2,1,0:T(8,128)(2,1)S(1)} %get-tuple-element.65), channel_id=1, source_target_pairs={{0,1},{1,0},{2,3},{3,2},{4,5},{5,4},{6,7},{7,6},{8,9},{9,8},{10,11... | collective-permute-start | bytes 1228808 | tf_op jit(solution)/shard_map/ppermute | solution.py:208
  34.4 2.3 %collective-permute-start.3 = (bf16[4,2,8,3200]{3,2,1,0:T(8,128)(2,1)S(1)}, bf16[4,2,8,3200]{3,2,1,0:T(8,128)(2,1)S(1)}, u32[]{:S(2)}, u32[]{:S(2)}) collective-permute-start(bf16[4,2,8,3200]{3,2,1,0:T(8,128)(2,1)S(1)} %get-tuple-element.66), channel_id=1, source_target_pairs={{0,1},{1,0},{2,3},{3,2},{4,5},{5,4},{6,7},{7,6},{8,9},{9,8},{10,11... | collective-permute-start | bytes 1228808 | tf_op jit(solution)/shard_map/ppermute | solution.py:208
  43.2 0.8 copy-start.9
  44.0 10.2 %collective-permute-start.5 = (bf16[4,2,8,3200]{3,2,1,0:T(8,128)(2,1)S(1)}, bf16[4,2,8,3200]{3,2,1,0:T(8,128)(2,1)S(1)}, u32[]{:S(2)}, u32[]{:S(2)}) collective-permute-start(bf16[4,2,8,3200]{3,2,1,0:T(8,128)(2,1)S(1)} %get-tuple-element.70), channel_id=1, source_target_pairs={{0,2},{1,3},{2,0},{3,1},{4,6},{5,7},{6,4},{7,5},{8,10},{9,11},{10,... | collective-permute-start | bytes 1228808 | tf_op jit(solution)/shard_map/ppermute | solution.py:208
  48.9 34.2 %collective-permute-start.15 = (bf16[1024,256]{1,0:T(8,128)(2,1)}, bf16[1024,256]{1,0:T(8,128)(2,1)}, u32[]{:S(2)}, u32[]{:S(2)}) collective-permute-start(bf16[1024,256]{1,0:T(8,128)(2,1)} %get-tuple-element.91), channel_id=1, source_target_pairs={{32,0},{64,32},{96,64},{128,96},{160,128},{192,160},{224,192},{33,... | collective-permute-start | bytes 1572872 | tf_op jit(solution)/shard_map/ppermute | solution.py:202
  54.2 8.9 %copy-start.8 = (f32[1024,256]{1,0:T(8,128)S(1)}, f32[1024,256]{1,0:T(8,128)}, u32[]{:S(2)}) copy-start(f32[1024,256]{1,0:T(8,128)} %get-tuple-element.82.part) | copy-start | bytes 3145732
  54.2 8.9 %copy-start.10 = (bf16[1024,256]{1,0:T(8,128)(2,1)S(1)}, bf16[1024,256]{1,0:T(8,128)(2,1)}, u32[]{:S(2)}) copy-start(bf16[1024,256]{1,0:T(8,128)(2,1)} %copy-done.9) | copy-start | bytes 1572868
  54.8 28.2 %copy-start.7 = (f32[1024,256]{1,0:T(8,128)S(1)}, f32[1024,256]{1,0:T(8,128)}, u32[]{:S(2)}) copy-start(f32[1024,256]{1,0:T(8,128)} %get-tuple-element.90.part) | copy-start | bytes 3145732
  54.8 9.1 %collective-permute-start.6 = (bf16[2,8,3200]{2,1,0:T(8,128)(2,1)S(1)}, bf16[2,8,3200]{2,1,0:T(8,128)(2,1)S(1)}, u32[]{:S(2)}, u32[]{:S(2)}) collective-permute-start(bf16[2,8,3200]{2,1,0:T(8,128)(2,1)S(1)} %get-tuple-element.79), channel_id=1, source_target_pairs={{0,4},{1,5},{2,6},{3,7},{4,8},{5,9},{6,10},{7,11},{8,12},{9,13},{1... | collective-permute-start | bytes 307208 | tf_op jit(solution)/shard_map/ppermute | solution.py:208
  59.2 10.0 %collective-permute-start.7 = (bf16[2,8,3200]{2,1,0:T(8,128)(2,1)S(1)}, bf16[2,8,3200]{2,1,0:T(8,128)(2,1)S(1)}, u32[]{:S(2)}, u32[]{:S(2)}) collective-permute-start(bf16[2,8,3200]{2,1,0:T(8,128)(2,1)S(1)} %get-tuple-element.80), channel_id=1, source_target_pairs={{0,8},{1,9},{2,10},{3,11},{4,12},{5,13},{6,14},{7,15},{8,0},{9,1},... | collective-permute-start | bytes 307208 | tf_op jit(solution)/shard_map/ppermute | solution.py:208
  60.2 9.8 %collective-permute-start.8 = (bf16[2,8,3200]{2,1,0:T(8,128)(2,1)S(1)}, bf16[2,8,3200]{2,1,0:T(8,128)(2,1)S(1)}, u32[]{:S(2)}, u32[]{:S(2)}) collective-permute-start(bf16[2,8,3200]{2,1,0:T(8,128)(2,1)S(1)} %get-tuple-element.81), channel_id=1, source_target_pairs={{0,12},{1,13},{2,14},{3,15},{4,0},{5,1},{6,2},{7,3},{8,4},{9,5},{1... | collective-permute-start | bytes 307208 | tf_op jit(solution)/shard_map/ppermute | solution.py:208
  70.6 5.8 %collective-permute-start.10 = (bf16[8,3200]{1,0:T(8,128)(2,1)S(1)}, bf16[8,3200]{1,0:T(8,128)(2,1)S(1)}, u32[]{:S(2)}, u32[]{:S(2)}) collective-permute-start(bf16[8,3200]{1,0:T(8,128)(2,1)S(1)} %get-tuple-element.88.own), channel_id=1, source_target_pairs={{0,32},{1,33},{2,34},{3,35},{4,36},{5,37},{6,38},{7,39},{8,40},{9,... | collective-permute-start | bytes 153608 | tf_op jit(solution)/shard_map/ppermute | solution.py:224
  71.0 6.3 %collective-permute-start.11 = (bf16[8,3200]{1,0:T(8,128)(2,1)S(1)}, bf16[8,3200]{1,0:T(8,128)(2,1)S(1)}, u32[]{:S(2)}, u32[]{:S(2)}) collective-permute-start(bf16[8,3200]{1,0:T(8,128)(2,1)S(1)} %get-tuple-element.89), channel_id=1, source_target_pairs={{0,48},{1,49},{2,50},{3,51},{4,52},{5,53},{6,54},{7,55},{8,56},{9,... | collective-permute-start | bytes 153608 | tf_op jit(solution)/shard_map/ppermute | solution.py:224
  75.6 5.3 %collective-permute-start.9 = (bf16[8,3200]{1,0:T(8,128)(2,1)S(1)}, bf16[8,3200]{1,0:T(8,128)(2,1)S(1)}, u32[]{:S(2)}, u32[]{:S(2)}) collective-permute-start(bf16[8,3200]{1,0:T(8,128)(2,1)S(1)} %get-tuple-element.89), channel_id=1, source_target_pairs={{0,16},{1,17},{2,18},{3,19},{4,20},{5,21},{6,22},{7,23},{8,24},{9,... | collective-permute-start | bytes 153608 | tf_op jit(solution)/shard_map/ppermute | solution.py:224
  81.0 4.2 %collective-permute-start.14 = (bf16[8,3200]{1,0:T(8,128)(2,1)S(1)}, bf16[8,3200]{1,0:T(8,128)(2,1)S(1)}, u32[]{:S(2)}, u32[]{:S(2)}) collective-permute-start(bf16[8,3200]{1,0:T(8,128)(2,1)S(1)} %by_x.1.own), channel_id=1, source_target_pairs={{0,192},{32,224},{64,0},{96,32},{128,64},{160,96},{192,128},{224,1... | collective-permute-start | bytes 153608 | tf_op jit(solution)/shard_map/ppermute | solution.py:208
  81.0 5.7 %collective-permute-start.13 = (bf16[8,3200]{1,0:T(8,128)(2,1)S(1)}, bf16[8,3200]{1,0:T(8,128)(2,1)S(1)}, u32[]{:S(2)}, u32[]{:S(2)}) collective-permute-start(bf16[8,3200]{1,0:T(8,128)(2,1)S(1)} %by_x.1.own), channel_id=1, source_target_pairs={{0,128},{32,160},{64,192},{96,224},{128,0},{160,32},{192,64},{224,... | collective-permute-start | bytes 153608 | tf_op jit(solution)/shard_map/ppermute | solution.py:208
  81.2 6.6 %collective-permute-start.12 = (bf16[8,3200]{1,0:T(8,128)(2,1)S(1)}, bf16[8,3200]{1,0:T(8,128)(2,1)S(1)}, u32[]{:S(2)}, u32[]{:S(2)}) collective-permute-start(bf16[8,3200]{1,0:T(8,128)(2,1)S(1)} %by_x.1.own), channel_id=1, source_target_pairs={{0,64},{32,96},{64,128},{96,160},{128,192},{160,224},{192,0},{224,... | collective-permute-start | bytes 153608 | tf_op jit(solution)/shard_map/ppermute | solution.py:208

commit v4 on v3

--- a/solution.py
+++ b/solution.py
@@ -36,51 +36,61 @@
     dg[rows, :] = dot_t(oc[...], res_w[...]) + dot_t(sk[...], skip_w[...])
 
 
-def gates(base, h, d, oc, sk, z_now, dg, past_w, g_taps, g_heads, g_bias):
+def gates(base, d, z_now, dg, past_w):
     rows = tile_rows(base)
-    delayed = d[tile_rows(), :]
-    z = z_now[rows, :] + dot(delayed, past_w[...])
+    z = z_now[rows, :] + dot(d[tile_rows(), :], past_w[...])
     half = z.shape[1] // 2
     th = jnp.tanh(z[:, :half])
     sg = 0.5 * jnp.tanh(0.5 * z[:, half:]) + 0.5
     ts = th * sg
-    gated = ts.astype(BF16)
     dgated = dg[rows, :]
     dza = dgated * (sg - ts * th)
     dzb = dgated * (ts - ts * sg)
-    dz = jnp.concatenate([dza.astype(BF16), dzb.astype(BF16)], axis=1)
-    g_taps[...] += dot_rows(jnp.concatenate([h[rows, :], delayed], axis=1), dz)
+    return ts.astype(BF16), jnp.concatenate([dza.astype(BF16), dzb.astype(BF16)], axis=1)
+
+
+def weight_sums(base, gated, dz, h, d, oc, sk, g_taps, g_heads, g_bias):
+    rows = tile_rows(base)
+    inputs = jnp.concatenate([h[rows, :], d[tile_rows(), :]], axis=1)
+    g_taps[...] += dot_rows(inputs, dz)
     g_heads[...] += dot_rows(gated, jnp.concatenate([oc[rows, :], sk[rows, :]], axis=1))
-    g_bias[...] += jnp.sum(dz.astype(F32).reshape(-1, 8, 2 * half), axis=0)
-    return gated, dz
-
-
-def results(base, gated, dz, h, oc, now_w, past_w, res_w, skip_w, res, skip, part, back):
+    g_bias[...] += jnp.sum(dz.astype(F32).reshape(-1, 8, dz.shape[1]), axis=0)
+
+
+def results(base, gated, dz, h, oc, now_w, res_w, skip_w, res, skip, part):
     rows = tile_rows(base)
     res[...] = (h[rows, :].astype(F32) + dot(gated, res_w[...])).astype(BF16)
     skip[...] = dot(gated, skip_w[...]).astype(BF16)
     part[...] = oc[rows, :].astype(F32) + dot_t(dz, now_w[...])
-    back[...] = dot_t(dz, past_w[...]).astype(BF16)
-
-
-def first_kernel(h, d, oc, sk, z_now, dg, now_w, past_w, res_w, skip_w, *outs):
-    res, skip, part, back, g_taps, g_heads, g_bias = outs
+
+
+def first_kernel(d, z_now, dg, past_w, back, gated, dz):
+    rows = tile_rows()
+    gated_rows, dz_rows = gates(0, d, z_now, dg, past_w)
+    back[...] = dot_t(dz_rows, past_w[...]).astype(BF16)
+    gated[rows, :], dz[rows, :] = gated_rows, dz_rows
+
+
+def rest_kernel(gated, dz, h, d, oc, sk, now_w, res_w, skip_w, *outs):
+    res, skip, part, *sums = outs
 
     @pl.when(pl.program_id(0) == 0)
     def _():
-        for g in (g_taps, g_heads, g_bias):
+        for g in sums:
             g[...] = jnp.zeros_like(g)
 
-    gated, dz = gates(0, h, d, oc, sk, z_now, dg, past_w, g_taps, g_heads, g_bias)
-    results(0, gated, dz, h, oc, now_w, past_w, res_w, skip_w, res, skip, part, back)
+    rows = tile_rows()
+    gated_rows, dz_rows = gated[rows, :], dz[rows, :]
+    weight_sums(0, gated_rows, dz_rows, h, d, oc, sk, *sums)
+    results(0, gated_rows, dz_rows, h, oc, now_w, res_w, skip_w, res, skip, part)
 
 
 def last_kernel(base, place, h, d, oc, sk, z_now, dg, past_w, *rest):
     gated, dz, send0, send1, keep, g_taps, g_heads, g_bias = rest[3:]
     rows = tile_rows()
-    gated[rows, :], dz[rows, :] = gates(
-        base, h, d, oc, sk, z_now, dg, past_w, g_taps, g_heads, g_bias
-    )
+    gated_rows, dz_rows = gates(base, d, z_now, dg, past_w)
+    gated[rows, :], dz[rows, :] = gated_rows, dz_rows
+    weight_sums(base, gated_rows, dz_rows, h, d, oc, sk, g_taps, g_heads, g_bias)
     width = h.shape[1]
 
     @pl.when(pl.program_id(0) == pl.num_programs(0) - 1)
@@ -152,7 +162,10 @@
 
 def after_kernel(base, gated, dz, h, oc, now_w, past_w, res_w, skip_w, *rest):
     rows = tile_rows()
-    results(base, gated[rows, :], dz[rows, :], h, oc, now_w, past_w, res_w, skip_w, *rest[2:])
+    dz_rows = dz[rows, :]
+    *outs, back = rest[2:]
+    results(base, gated[rows, :], dz_rows, h, oc, now_w, res_w, skip_w, *outs)
+    back[...] = dot_t(dz_rows, past_w[...]).astype(BF16)
 
 
 def finish_kernel(part, came, *refs):
@@ -255,15 +268,25 @@
     ]
     tail_out = lambda n: [((n, width), F32, 1), ((n, width), BF16)]
     block = lambda base: pl.BlockSpec((TILE, width), lambda i: (base // TILE + i, 0))
-    res, skip, part0, back0, g_taps, g_heads, g_bias = call(
+    back0, gated0, dz0 = call(
         first_kernel,
         "first",
         first // TILE,
-        (h, d_first, oc, sk, z_now, dg, now_w, past_w, res_w, skip_w),
-        [VMEM] * 10,
-        rows_out + tail_out(first) + sums,
-        [block(0)] * 4 + [VMEM] * 3,
-        macs * 28 * first // total,
+        (d_first, z_now, dg, past_w),
+        [VMEM] * 4,
+        [((first, width), BF16), ((first, 2 * width), BF16), ((first, 4 * width), BF16)],
+        [block(0)] + [VMEM] * 2,
+        macs * 12 * first // total,
+    )
+    res, skip, part0, g_taps, g_heads, g_bias = call(
+        rest_kernel,
+        "rest",
+        first // TILE,
+        (gated0, dz0, h, d_first, oc, sk, now_w, res_w, skip_w),
+        [VMEM] * 9,
+        rows_out + tail_out(first)[:1] + sums,
+        [block(0)] * 3 + [VMEM] * 3,
+        1 << 20,
     )
     block_shape = (8, 12 * width + LANES)
     packed = (2, 4, 2, *block_shape)

time: 89.6 us -> 91.6 us (1.022)
  starting transfers between devices: 28.7 us -> 31.2 us
    ppermute x9, starting transfers between devices: 12.8 us -> 15.1 us  [exchange(): lax.ppermute(value, axis, [(i, partner(i)) for i in range(lax.axis_size(a...]
    pallas_call x11 -> x12, Pallas kernels: 23.9 us -> 24.5 us  [call(): pl.pallas_call(body, out_shape=[kind(s, t) for s, t, *_ in outs for kind...]
  transfers between devices with their start and end apart: 16 -> 16, of which waited for: 14 -> 13; matrix products, arithmetic and copies ran while one was open for 0% -> 0% of each run, Pallas kernels for 27% -> 27%
where the time goes in v4:
time: 91.6 us; the launch traced here: 91.2 us
  starting transfers between devices  31.2 us (34%)
  waiting for transfers between devices  30.7 us (34%)
  Pallas kernels  28.2 us (31%)
    pallas_call x12, Pallas kernels, call(): pl.pallas_call(body, out_shape=[kind(s, t) for s, t, *_ in outs for kind...  24.5 us
    ppermute x9, waiting for transfers between devices, exchange(): lax.ppermute(value, axis, [(i, partner(i)) for i in range(lax.axis_size(a...  15.5 us
    ppermute x9, starting transfers between devices, exchange(): lax.ppermute(value, axis, [(i, partner(i)) for i in range(lax.axis_size(a...  15.1 us
    ppermute x4, starting transfers between devices, shift(): lax.ppermute(value, 'tm', [(s, s + steps) for s in range(max(0, -steps),...  11 us
    ppermute x4, waiting for transfers between devices, shift(): lax.ppermute(value, 'tm', [(s, s + steps) for s in range(max(0, -steps),...  10.7 us
    ppermute x3, starting transfers between devices, along_x(): lax.ppermute(value, ('tm', 'dp'), [(i, target(i)) for i in range(256)])  5.14 us
    ppermute x3, waiting for transfers between devices, along_x(): lax.ppermute(value, ('tm', 'dp'), [(i, target(i)) for i in range(256)])  4.43 us
    pallas_call x2, Pallas kernels, copy_rows(): pl.pallas_call(functools.partial(copy_rows_kernel, base), out_shape=jax.S...  3.68 us
  transfers between devices with their start and end apart: 16, of which 13 were waited for; matrix products, arithmetic and copies ran while one was open for 0% of the time, Pallas kernels for 27%

profile of v4, /device:TPU:64, one launch (start us, length us, event | category | flops | bytes accessed | tf_op | source)
XLA Modules:
  0.0 91.2 jit_solution(13090222684759267628)
XLA Ops:
  0.6 1.8 %copy_rows.3 = bf16[1024,256]{1,0:T(8,128)(2,1)} custom-call(bf16[2048,256]{1,0:T(8,128)(2,1)} %bitcast.13), custom_call_target="tpu_custom_call" | custom-call | bytes 1048576 | tf_op jit(solution)/shard_map/copy_rows/pallas_call | solution.py:202
  2.5 5.0 %collective-permute-start.1 = (bf16[1024,256]{1,0:T(8,128)(2,1)}, bf16[1024,256]{1,0:T(8,128)(2,1)S(1)}, u32[]{:S(2)}, u32[]{:S(2)}) collective-permute-start(bf16[1024,256]{1,0:T(8,128)(2,1)} %copy_rows.3), channel_id=1, source_target_pairs={{0,32},{32,64},{64,96},{96,128},{128,160},{160,192},{192,224},{1,3... | collective-permute-start | bytes 1572872 | tf_op jit(solution)/shard_map/ppermute | solution.py:215
  7.5 1.8 %copy_rows.2 = bf16[1024,256]{1,0:T(8,128)(2,1)} custom-call(bf16[2048,256]{1,0:T(8,128)(2,1)} %bitcast.14), custom_call_target="tpu_custom_call" | custom-call | bytes 1048576 | tf_op jit(solution)/shard_map/copy_rows/pallas_call | solution.py:202
  9.3 3.4 %collective-permute-start = (bf16[1024,256]{1,0:T(8,128)(2,1)}, bf16[1024,256]{1,0:T(8,128)(2,1)S(1)}, u32[]{:S(2)}, u32[]{:S(2)}) collective-permute-start(bf16[1024,256]{1,0:T(8,128)(2,1)} %copy_rows.2), channel_id=1, source_target_pairs={{0,32},{32,64},{64,96},{96,128},{128,160},{160,192},{192,224},{1,3... | collective-permute-start | bytes 1572872 | tf_op jit(solution)/shard_map/ppermute | solution.py:215
  12.8 0.1 stack.23.place
  12.9 0.0 copy-start.2
  12.9 5.0 %before.1 = (f32[2048,1024]{1,0:T(8,128)S(1)}, f32[2048,512]{1,0:T(8,128)S(1)}) custom-call(bf16[2048,256]{1,0:T(8,128)(2,1)} %bitcast.15, bf16[2048,256]{1,0:T(8,128)(2,1)} %bitcast.19, bf16[2048,256]{1,0:T(8,128)(2,1)} %bitcast.23, bf16[256,1024]{1,0:T(8,128)(2,1)} %now_w.5, f32[1,1024]{1,0:T(1,128)} %bitcast.29, bf16[512,256]{1,0:T(8,128)(2,1)} %res_w.5, ...), custom_call_target="tpu_custom_call" | custom-call | flops 2147483648 | bytes 4194304 | tf_op jit(solution)/shard_map/before/pallas_call | solution.py:176
  17.9 2.2 %collective-permute-done.1.d = bf16[1024,256]{1,0:T(8,128)(2,1)S(1)} collective-permute-done((bf16[1024,256]{1,0:T(8,128)(2,1)}, bf16[1024,256]{1,0:T(8,128)(2,1)S(1)}, u32[]{:S(2)}, u32[]{:S(2)}) %collective-permute-start.1) | collective-permute-done | bytes 524320 | tf_op jit(solution)/shard_map/ppermute | solution.py:215
  20.0 0.0 copy-done.2
  20.0 0.0 copy-start
  20.1 0.0 copy-start.1
  20.1 0.0 copy-start.4
  20.1 0.0 copy-start.6
  20.1 0.0 copy-start.7
  20.1 2.4 %first.1 = (bf16[1024,256]{1,0:T(8,128)(2,1)S(1)}, bf16[1024,512]{1,0:T(8,128)(2,1)S(1)}, bf16[1024,1024]{1,0:T(8,128)(2,1)S(1)}) custom-call(bf16[1024,256]{1,0:T(8,128)(2,1)S(1)} %collective-permute-done.1.d, f32[2048,1024]{1,0:T(8,128)S(1)} %get-tuple-element.59.z_now, f32[2048,512]{1,0:T(8,128)S(1)} %get-tuple-element.60.dg, bf16[256,1024]{1,0:T(8,128)(2,1)S(1)} %copy-done.2), custom_call_target="tpu_custom_call" | custom-call | flops 1610612736 | bytes 3145728 | tf_op jit(solution)/shard_map/first/pallas_call | solution.py:176
  22.5 1.3 %collective-permute-start.4 = (bf16[1024,256]{1,0:T(8,128)(2,1)S(1)}, bf16[1024,256]{1,0:T(8,128)(2,1)S(1)}, u32[]{:S(2)}, u32[]{:S(2)}) collective-permute-start(bf16[1024,256]{1,0:T(8,128)(2,1)S(1)} %get-tuple-element.71), channel_id=1, source_target_pairs={{32,0},{64,32},{96,64},{128,96},{160,128},{192,160},{224,192},{33,... | collective-permute-start | bytes 1572872 | tf_op jit(solution)/shard_map/ppermute | solution.py:215
  23.8 0.0 copy-done
  23.8 0.0 copy-done.1
  23.8 0.0 copy-done.3
  23.8 0.0 copy-done.4
  23.8 0.0 copy-done.6
  23.8 0.0 copy-done.7
  23.8 4.3 %rest.1 = (bf16[2048,256]{1,0:T(8,128)(2,1)}, bf16[2048,256]{1,0:T(8,128)(2,1)}, f32[1024,256]{1,0:T(8,128)}, f32[512,1024]{1,0:T(8,128)S(1)}, f32[512,512]{1,0:T(8,128)S(1)}, /*index=5*/f32[8,1024]{1,0:T(8,128)S(1)}) custom-call(bf16[1024,512]{1,0:T(8,128)(2,1)S(1)} %get-tuple-element.61.gated, bf16[1024,1024]{1,0:T(8,128)(2,1)S(1)} %get-tuple-element.62.dz, ...), custom_call_target="tpu_custom_call" | custom-call | flops 1048576 | bytes 2048 | tf_op jit(solution)/shard_map/rest/pallas_call | solution.py:176
  28.1 2.0 %collective-permute-done.d = bf16[1024,256]{1,0:T(8,128)(2,1)S(1)} collective-permute-done((bf16[1024,256]{1,0:T(8,128)(2,1)}, bf16[1024,256]{1,0:T(8,128)(2,1)S(1)}, u32[]{:S(2)}, u32[]{:S(2)}) %collective-permute-start) | collective-permute-done | bytes 524320 | tf_op jit(solution)/shard_map/ppermute | solution.py:215
  30.1 4.1 %last.1 = (bf16[1024,512]{1,0:T(8,128)(2,1)S(1)}, bf16[1024,1024]{1,0:T(8,128)(2,1)S(1)}, bf16[4,2,8,3200]{3,2,1,0:T(8,128)(2,1)S(1)}, bf16[4,2,8,3200]{3,2,1,0:...) custom-call(s32[5]{0:T(128)S(1)} %stack.23.place, ...), custom_call_target="tpu_custom_call", output_to_operand_aliasing={{5}: (8, {}), {6}: (9, {}), {7}: (10, {})} | custom-call | flops 1048576 | bytes 2048 | tf_op jit(solution)/shard_map/last/pallas_call | solution.py:176
  34.3 0.1 collective-permute-start.2
  34.4 0.5 collective-permute-start.3
  34.9 1.2 %collective-permute-done.2.came0 = bf16[4,2,8,3200]{3,2,1,0:T(8,128)(2,1)S(1)} collective-permute-done((bf16[4,2,8,3200]{3,2,1,0:T(8,128)(2,1)S(1)}, bf16[4,2,8,3200]{3,2,1,0:T(8,128)(2,1)S(1)}, u32[]{:S(2)}, u32[]{:S(2)}) %collective-permute-start.2) | collective-permute-done | bytes 409632 | tf_op jit(solution)/shard_map/ppermute | solution.py:221
  36.1 0.6 collective-permute-done.3.came1
  36.7 6.5 %collective-permute-done.4.came = bf16[1024,256]{1,0:T(8,128)(2,1)S(1)} collective-permute-done((bf16[1024,256]{1,0:T(8,128)(2,1)S(1)}, bf16[1024,256]{1,0:T(8,128)(2,1)S(1)}, u32[]{:S(2)}, u32[]{:S(2)}) %collective-permute-start.4) | collective-permute-done | bytes 524320 | tf_op jit(solution)/shard_map/ppermute | solution.py:215
  43.2 0.7 by_core.1
  43.9 0.1 copy-done.9
  44.1 1.9 %collective-permute-start.5 = (bf16[4,2,8,3200]{3,2,1,0:T(8,128)(2,1)S(1)}, bf16[4,2,8,3200]{3,2,1,0:T(8,128)(2,1)S(1)}, u32[]{:S(2)}, u32[]{:S(2)}) collective-permute-start(bf16[4,2,8,3200]{3,2,1,0:T(8,128)(2,1)S(1)} %get-tuple-element.74), channel_id=1, source_target_pairs={{0,2},{1,3},{2,0},{3,1},{4,6},{5,7},{6,4},{7,5},{8,10},{9,11},{10,... | collective-permute-start | bytes 1228808 | tf_op jit(solution)/shard_map/ppermute | solution.py:221
  46.0 2.9 %after.1 = (bf16[2048,256]{1,0:T(8,128)(2,1)}, bf16[2048,256]{1,0:T(8,128)(2,1)}, f32[1024,256]{1,0:T(8,128)}, bf16[1024,256]{1,0:T(8,128)(2,1)}) custom-call(bf16[1024,512]{1,0:T(8,128)(2,1)S(1)} %get-tuple-element.75.gated, bf16[1024,1024]{1,0:T(8,128)(2,1)S(1)} %get-tuple-element.76.dz, ...), custom_call_target="tpu_custom_call", output_to_operand_aliasing={{0}: (8, {}), {1}: (9, {})} | custom-call | flops 1610612736 | bytes 3145728 | tf_op jit(solution)/shard_map/after/pallas_call | solution.py:176
  48.9 1.3 %collective-permute-start.15 = (bf16[1024,256]{1,0:T(8,128)(2,1)}, bf16[1024,256]{1,0:T(8,128)(2,1)}, u32[]{:S(2)}, u32[]{:S(2)}) collective-permute-start(bf16[1024,256]{1,0:T(8,128)(2,1)} %get-tuple-element.95), channel_id=1, source_target_pairs={{32,0},{64,32},{96,64},{128,96},{160,128},{192,160},{224,192},{33,... | collective-permute-start | bytes 1572872 | tf_op jit(solution)/shard_map/ppermute | solution.py:215
  50.2 4.4 %collective-permute-done.5.came = bf16[4,2,8,3200]{3,2,1,0:T(8,128)(2,1)S(1)} collective-permute-done((bf16[4,2,8,3200]{3,2,1,0:T(8,128)(2,1)S(1)}, bf16[4,2,8,3200]{3,2,1,0:T(8,128)(2,1)S(1)}, u32[]{:S(2)}, u32[]{:S(2)}) %collective-permute-start.5) | collective-permute-done | bytes 409632 | tf_op jit(solution)/shard_map/ppermute | solution.py:221
  54.6 0.6 by_pair.1
  55.2 0.0 copy-start.5
  55.2 4.4 %collective-permute-start.6 = (bf16[2,8,3200]{2,1,0:T(8,128)(2,1)S(1)}, bf16[2,8,3200]{2,1,0:T(8,128)(2,1)S(1)}, u32[]{:S(2)}, u32[]{:S(2)}) collective-permute-start(bf16[2,8,3200]{2,1,0:T(8,128)(2,1)S(1)} %get-tuple-element.83), channel_id=1, source_target_pairs={{0,4},{1,5},{2,6},{3,7},{4,8},{5,9},{6,10},{7,11},{8,12},{9,13},{1... | collective-permute-start | bytes 307208 | tf_op jit(solution)/shard_map/ppermute | solution.py:221
  59.6 1.0 %collective-permute-start.7 = (bf16[2,8,3200]{2,1,0:T(8,128)(2,1)S(1)}, bf16[2,8,3200]{2,1,0:T(8,128)(2,1)S(1)}, u32[]{:S(2)}, u32[]{:S(2)}) collective-permute-start(bf16[2,8,3200]{2,1,0:T(8,128)(2,1)S(1)} %get-tuple-element.84), channel_id=1, source_target_pairs={{0,8},{1,9},{2,10},{3,11},{4,12},{5,13},{6,14},{7,15},{8,0},{9,1},... | collective-permute-start | bytes 307208 | tf_op jit(solution)/shard_map/ppermute | solution.py:221
  60.6 2.8 %collective-permute-start.8 = (bf16[2,8,3200]{2,1,0:T(8,128)(2,1)S(1)}, bf16[2,8,3200]{2,1,0:T(8,128)(2,1)S(1)}, u32[]{:S(2)}, u32[]{:S(2)}) collective-permute-start(bf16[2,8,3200]{2,1,0:T(8,128)(2,1)S(1)} %get-tuple-element.85), channel_id=1, source_target_pairs={{0,12},{1,13},{2,14},{3,15},{4,0},{5,1},{6,2},{7,3},{8,4},{9,5},{1... | collective-permute-start | bytes 307208 | tf_op jit(solution)/shard_map/ppermute | solution.py:221
  63.4 0.0 copy-done.8
  63.4 0.0 copy-done.10
  63.4 0.8 finish.2.refs_0_
  64.3 0.0 collective-permute-done.6.one
  64.3 5.1 %collective-permute-done.7.two = bf16[2,8,3200]{2,1,0:T(8,128)(2,1)S(1)} collective-permute-done((bf16[2,8,3200]{2,1,0:T(8,128)(2,1)S(1)}, bf16[2,8,3200]{2,1,0:T(8,128)(2,1)S(1)}, u32[]{:S(2)}, u32[]{:S(2)}) %collective-permute-start.7) | collective-permute-done | bytes 102432 | tf_op jit(solution)/shard_map/ppermute | solution.py:221
  69.4 1.3 %collective-permute-done.8.three = bf16[2,8,3200]{2,1,0:T(8,128)(2,1)S(1)} collective-permute-done((bf16[2,8,3200]{2,1,0:T(8,128)(2,1)S(1)}, bf16[2,8,3200]{2,1,0:T(8,128)(2,1)S(1)}, u32[]{:S(2)}, u32[]{:S(2)}) %collective-permute-start.8) | collective-permute-done | bytes 102432 | tf_op jit(solution)/shard_map/ppermute | solution.py:221
  70.8 0.6 by_z.1
  71.4 3.1 %collective-permute-start.10 = (bf16[8,3200]{1,0:T(8,128)(2,1)S(1)}, bf16[8,3200]{1,0:T(8,128)(2,1)S(1)}, u32[]{:S(2)}, u32[]{:S(2)}) collective-permute-start(bf16[8,3200]{1,0:T(8,128)(2,1)S(1)} %get-tuple-element.92.own), channel_id=1, source_target_pairs={{0,32},{1,33},{2,34},{3,35},{4,36},{5,37},{6,38},{7,39},{8,40},{9,... | collective-permute-start | bytes 153608 | tf_op jit(solution)/shard_map/ppermute | solution.py:237
  74.5 1.1 %collective-permute-start.11 = (bf16[8,3200]{1,0:T(8,128)(2,1)S(1)}, bf16[8,3200]{1,0:T(8,128)(2,1)S(1)}, u32[]{:S(2)}, u32[]{:S(2)}) collective-permute-start(bf16[8,3200]{1,0:T(8,128)(2,1)S(1)} %get-tuple-element.93), channel_id=1, source_target_pairs={{0,48},{1,49},{2,50},{3,51},{4,52},{5,53},{6,54},{7,55},{8,56},{9,... | collective-permute-start | bytes 153608 | tf_op jit(solution)/shard_map/ppermute | solution.py:237
  75.6 0.9 collective-permute-start.9
  76.5 0.6 collective-permute-done.10.two
  77.1 1.5 %collective-permute-done.11.three = bf16[8,3200]{1,0:T(8,128)(2,1)S(1)} collective-permute-done((bf16[8,3200]{1,0:T(8,128)(2,1)S(1)}, bf16[8,3200]{1,0:T(8,128)(2,1)S(1)}, u32[]{:S(2)}, u32[]{:S(2)}) %collective-permute-start.11) | collective-permute-done | bytes 51232 | tf_op jit(solution)/shard_map/ppermute | solution.py:237
  78.6 2.4 %collective-permute-done.9.one = bf16[8,3200]{1,0:T(8,128)(2,1)S(1)} collective-permute-done((bf16[8,3200]{1,0:T(8,128)(2,1)S(1)}, bf16[8,3200]{1,0:T(8,128)(2,1)S(1)}, u32[]{:S(2)}, u32[]{:S(2)}) %collective-permute-start.9) | collective-permute-done | bytes 51232 | tf_op jit(solution)/shard_map/ppermute | solution.py:237
  81.0 1.0 %collective-permute-start.14 = (bf16[8,3200]{1,0:T(8,128)(2,1)S(1)}, bf16[8,3200]{1,0:T(8,128)(2,1)S(1)}, u32[]{:S(2)}, u32[]{:S(2)}) collective-permute-start(bf16[8,3200]{1,0:T(8,128)(2,1)S(1)} %by_x.1.own), channel_id=1, source_target_pairs={{0,192},{32,224},{64,0},{96,32},{128,64},{160,96},{192,128},{224,1... | collective-permute-start | bytes 153608 | tf_op jit(solution)/shard_map/ppermute | solution.py:221
  82.0 2.7 %collective-permute-start.13 = (bf16[8,3200]{1,0:T(8,128)(2,1)S(1)}, bf16[8,3200]{1,0:T(8,128)(2,1)S(1)}, u32[]{:S(2)}, u32[]{:S(2)}) collective-permute-start(bf16[8,3200]{1,0:T(8,128)(2,1)S(1)} %by_x.1.own), channel_id=1, source_target_pairs={{0,128},{32,160},{64,192},{96,224},{128,0},{160,32},{192,64},{224,... | collective-permute-start | bytes 153608 | tf_op jit(solution)/shard_map/ppermute | solution.py:221
  84.7 0.7 collective-permute-start.12
  85.4 0.0 collective-permute-done.15.came
  85.4 0.0 copy-done.5
  85.4 1.8 %finish.3 = bf16[2048,256]{1,0:T(8,128)(2,1)} custom-call(f32[1024,256]{1,0:T(8,128)S(1)} %copy-done.5, bf16[1024,256]{1,0:T(8,128)(2,1)} %collective-permute-done.15.came, bf16[2048,256]{1,0:T(8,128)(2,1)} %finish.2.refs_0_), custom_call_target="tpu_custom_call", output_to_operand_aliasing={{}: (2, {})} | custom-call | flops 268435456 | bytes 524288 | tf_op jit(solution)/shard_map/finish/pallas_call | solution.py:176
  87.2 0.0 collective-permute-done.14.three
  87.2 0.4 collective-permute-done.13.two
  87.6 2.4 %collective-permute-done.12.one = bf16[8,3200]{1,0:T(8,128)(2,1)S(1)} collective-permute-done((bf16[8,3200]{1,0:T(8,128)(2,1)S(1)}, bf16[8,3200]{1,0:T(8,128)(2,1)S(1)}, u32[]{:S(2)}, u32[]{:S(2)}) %collective-permute-start.12) | collective-permute-done | bytes 51232 | tf_op jit(solution)/shard_map/ppermute | solution.py:221
  90.0 1.2 %owner.1 = (f32[8,1024]{1,0:T(8,128)}, f32[8,1024]{1,0:T(8,128)}, f32[16,256]{1,0:T(8,128)}, f32[16,256]{1,0:T(8,128)}, f32[1,32]{1,0:T(1,128)}) custom-call(s32[5]{0:T(128)S(1)} %stack.23.place, bf16[8,3200]{1,0:T(8,128)(2,1)S(1)} %by_x.1.own, bf16[8,3200]{1,0:T(8,128)(2,1)S(1)} %collective-permute-done.12.one, ...), custom_call_target="tpu_custom_call" | custom-call | flops 1048576 | bytes 2048 | tf_op jit(solution)/shard_map/owner/pallas_call | solution.py:176
  (5 shorter events, 0.0 us)
Async XLA Ops:
  2.5 17.6 %collective-permute-start.1 = (bf16[1024,256]{1,0:T(8,128)(2,1)}, bf16[1024,256]{1,0:T(8,128)(2,1)S(1)}, u32[]{:S(2)}, u32[]{:S(2)}) collective-permute-start(bf16[1024,256]{1,0:T(8,128)(2,1)} %copy_rows.3), channel_id=1, source_target_pairs={{0,32},{32,64},{64,96},{96,128},{128,160},{160,192},{192,224},{1,3... | collective-permute-start | bytes 1572872 | tf_op jit(solution)/shard_map/ppermute | solution.py:215
  9.3 20.8 %collective-permute-start = (bf16[1024,256]{1,0:T(8,128)(2,1)}, bf16[1024,256]{1,0:T(8,128)(2,1)S(1)}, u32[]{:S(2)}, u32[]{:S(2)}) collective-permute-start(bf16[1024,256]{1,0:T(8,128)(2,1)} %copy_rows.2), channel_id=1, source_target_pairs={{0,32},{32,64},{64,96},{96,128},{128,160},{160,192},{192,224},{1,3... | collective-permute-start | bytes 1572872 | tf_op jit(solution)/shard_map/ppermute | solution.py:215
  12.9 7.2 %copy-start.2 = (bf16[256,1024]{1,0:T(8,128)(2,1)S(1)}, bf16[256,1024]{1,0:T(8,128)(2,1)}, u32[]{:S(2)}) copy-start(bf16[256,1024]{1,0:T(8,128)(2,1)} %past_w.5) | copy-start | bytes 1572868
  20.0 3.7 %copy-start = (bf16[1,2048,256]{2,1,0:T(8,128)(2,1)S(1)}, bf16[1,2048,256]{2,1,0:T(8,128)(2,1)}, u32[]{:S(2)}) copy-start(bf16[1,2048,256]{2,1,0:T(8,128)(2,1)} %param.8) | copy-start | bytes 3145732
  20.1 3.7 %copy-start.1 = (bf16[1,2048,256]{2,1,0:T(8,128)(2,1)S(1)}, bf16[1,2048,256]{2,1,0:T(8,128)(2,1)}, u32[]{:S(2)}) copy-start(bf16[1,2048,256]{2,1,0:T(8,128)(2,1)} %param.14) | copy-start | bytes 3145732
  20.1 3.7 %copy-start.3 = (bf16[1,2048,256]{2,1,0:T(8,128)(2,1)S(1)}, bf16[1,2048,256]{2,1,0:T(8,128)(2,1)}, u32[]{:S(2)}) copy-start(bf16[1,2048,256]{2,1,0:T(8,128)(2,1)} %param.15) | copy-start | bytes 3145732
  20.1 3.8 %copy-start.4 = (bf16[256,1024]{1,0:T(8,128)(2,1)S(1)}, bf16[256,1024]{1,0:T(8,128)(2,1)}, u32[]{:S(2)}) copy-start(bf16[256,1024]{1,0:T(8,128)(2,1)} %now_w.5) | copy-start | bytes 1572868
  20.1 3.8 %copy-start.6 = (bf16[512,256]{1,0:T(8,128)(2,1)S(1)}, bf16[512,256]{1,0:T(8,128)(2,1)}, u32[]{:S(2)}) copy-start(bf16[512,256]{1,0:T(8,128)(2,1)} %res_w.5) | copy-start | bytes 786436
  20.1 3.7 %copy-start.7 = (bf16[512,256]{1,0:T(8,128)(2,1)S(1)}, bf16[512,256]{1,0:T(8,128)(2,1)}, u32[]{:S(2)}) copy-start(bf16[512,256]{1,0:T(8,128)(2,1)} %skip_w.5) | copy-start | bytes 786436
  22.5 20.8 %collective-permute-start.4 = (bf16[1024,256]{1,0:T(8,128)(2,1)S(1)}, bf16[1024,256]{1,0:T(8,128)(2,1)S(1)}, u32[]{:S(2)}, u32[]{:S(2)}) collective-permute-start(bf16[1024,256]{1,0:T(8,128)(2,1)S(1)} %get-tuple-element.71), channel_id=1, source_target_pairs={{32,0},{64,32},{96,64},{128,96},{160,128},{192,160},{224,192},{33,... | collective-permute-start | bytes 1572872 | tf_op jit(solution)/shard_map/ppermute | solution.py:215
  34.3 1.8 %collective-permute-start.2 = (bf16[4,2,8,3200]{3,2,1,0:T(8,128)(2,1)S(1)}, bf16[4,2,8,3200]{3,2,1,0:T(8,128)(2,1)S(1)}, u32[]{:S(2)}, u32[]{:S(2)}) collective-permute-start(bf16[4,2,8,3200]{3,2,1,0:T(8,128)(2,1)S(1)} %get-tuple-element.69), channel_id=1, source_target_pairs={{0,1},{1,0},{2,3},{3,2},{4,5},{5,4},{6,7},{7,6},{8,9},{9,8},{10,11... | collective-permute-start | bytes 1228808 | tf_op jit(solution)/shard_map/ppermute | solution.py:221
  34.4 2.3 %collective-permute-start.3 = (bf16[4,2,8,3200]{3,2,1,0:T(8,128)(2,1)S(1)}, bf16[4,2,8,3200]{3,2,1,0:T(8,128)(2,1)S(1)}, u32[]{:S(2)}, u32[]{:S(2)}) collective-permute-start(bf16[4,2,8,3200]{3,2,1,0:T(8,128)(2,1)S(1)} %get-tuple-element.70), channel_id=1, source_target_pairs={{0,1},{1,0},{2,3},{3,2},{4,5},{5,4},{6,7},{7,6},{8,9},{9,8},{10,11... | collective-permute-start | bytes 1228808 | tf_op jit(solution)/shard_map/ppermute | solution.py:221
  43.2 0.8 copy-start.9
  44.1 10.5 %collective-permute-start.5 = (bf16[4,2,8,3200]{3,2,1,0:T(8,128)(2,1)S(1)}, bf16[4,2,8,3200]{3,2,1,0:T(8,128)(2,1)S(1)}, u32[]{:S(2)}, u32[]{:S(2)}) collective-permute-start(bf16[4,2,8,3200]{3,2,1,0:T(8,128)(2,1)S(1)} %get-tuple-element.74), channel_id=1, source_target_pairs={{0,2},{1,3},{2,0},{3,1},{4,6},{5,7},{6,4},{7,5},{8,10},{9,11},{10,... | collective-permute-start | bytes 1228808 | tf_op jit(solution)/shard_map/ppermute | solution.py:221
  48.9 36.5 %collective-permute-start.15 = (bf16[1024,256]{1,0:T(8,128)(2,1)}, bf16[1024,256]{1,0:T(8,128)(2,1)}, u32[]{:S(2)}, u32[]{:S(2)}) collective-permute-start(bf16[1024,256]{1,0:T(8,128)(2,1)} %get-tuple-element.95), channel_id=1, source_target_pairs={{32,0},{64,32},{96,64},{128,96},{160,128},{192,160},{224,192},{33,... | collective-permute-start | bytes 1572872 | tf_op jit(solution)/shard_map/ppermute | solution.py:215
  54.6 8.9 %copy-start.8 = (f32[1024,256]{1,0:T(8,128)S(1)}, f32[1024,256]{1,0:T(8,128)}, u32[]{:S(2)}) copy-start(f32[1024,256]{1,0:T(8,128)} %get-tuple-element.86.part) | copy-start | bytes 3145732
  54.6 8.9 %copy-start.10 = (bf16[1024,256]{1,0:T(8,128)(2,1)S(1)}, bf16[1024,256]{1,0:T(8,128)(2,1)}, u32[]{:S(2)}) copy-start(bf16[1024,256]{1,0:T(8,128)(2,1)} %copy-done.9) | copy-start | bytes 1572868
  55.2 30.2 %copy-start.5 = (f32[1024,256]{1,0:T(8,128)S(1)}, f32[1024,256]{1,0:T(8,128)}, u32[]{:S(2)}) copy-start(f32[1024,256]{1,0:T(8,128)} %get-tuple-element.94.part) | copy-start | bytes 3145732
  55.2 9.1 %collective-permute-start.6 = (bf16[2,8,3200]{2,1,0:T(8,128)(2,1)S(1)}, bf16[2,8,3200]{2,1,0:T(8,128)(2,1)S(1)}, u32[]{:S(2)}, u32[]{:S(2)}) collective-permute-start(bf16[2,8,3200]{2,1,0:T(8,128)(2,1)S(1)} %get-tuple-element.83), channel_id=1, source_target_pairs={{0,4},{1,5},{2,6},{3,7},{4,8},{5,9},{6,10},{7,11},{8,12},{9,13},{1... | collective-permute-start | bytes 307208 | tf_op jit(solution)/shard_map/ppermute | solution.py:221
  59.6 9.8 %collective-permute-start.7 = (bf16[2,8,3200]{2,1,0:T(8,128)(2,1)S(1)}, bf16[2,8,3200]{2,1,0:T(8,128)(2,1)S(1)}, u32[]{:S(2)}, u32[]{:S(2)}) collective-permute-start(bf16[2,8,3200]{2,1,0:T(8,128)(2,1)S(1)} %get-tuple-element.84), channel_id=1, source_target_pairs={{0,8},{1,9},{2,10},{3,11},{4,12},{5,13},{6,14},{7,15},{8,0},{9,1},... | collective-permute-start | bytes 307208 | tf_op jit(solution)/shard_map/ppermute | solution.py:221
  60.6 10.1 %collective-permute-start.8 = (bf16[2,8,3200]{2,1,0:T(8,128)(2,1)S(1)}, bf16[2,8,3200]{2,1,0:T(8,128)(2,1)S(1)}, u32[]{:S(2)}, u32[]{:S(2)}) collective-permute-start(bf16[2,8,3200]{2,1,0:T(8,128)(2,1)S(1)} %get-tuple-element.85), channel_id=1, source_target_pairs={{0,12},{1,13},{2,14},{3,15},{4,0},{5,1},{6,2},{7,3},{8,4},{9,5},{1... | collective-permute-start | bytes 307208 | tf_op jit(solution)/shard_map/ppermute | solution.py:221
  71.4 5.7 %collective-permute-start.10 = (bf16[8,3200]{1,0:T(8,128)(2,1)S(1)}, bf16[8,3200]{1,0:T(8,128)(2,1)S(1)}, u32[]{:S(2)}, u32[]{:S(2)}) collective-permute-start(bf16[8,3200]{1,0:T(8,128)(2,1)S(1)} %get-tuple-element.92.own), channel_id=1, source_target_pairs={{0,32},{1,33},{2,34},{3,35},{4,36},{5,37},{6,38},{7,39},{8,40},{9,... | collective-permute-start | bytes 153608 | tf_op jit(solution)/shard_map/ppermute | solution.py:237
  74.5 4.1 %collective-permute-start.11 = (bf16[8,3200]{1,0:T(8,128)(2,1)S(1)}, bf16[8,3200]{1,0:T(8,128)(2,1)S(1)}, u32[]{:S(2)}, u32[]{:S(2)}) collective-permute-start(bf16[8,3200]{1,0:T(8,128)(2,1)S(1)} %get-tuple-element.93), channel_id=1, source_target_pairs={{0,48},{1,49},{2,50},{3,51},{4,52},{5,53},{6,54},{7,55},{8,56},{9,... | collective-permute-start | bytes 153608 | tf_op jit(solution)/shard_map/ppermute | solution.py:237
  75.6 5.3 %collective-permute-start.9 = (bf16[8,3200]{1,0:T(8,128)(2,1)S(1)}, bf16[8,3200]{1,0:T(8,128)(2,1)S(1)}, u32[]{:S(2)}, u32[]{:S(2)}) collective-permute-start(bf16[8,3200]{1,0:T(8,128)(2,1)S(1)} %get-tuple-element.93), channel_id=1, source_target_pairs={{0,16},{1,17},{2,18},{3,19},{4,20},{5,21},{6,22},{7,23},{8,24},{9,... | collective-permute-start | bytes 153608 | tf_op jit(solution)/shard_map/ppermute | solution.py:237
  81.0 6.2 %collective-permute-start.14 = (bf16[8,3200]{1,0:T(8,128)(2,1)S(1)}, bf16[8,3200]{1,0:T(8,128)(2,1)S(1)}, u32[]{:S(2)}, u32[]{:S(2)}) collective-permute-start(bf16[8,3200]{1,0:T(8,128)(2,1)S(1)} %by_x.1.own), channel_id=1, source_target_pairs={{0,192},{32,224},{64,0},{96,32},{128,64},{160,96},{192,128},{224,1... | collective-permute-start | bytes 153608 | tf_op jit(solution)/shard_map/ppermute | solution.py:221
  82.0 5.6 %collective-permute-start.13 = (bf16[8,3200]{1,0:T(8,128)(2,1)S(1)}, bf16[8,3200]{1,0:T(8,128)(2,1)S(1)}, u32[]{:S(2)}, u32[]{:S(2)}) collective-permute-start(bf16[8,3200]{1,0:T(8,128)(2,1)S(1)} %by_x.1.own), channel_id=1, source_target_pairs={{0,128},{32,160},{64,192},{96,224},{128,0},{160,32},{192,64},{224,... | collective-permute-start | bytes 153608 | tf_op jit(solution)/shard_map/ppermute | solution.py:221
  84.7 5.3 %collective-permute-start.12 = (bf16[8,3200]{1,0:T(8,128)(2,1)S(1)}, bf16[8,3200]{1,0:T(8,128)(2,1)S(1)}, u32[]{:S(2)}, u32[]{:S(2)}) collective-permute-start(bf16[8,3200]{1,0:T(8,128)(2,1)S(1)} %by_x.1.own), channel_id=1, source_target_pairs={{0,64},{32,96},{64,128},{96,160},{128,192},{160,224},{192,0},{224,... | collective-permute-start | bytes 153608 | tf_op jit(solution)/shard_map/ppermute | solution.py:221

commit v5 on v3

--- a/solution.py
+++ b/solution.py
@@ -9,7 +9,6 @@
 
 BF16, F32 = jnp.bfloat16, jnp.float32
 TILE = 512
-CHUNKS = (1024, 1024)
 LANES = 128
 VMEM = pl.BlockSpec(memory_space=pltpu.VMEM)
 
@@ -36,52 +35,48 @@
     dg[rows, :] = dot_t(oc[...], res_w[...]) + dot_t(sk[...], skip_w[...])
 
 
-def gates(base, h, d, oc, sk, z_now, dg, past_w, g_taps, g_heads, g_bias):
-    rows = tile_rows(base)
-    delayed = d[tile_rows(), :]
-    z = z_now[rows, :] + dot(delayed, past_w[...])
+def gates(rows, d, z_now, dg, past_w):
+    z = z_now[rows, :] + dot(d[rows, :], past_w[...])
     half = z.shape[1] // 2
     th = jnp.tanh(z[:, :half])
     sg = 0.5 * jnp.tanh(0.5 * z[:, half:]) + 0.5
     ts = th * sg
-    gated = ts.astype(BF16)
     dgated = dg[rows, :]
     dza = dgated * (sg - ts * th)
     dzb = dgated * (ts - ts * sg)
-    dz = jnp.concatenate([dza.astype(BF16), dzb.astype(BF16)], axis=1)
-    g_taps[...] += dot_rows(jnp.concatenate([h[rows, :], delayed], axis=1), dz)
-    g_heads[...] += dot_rows(gated, jnp.concatenate([oc[rows, :], sk[rows, :]], axis=1))
-    g_bias[...] += jnp.sum(dz.astype(F32).reshape(-1, 8, 2 * half), axis=0)
-    return gated, dz
-
-
-def results(base, gated, dz, h, oc, now_w, past_w, res_w, skip_w, res, skip, part, back):
+    return ts.astype(BF16), jnp.concatenate([dza.astype(BF16), dzb.astype(BF16)], axis=1)
+
+
+def weight_sums(rows, gated, dz, h, d, oc, sk):
+    return (
+        dot_rows(jnp.concatenate([h[rows, :], d[rows, :]], axis=1), dz),
+        dot_rows(gated, jnp.concatenate([oc[rows, :], sk[rows, :]], axis=1)),
+        jnp.sum(dz.astype(F32).reshape(-1, 8, dz.shape[1]), axis=0),
+    )
+
+
+def results(base, gated, dz, h, oc, now_w, res_w, skip_w, res, skip, part):
     rows = tile_rows(base)
     res[...] = (h[rows, :].astype(F32) + dot(gated, res_w[...])).astype(BF16)
     skip[...] = dot(gated, skip_w[...]).astype(BF16)
     part[...] = oc[rows, :].astype(F32) + dot_t(dz, now_w[...])
-    back[...] = dot_t(dz, past_w[...]).astype(BF16)
-
-
-def first_kernel(h, d, oc, sk, z_now, dg, now_w, past_w, res_w, skip_w, *outs):
-    res, skip, part, back, g_taps, g_heads, g_bias = outs
-
-    @pl.when(pl.program_id(0) == 0)
-    def _():
-        for g in (g_taps, g_heads, g_bias):
-            g[...] = jnp.zeros_like(g)
-
-    gated, dz = gates(0, h, d, oc, sk, z_now, dg, past_w, g_taps, g_heads, g_bias)
-    results(0, gated, dz, h, oc, now_w, past_w, res_w, skip_w, res, skip, part, back)
-
-
-def last_kernel(base, place, h, d, oc, sk, z_now, dg, past_w, *rest):
-    gated, dz, send0, send1, keep, g_taps, g_heads, g_bias = rest[3:]
-    rows = tile_rows()
-    gated[rows, :], dz[rows, :] = gates(
-        base, h, d, oc, sk, z_now, dg, past_w, g_taps, g_heads, g_bias
-    )
+
+
+def last_kernel(place, h, d, oc, sk, z_now, dg, past_w, *rest):
+    gated, dz, send0, send1, keep, *sums = rest
+    g_taps, g_heads, g_bias = sums
     width = h.shape[1]
+    before = None
+    for tile in range(h.shape[0] // TILE + 1):
+        now = None
+        if tile * TILE < h.shape[0]:
+            rows = slice(tile * TILE, (tile + 1) * TILE)
+            now = (rows, *gates(rows, d, z_now, dg, past_w))
+            gated[rows, :], dz[rows, :] = now[1:]
+        if before is not None:
+            for g, term in zip(sums, weight_sums(*before, h, d, oc, sk)):
+                g[...] = term if tile == 1 else g[...] + term
+        before = now
 
     @pl.when(pl.program_id(0) == pl.num_programs(0) - 1)
     def _():
@@ -150,9 +145,13 @@
             g_bias[...] = sums[:, m * 32 : (m + 1) * 32]
 
 
-def after_kernel(base, gated, dz, h, oc, now_w, past_w, res_w, skip_w, *rest):
+def back_kernel(dz, past_w, back):
+    back[...] = dot_t(dz[tile_rows(), :], past_w[...]).astype(BF16)
+
+
+def results_kernel(gated, dz, h, oc, now_w, res_w, skip_w, *outs):
     rows = tile_rows()
-    results(base, gated[rows, :], dz[rows, :], h, oc, now_w, past_w, res_w, skip_w, *rest[2:])
+    results(0, gated[rows, :], dz[rows, :], h, oc, now_w, res_w, skip_w, *outs)
 
 
 def finish_kernel(part, came, *refs):
@@ -179,24 +178,6 @@
     return pltpu.with_memory_space_constraint(value, pltpu.HBM)
 
 
-def copy_rows_kernel(base, src, dst, sem):
-    copy = pltpu.make_async_copy(src.at[pl.ds(base, dst.shape[0]), :], dst, sem)
-    copy.start()
-    copy.wait()
-
-
-def copy_rows(value, base, rows):
-    return pl.pallas_call(
-        functools.partial(copy_rows_kernel, base),
-        out_shape=jax.ShapeDtypeStruct((rows, value.shape[1]), value.dtype),
-        in_specs=[pl.BlockSpec(memory_space=pl.ANY)],
-        out_specs=VMEM,
-        scratch_shapes=[pltpu.SemaphoreType.DMA],
-        cost_estimate=pl.CostEstimate(flops=0, bytes_accessed=1 << 20, transcendentals=0),
-        name="copy_rows",
-    )(in_hbm(value))
-
-
 def shift(value, steps):
     n = lax.axis_size("tm")
     return lax.ppermute(
@@ -231,12 +212,8 @@
     z = (dp // 2) % 8
     place = jnp.stack([dp % 2, z % 2, z // 2, dp // 16, dp % 4]).astype(jnp.int32)
     place, gate_bias = lax.optimization_barrier((place, gate_bias))
-    first, last = CHUNKS
     macs = 2 * total * width * width
-
-    d_first = shift(copy_rows(h, 0, first), 1)
-    d_last = shift(copy_rows(h, first, last), 1)
-
+    d = shift(history, 1)[0]
     z_now, dg = call(
         before_kernel,
         "before",
@@ -253,35 +230,22 @@
         ((total, width), BF16),
         ((total, width), BF16),
     ]
-    tail_out = lambda n: [((n, width), F32, 1), ((n, width), BF16)]
     block = lambda base: pl.BlockSpec((TILE, width), lambda i: (base // TILE + i, 0))
-    res, skip, part0, back0, g_taps, g_heads, g_bias = call(
-        first_kernel,
-        "first",
-        first // TILE,
-        (h, d_first, oc, sk, z_now, dg, now_w, past_w, res_w, skip_w),
-        [VMEM] * 10,
-        rows_out + tail_out(first) + sums,
-        [block(0)] * 4 + [VMEM] * 3,
-        macs * 28 * first // total,
-    )
     block_shape = (8, 12 * width + LANES)
     packed = (2, 4, 2, *block_shape)
-    came0 = shift(back0, -1)
     gated, dz, send0, send1, keep, *_ = call(
-        functools.partial(last_kernel, first),
-        "last",
-        last // TILE,
-        (place, h, d_last, oc, sk, z_now, dg, past_w, g_taps, g_heads, g_bias),
-        [pl.BlockSpec(memory_space=pltpu.SMEM)] + [VMEM] * 10,
-        [((last, 2 * width), BF16), ((last, 4 * width), BF16), (packed[1:], BF16), (packed[1:], BF16), (packed, F32)]
+        last_kernel,
+        "sums",
+        1,
+        (place, h, d, oc, sk, z_now, dg, past_w),
+        [pl.BlockSpec(memory_space=pltpu.SMEM)] + [VMEM] * 7,
+        [((total, 2 * width), BF16), ((total, 4 * width), BF16)]
+        + [(packed[1:], BF16), (packed[1:], BF16), (packed, F32)]
         + sums,
         [VMEM] * 8,
-        1 << 20,
-        {8: 5, 9: 6, 10: 7},
+        macs * 16,
     )
     halves = [exchange(v, "dp", lambda i: i ^ 1) for v in (send0, send1)]
-    *halves, came0 = lax.optimization_barrier((*halves, came0))
     smem = pl.BlockSpec(memory_space=pltpu.SMEM)
     step = lambda body, name, ins, outs, flops=1 << 20: call(
         body, name, 1, ins, [smem] * (ins[0] is place) + [VMEM] * (len(ins) - (ins[0] is place)), outs,
@@ -290,39 +254,44 @@
     keep, send = step(by_core_kernel, "by_core", (place, keep, *halves), [(packed[1:], F32), (packed[1:], BF16)])
     came = along_z(send, lambda z: z ^ 1)
     gated, dz, _ = lax.optimization_barrier((gated, dz, send))
-    res, skip, part1, back1 = call(
-        functools.partial(after_kernel, first),
-        "after",
-        last // TILE,
-        (gated, dz, h, oc, now_w, past_w, res_w, skip_w, res, skip),
-        [VMEM] * 8 + [pl.BlockSpec(memory_space=pl.ANY)] * 2,
-        rows_out + tail_out(last),
-        [block(first)] * 2 + [block(0)] * 2,
-        macs * 12 * last // total,
-        {8: 0, 9: 1},
-    )
-
+    (back,) = call(
+        back_kernel, "back", total // TILE, (dz, past_w), [VMEM] * 2, [((total, width), BF16)],
+        [block(0)], 1 << 20,
+    )
     own, *others = step(
         by_pair_kernel, "by_pair", (place, keep, came), [(packed[2:], F32)] + [(packed[2:], BF16)] * 3,
         macs * 1000,
     )
     one, two, three = (along_z(v, lambda z, k=k: (z + 2 * k) % 8) for k, v in enumerate(others, 1))
-    finish = lambda base, rows, ins, aliases: call(
-        finish_kernel, "finish", rows // TILE, ins,
-        [block(0)] * 2 + [pl.BlockSpec(memory_space=pl.ANY)] * len(aliases),
+    gated, dz, *_ = lax.optimization_barrier((gated, dz, back, *others))
+    res, skip, part = call(
+        results_kernel,
+        "results",
+        total // TILE,
+        (gated, dz, h, oc, now_w, res_w, skip_w),
+        [VMEM] * 7,
+        rows_out + [((total, width), F32, 1)],
+        [block(0)] * 3,
+        1 << 20,
+    )
+    one, two, three, part = lax.optimization_barrier((one, two, three, part))
+    moved = shift(back, -1)
+    half = total // 2
+    finish = lambda base, ins, aliases: call(
+        finish_kernel, "finish", half // TILE, ins,
+        [block(base)] * 2 + [pl.BlockSpec(memory_space=pl.ANY)] * len(aliases),
         [((total, width), BF16)], [block(base)], macs, aliases,
     )[0]
-    grad_in = finish(0, first, (part0, came0), {})
-    own, one, two, three, grad_in = lax.optimization_barrier((own, one, two, three, grad_in))
-    grad_in = finish(first, last, (part1, shift(back1, -1), grad_in), {2: 0})
+    first_half = finish(0, (part, moved), {})
     same, other = step(
         by_z_kernel, "by_z", (place, own, one, two, three), [(block_shape, BF16)] * 2
     )
-    (mine,) = step(
-        by_x_kernel, "by_x", (same, along_x(other, 1), along_x(same, 2), along_x(other, 3)), [(block_shape, BF16)]
-    )
+    xs = along_x(other, 1), along_x(same, 2), along_x(other, 3)
+    *xs, first_half = lax.optimization_barrier((*xs, first_half))
+    (mine,) = step(by_x_kernel, "by_x", (same, *xs), [(block_shape, BF16)])
+    grad_in_whole = finish(half, (part, moved, first_half), {2: 0})
     others = [along_y(mine, k) for k in (1, 2, 3)]
-    *others, grad_in = lax.optimization_barrier((*others, grad_in))
+    *others, grad_in = lax.optimization_barrier((*others, grad_in_whole))
     g_now, g_past, g_res, g_skip, g_bias = step(
         owner_kernel,
         "owner",

time: 89.6 us -> 91.5 us (1.021)
  local copies, waits for them, and re-layouts: 0.24 us -> 1.72 us
    ppermute x4 -> x2, waiting for transfers between devices: 11.3 us -> 17.4 us  [shift(): lax.ppermute(value, 'tm', [(s, s + steps) for s in range(max(0, -steps),...]
    ppermute x3, waiting for transfers between devices: 5.32 us -> 0.01 us  [along_x(): lax.ppermute(value, ('tm', 'dp'), [(i, target(i)) for i in range(256)])]
    ppermute x4 -> x2, starting transfers between devices: 10.9 us -> 6.28 us  [shift(): lax.ppermute(value, 'tm', [(s, s + steps) for s in range(max(0, -steps),...]
    ppermute x9, starting transfers between devices: 12.8 us -> 17.2 us  [exchange(): lax.ppermute(value, axis, [(i, partner(i)) for i in range(lax.axis_size(a...]
    pallas_call x2 -> x0, Pallas kernels: 3.69 us -> none  [copy_rows(): pl.pallas_call(functools.partial(copy_rows_kernel, base), out_shape=jax.S...]
    pallas_call x11, Pallas kernels: 23.9 us -> 26.8 us  [call(): pl.pallas_call(body, out_shape=[kind(s, t) for s, t, *_ in outs for kind...]
    unnamed x22, local copies, waits for them, and re-layouts: 0.15 us -> 1.63 us
    ppermute x3, starting transfers between devices: 4.98 us -> 6.01 us  [along_x(): lax.ppermute(value, ('tm', 'dp'), [(i, target(i)) for i in range(256)])]
  transfers between devices with their start and end apart: 16 -> 14, of which waited for: 14 -> 8; matrix products, arithmetic and copies ran while one was open for 0% -> 0% of each run, Pallas kernels for 27% -> 18%
where the time goes in v5:
time: 91.5 us; the launch traced here: 91.2 us
  waiting for transfers between devices  32.4 us (35%)
  starting transfers between devices  29.5 us (32%)
  Pallas kernels  26.8 us (29%)
  local copies, waits for them, and re-layouts  1.72 us (2%)
    pallas_call x11, Pallas kernels, call(): pl.pallas_call(body, out_shape=[kind(s, t) for s, t, *_ in outs for kind...  26.8 us
    ppermute x2, waiting for transfers between devices, shift(): lax.ppermute(value, 'tm', [(s, s + steps) for s in range(max(0, -steps),...  17.4 us
    ppermute x9, starting transfers between devices, exchange(): lax.ppermute(value, axis, [(i, partner(i)) for i in range(lax.axis_size(a...  17.2 us
    ppermute x9, waiting for transfers between devices, exchange(): lax.ppermute(value, axis, [(i, partner(i)) for i in range(lax.axis_size(a...  15 us
    ppermute x2, starting transfers between devices, shift(): lax.ppermute(value, 'tm', [(s, s + steps) for s in range(max(0, -steps),...  6.28 us
    ppermute x3, starting transfers between devices, along_x(): lax.ppermute(value, ('tm', 'dp'), [(i, target(i)) for i in range(256)])  6.01 us
  transfers between devices with their start and end apart: 14, of which 8 were waited for; matrix products, arithmetic and copies ran while one was open for 0% of the time, Pallas kernels for 18%

profile of v5, /device:TPU:64, one launch (start us, length us, event | category | flops | bytes accessed | tf_op | source)
XLA Modules:
  0.0 91.2 jit_solution(15184023446286767841)
XLA Ops:
  0.6 5.0 %collective-permute-start = (bf16[1,2048,256]{2,1,0:T(8,128)(2,1)}, bf16[1,2048,256]{2,1,0:T(8,128)(2,1)S(1)}, u32[]{:S(2)}, u32[]{:S(2)}) collective-permute-start(bf16[1,2048,256]{2,1,0:T(8,128)(2,1)} %param.8), channel_id=1, source_target_pairs={{0,32},{32,64},{64,96},{96,128},{128,160},{160,192},{192,224},{1,3... | collective-permute-start | bytes 3145736 | tf_op jit(solution)/shard_map/ppermute | solution.py:183
  5.7 0.1 stack.23.place
  5.8 0.0 copy-start.2
  5.8 0.0 copy-start.4
  5.8 0.0 copy-start.6
  5.8 0.0 copy-start.7
  5.8 5.1 %before.1 = (f32[2048,1024]{1,0:T(8,128)S(1)}, f32[2048,512]{1,0:T(8,128)S(1)}) custom-call(bf16[2048,256]{1,0:T(8,128)(2,1)} %bitcast.14, bf16[2048,256]{1,0:T(8,128)(2,1)} %bitcast.17, bf16[2048,256]{1,0:T(8,128)(2,1)} %bitcast.20, bf16[256,1024]{1,0:T(8,128)(2,1)} %now_w.3, f32[1,1024]{1,0:T(1,128)} %bitcast.26, bf16[512,256]{1,0:T(8,128)(2,1)} %res_w.3, ...), custom_call_target="tpu_custom_call" | custom-call | flops 2147483648 | bytes 4194304 | tf_op jit(solution)/shard_map/before/pallas_call | solution.py:162
  10.9 17.4 %collective-permute-done = bf16[1,2048,256]{2,1,0:T(8,128)(2,1)S(1)} collective-permute-done((bf16[1,2048,256]{2,1,0:T(8,128)(2,1)}, bf16[1,2048,256]{2,1,0:T(8,128)(2,1)S(1)}, u32[]{:S(2)}, u32[]{:S(2)}) %collective-permute-start) | collective-permute-done | bytes 1048608 | tf_op jit(solution)/shard_map/ppermute | solution.py:183
  28.3 0.0 copy-done.2
  28.3 0.0 copy-done.4
  28.3 0.0 copy-done.6
  28.3 0.0 copy-done.7
  28.3 8.2 %sums.1 = (bf16[2048,512]{1,0:T(8,128)(2,1)S(1)}, bf16[2048,1024]{1,0:T(8,128)(2,1)S(1)}, bf16[4,2,8,3200]{3,2,1,0:T(8,128)(2,1)S(1)}, bf16[4,2,8,3200]{3,2,1,0:...) custom-call(s32[5]{0:T(128)S(1)} %stack.23.place, ...), custom_call_target="tpu_custom_call" | custom-call | flops 4294967296 | bytes 8388608 | tf_op jit(solution)/shard_map/sums/pallas_call | solution.py:162
  36.5 0.0 collective-permute-start.1
  36.5 0.5 collective-permute-start.2
  37.0 1.2 %collective-permute-done.1.came0 = bf16[4,2,8,3200]{3,2,1,0:T(8,128)(2,1)S(1)} collective-permute-done((bf16[4,2,8,3200]{3,2,1,0:T(8,128)(2,1)S(1)}, bf16[4,2,8,3200]{3,2,1,0:T(8,128)(2,1)S(1)}, u32[]{:S(2)}, u32[]{:S(2)}) %collective-permute-start.1) | collective-permute-done | bytes 409632 | tf_op jit(solution)/shard_map/ppermute | solution.py:189
  38.2 0.6 collective-permute-done.2.came1
  38.8 0.7 by_core.1
  39.5 2.0 %collective-permute-start.3 = (bf16[4,2,8,3200]{3,2,1,0:T(8,128)(2,1)S(1)}, bf16[4,2,8,3200]{3,2,1,0:T(8,128)(2,1)S(1)}, u32[]{:S(2)}, u32[]{:S(2)}) collective-permute-start(bf16[4,2,8,3200]{3,2,1,0:T(8,128)(2,1)S(1)} %get-tuple-element.58), channel_id=1, source_target_pairs={{0,2},{1,3},{2,0},{3,1},{4,6},{5,7},{6,4},{7,5},{8,10},{9,11},{10,... | collective-permute-start | bytes 1228808 | tf_op jit(solution)/shard_map/ppermute | solution.py:189
  41.5 2.8 %back.1 = bf16[2048,256]{1,0:T(8,128)(2,1)} custom-call(bf16[2048,1024]{1,0:T(8,128)(2,1)S(1)} %get-tuple-element.66.dz, bf16[256,1024]{1,0:T(8,128)(2,1)S(1)} %copy-done.6), custom_call_target="tpu_custom_call" | custom-call | flops 1048576 | bytes 2048 | tf_op jit(solution)/shard_map/back/pallas_call | solution.py:162
  44.4 1.3 %collective-permute-start.10 = (bf16[2048,256]{1,0:T(8,128)(2,1)}, bf16[2048,256]{1,0:T(8,128)(2,1)}, u32[]{:S(2)}, u32[]{:S(2)}) collective-permute-start(bf16[2048,256]{1,0:T(8,128)(2,1)} %back.1), channel_id=1, source_target_pairs={{32,0},{64,32},{96,64},{128,96},{160,128},{192,160},{224,192},{33,... | collective-permute-start | bytes 3145736 | tf_op jit(solution)/shard_map/ppermute | solution.py:183
  45.6 5.6 %collective-permute-done.3.came = bf16[4,2,8,3200]{3,2,1,0:T(8,128)(2,1)S(1)} collective-permute-done((bf16[4,2,8,3200]{3,2,1,0:T(8,128)(2,1)S(1)}, bf16[4,2,8,3200]{3,2,1,0:T(8,128)(2,1)S(1)}, u32[]{:S(2)}, u32[]{:S(2)}) %collective-permute-start.3) | collective-permute-done | bytes 409632 | tf_op jit(solution)/shard_map/ppermute | solution.py:189
  51.3 0.0 copy-start.3
  51.3 0.0 copy-start.5
  51.3 0.0 copy-start.8
  51.3 0.0 copy-start.9
  51.3 0.0 copy-start.10
  51.3 0.6 by_pair.1
  51.9 4.4 %collective-permute-start.4 = (bf16[2,8,3200]{2,1,0:T(8,128)(2,1)S(1)}, bf16[2,8,3200]{2,1,0:T(8,128)(2,1)S(1)}, u32[]{:S(2)}, u32[]{:S(2)}) collective-permute-start(bf16[2,8,3200]{2,1,0:T(8,128)(2,1)S(1)} %get-tuple-element.62), channel_id=1, source_target_pairs={{0,4},{1,5},{2,6},{3,7},{4,8},{5,9},{6,10},{7,11},{8,12},{9,13},{1... | collective-permute-start | bytes 307208 | tf_op jit(solution)/shard_map/ppermute | solution.py:189
  56.3 1.0 %collective-permute-start.5 = (bf16[2,8,3200]{2,1,0:T(8,128)(2,1)S(1)}, bf16[2,8,3200]{2,1,0:T(8,128)(2,1)S(1)}, u32[]{:S(2)}, u32[]{:S(2)}) collective-permute-start(bf16[2,8,3200]{2,1,0:T(8,128)(2,1)S(1)} %get-tuple-element.63), channel_id=1, source_target_pairs={{0,8},{1,9},{2,10},{3,11},{4,12},{5,13},{6,14},{7,15},{8,0},{9,1},... | collective-permute-start | bytes 307208 | tf_op jit(solution)/shard_map/ppermute | solution.py:189
  57.3 2.8 %collective-permute-start.6 = (bf16[2,8,3200]{2,1,0:T(8,128)(2,1)S(1)}, bf16[2,8,3200]{2,1,0:T(8,128)(2,1)S(1)}, u32[]{:S(2)}, u32[]{:S(2)}) collective-permute-start(bf16[2,8,3200]{2,1,0:T(8,128)(2,1)S(1)} %get-tuple-element.64), channel_id=1, source_target_pairs={{0,12},{1,13},{2,14},{3,15},{4,0},{5,1},{6,2},{7,3},{8,4},{9,5},{1... | collective-permute-start | bytes 307208 | tf_op jit(solution)/shard_map/ppermute | solution.py:189
  60.2 0.0 copy-done.3
  60.2 0.0 copy-done.5
  60.2 0.0 copy-done.8
  60.2 0.0 copy-done.9
  60.2 0.0 copy-done.10
  60.2 3.8 %results.1 = (bf16[2048,256]{1,0:T(8,128)(2,1)}, bf16[2048,256]{1,0:T(8,128)(2,1)}, f32[2048,256]{1,0:T(8,128)}) custom-call(bf16[2048,512]{1,0:T(8,128)(2,1)S(1)} %get-tuple-element.65.gated, bf16[2048,1024]{1,0:T(8,128)(2,1)S(1)} %get-tuple-element.66.dz, bf16[2048,256]{1,0:T(8,128)(2,1)S(1)} %bitcast.16, bf16[2048,256]{1,0:T(8,128)(2,1)S(1)} %bitcast.19, ...), custom_call_target="tpu_custom_call" | custom-call | flops 1048576 | bytes 2048 | tf_op jit(solution)/shard_map/results/pallas_call | solution.py:162
  64.0 0.0 collective-permute-done.4.one
  64.0 2.7 %collective-permute-done.5.two = bf16[2,8,3200]{2,1,0:T(8,128)(2,1)S(1)} collective-permute-done((bf16[2,8,3200]{2,1,0:T(8,128)(2,1)S(1)}, bf16[2,8,3200]{2,1,0:T(8,128)(2,1)S(1)}, u32[]{:S(2)}, u32[]{:S(2)}) %collective-permute-start.5) | collective-permute-done | bytes 102432 | tf_op jit(solution)/shard_map/ppermute | solution.py:189
  66.7 2.0 %collective-permute-done.6.three = bf16[2,8,3200]{2,1,0:T(8,128)(2,1)S(1)} collective-permute-done((bf16[2,8,3200]{2,1,0:T(8,128)(2,1)S(1)}, bf16[2,8,3200]{2,1,0:T(8,128)(2,1)S(1)}, u32[]{:S(2)}, u32[]{:S(2)}) %collective-permute-start.6) | collective-permute-done | bytes 102432 | tf_op jit(solution)/shard_map/ppermute | solution.py:189
  68.7 0.6 by_z.1
  69.3 4.0 %collective-permute-start.8 = (bf16[8,3200]{1,0:T(8,128)(2,1)S(1)}, bf16[8,3200]{1,0:T(8,128)(2,1)S(1)}, u32[]{:S(2)}, u32[]{:S(2)}) collective-permute-start(bf16[8,3200]{1,0:T(8,128)(2,1)S(1)} %get-tuple-element.74.own), channel_id=1, source_target_pairs={{0,32},{1,33},{2,34},{3,35},{4,36},{5,37},{6,38},{7,39},{8,40},{9,... | collective-permute-start | bytes 153608 | tf_op jit(solution)/shard_map/ppermute | solution.py:205
  73.3 0.0 collective-permute-start.9
  73.3 2.0 %collective-permute-start.7 = (bf16[8,3200]{1,0:T(8,128)(2,1)S(1)}, bf16[8,3200]{1,0:T(8,128)(2,1)S(1)}, u32[]{:S(2)}, u32[]{:S(2)}) collective-permute-start(bf16[8,3200]{1,0:T(8,128)(2,1)S(1)} %get-tuple-element.75), channel_id=1, source_target_pairs={{0,16},{1,17},{2,18},{3,19},{4,20},{5,21},{6,22},{7,23},{8,24},{9,... | collective-permute-start | bytes 153608 | tf_op jit(solution)/shard_map/ppermute | solution.py:205
  75.4 0.0 collective-permute-done.10.came
  75.4 0.0 copy-start
  75.4 1.6 %copy-done = f32[2048,256]{1,0:T(8,128)S(1)} copy-done((f32[2048,256]{1,0:T(8,128)S(1)}, f32[2048,256]{1,0:T(8,128)}, u32[]{:S(2)}) %copy-start) | copy-done | bytes 2097176
  77.0 0.0 copy-start.1
  77.0 1.9 %finish.2.refs_0_ = bf16[2048,256]{1,0:T(8,128)(2,1)} custom-call(f32[2048,256]{1,0:T(8,128)S(1)} %copy-done, bf16[2048,256]{1,0:T(8,128)(2,1)} %collective-permute-done.10.came), custom_call_target="tpu_custom_call" | custom-call | flops 268435456 | bytes 524288 | tf_op jit(solution)/shard_map/finish/pallas_call | solution.py:162
  78.9 0.0 collective-permute-done.8.two
  78.9 0.0 collective-permute-done.9.three
  78.9 0.0 collective-permute-done.7.one
  78.9 4.9 %collective-permute-start.13 = (bf16[8,3200]{1,0:T(8,128)(2,1)S(1)}, bf16[8,3200]{1,0:T(8,128)(2,1)S(1)}, u32[]{:S(2)}, u32[]{:S(2)}) collective-permute-start(bf16[8,3200]{1,0:T(8,128)(2,1)S(1)} %by_x.1.own), channel_id=1, source_target_pairs={{0,192},{32,224},{64,0},{96,32},{128,64},{160,96},{192,128},{224,1... | collective-permute-start | bytes 153608 | tf_op jit(solution)/shard_map/ppermute | solution.py:189
  83.8 0.6 collective-permute-start.12
  84.4 1.0 %collective-permute-start.11 = (bf16[8,3200]{1,0:T(8,128)(2,1)S(1)}, bf16[8,3200]{1,0:T(8,128)(2,1)S(1)}, u32[]{:S(2)}, u32[]{:S(2)}) collective-permute-start(bf16[8,3200]{1,0:T(8,128)(2,1)S(1)} %by_x.1.own), channel_id=1, source_target_pairs={{0,64},{32,96},{64,128},{96,160},{128,192},{160,224},{192,0},{224,... | collective-permute-start | bytes 153608 | tf_op jit(solution)/shard_map/ppermute | solution.py:189
  85.4 0.0 copy-done.1
  85.4 1.8 %finish.3 = bf16[2048,256]{1,0:T(8,128)(2,1)} custom-call(f32[2048,256]{1,0:T(8,128)S(1)} %copy-done.1, bf16[2048,256]{1,0:T(8,128)(2,1)} %collective-permute-done.10.came, bf16[2048,256]{1,0:T(8,128)(2,1)} %finish.2.refs_0_), custom_call_target="tpu_custom_call", output_to_operand_aliasing={{}: (2, {})} | custom-call | flops 268435456 | bytes 524288 | tf_op jit(solution)/shard_map/finish/pallas_call | solution.py:162
  87.2 0.0 collective-permute-done.13.three
  87.2 2.2 %collective-permute-done.12.two = bf16[8,3200]{1,0:T(8,128)(2,1)S(1)} collective-permute-done((bf16[8,3200]{1,0:T(8,128)(2,1)S(1)}, bf16[8,3200]{1,0:T(8,128)(2,1)S(1)}, u32[]{:S(2)}, u32[]{:S(2)}) %collective-permute-start.12) | collective-permute-done | bytes 51232 | tf_op jit(solution)/shard_map/ppermute | solution.py:189
  89.5 0.5 collective-permute-done.11.one
  90.0 1.2 %owner.1 = (f32[8,1024]{1,0:T(8,128)}, f32[8,1024]{1,0:T(8,128)}, f32[16,256]{1,0:T(8,128)}, f32[16,256]{1,0:T(8,128)}, f32[1,32]{1,0:T(1,128)}) custom-call(s32[5]{0:T(128)S(1)} %stack.23.place, bf16[8,3200]{1,0:T(8,128)(2,1)S(1)} %by_x.1.own, bf16[8,3200]{1,0:T(8,128)(2,1)S(1)} %collective-permute-done.11.one, ...), custom_call_target="tpu_custom_call" | custom-call | flops 1048576 | bytes 2048 | tf_op jit(solution)/shard_map/owner/pallas_call | solution.py:162
  (1 shorter events, 0.0 us)
Async XLA Ops:
  0.6 27.7 %collective-permute-start = (bf16[1,2048,256]{2,1,0:T(8,128)(2,1)}, bf16[1,2048,256]{2,1,0:T(8,128)(2,1)S(1)}, u32[]{:S(2)}, u32[]{:S(2)}) collective-permute-start(bf16[1,2048,256]{2,1,0:T(8,128)(2,1)} %param.8), channel_id=1, source_target_pairs={{0,32},{32,64},{64,96},{96,128},{128,160},{160,192},{192,224},{1,3... | collective-permute-start | bytes 3145736 | tf_op jit(solution)/shard_map/ppermute | solution.py:183
  5.8 22.5 %copy-start.2 = (bf16[1,2048,256]{2,1,0:T(8,128)(2,1)S(1)}, bf16[1,2048,256]{2,1,0:T(8,128)(2,1)}, u32[]{:S(2)}) copy-start(bf16[1,2048,256]{2,1,0:T(8,128)(2,1)} %param.8) | copy-start | bytes 3145732
  5.8 22.5 %copy-start.4 = (bf16[1,2048,256]{2,1,0:T(8,128)(2,1)S(1)}, bf16[1,2048,256]{2,1,0:T(8,128)(2,1)}, u32[]{:S(2)}) copy-start(bf16[1,2048,256]{2,1,0:T(8,128)(2,1)} %param.14) | copy-start | bytes 3145732
  5.8 22.5 %copy-start.6 = (bf16[256,1024]{1,0:T(8,128)(2,1)S(1)}, bf16[256,1024]{1,0:T(8,128)(2,1)}, u32[]{:S(2)}) copy-start(bf16[256,1024]{1,0:T(8,128)(2,1)} %past_w.3) | copy-start | bytes 1572868
  5.8 22.5 %copy-start.7 = (bf16[1,2048,256]{2,1,0:T(8,128)(2,1)S(1)}, bf16[1,2048,256]{2,1,0:T(8,128)(2,1)}, u32[]{:S(2)}) copy-start(bf16[1,2048,256]{2,1,0:T(8,128)(2,1)} %param.15) | copy-start | bytes 3145732
  36.5 1.7 %collective-permute-start.1 = (bf16[4,2,8,3200]{3,2,1,0:T(8,128)(2,1)S(1)}, bf16[4,2,8,3200]{3,2,1,0:T(8,128)(2,1)S(1)}, u32[]{:S(2)}, u32[]{:S(2)}) collective-permute-start(bf16[4,2,8,3200]{3,2,1,0:T(8,128)(2,1)S(1)} %get-tuple-element.56), channel_id=1, source_target_pairs={{0,1},{1,0},{2,3},{3,2},{4,5},{5,4},{6,7},{7,6},{8,9},{9,8},{10,11... | collective-permute-start | bytes 1228808 | tf_op jit(solution)/shard_map/ppermute | solution.py:189
  36.5 2.3 %collective-permute-start.2 = (bf16[4,2,8,3200]{3,2,1,0:T(8,128)(2,1)S(1)}, bf16[4,2,8,3200]{3,2,1,0:T(8,128)(2,1)S(1)}, u32[]{:S(2)}, u32[]{:S(2)}) collective-permute-start(bf16[4,2,8,3200]{3,2,1,0:T(8,128)(2,1)S(1)} %get-tuple-element.57), channel_id=1, source_target_pairs={{0,1},{1,0},{2,3},{3,2},{4,5},{5,4},{6,7},{7,6},{8,9},{9,8},{10,11... | collective-permute-start | bytes 1228808 | tf_op jit(solution)/shard_map/ppermute | solution.py:189
  39.5 11.8 %collective-permute-start.3 = (bf16[4,2,8,3200]{3,2,1,0:T(8,128)(2,1)S(1)}, bf16[4,2,8,3200]{3,2,1,0:T(8,128)(2,1)S(1)}, u32[]{:S(2)}, u32[]{:S(2)}) collective-permute-start(bf16[4,2,8,3200]{3,2,1,0:T(8,128)(2,1)S(1)} %get-tuple-element.58), channel_id=1, source_target_pairs={{0,2},{1,3},{2,0},{3,1},{4,6},{5,7},{6,4},{7,5},{8,10},{9,11},{10,... | collective-permute-start | bytes 1228808 | tf_op jit(solution)/shard_map/ppermute | solution.py:189
  44.4 31.0 %collective-permute-start.10 = (bf16[2048,256]{1,0:T(8,128)(2,1)}, bf16[2048,256]{1,0:T(8,128)(2,1)}, u32[]{:S(2)}, u32[]{:S(2)}) collective-permute-start(bf16[2048,256]{1,0:T(8,128)(2,1)} %back.1), channel_id=1, source_target_pairs={{32,0},{64,32},{96,64},{128,96},{160,128},{192,160},{224,192},{33,... | collective-permute-start | bytes 3145736 | tf_op jit(solution)/shard_map/ppermute | solution.py:183
  51.3 8.9 %copy-start.3 = (bf16[1,2048,256]{2,1,0:T(8,128)(2,1)S(1)}, bf16[1,2048,256]{2,1,0:T(8,128)(2,1)}, u32[]{:S(2)}) copy-start(bf16[1,2048,256]{2,1,0:T(8,128)(2,1)} %param.8) | copy-start | bytes 3145732
  51.3 8.9 %copy-start.5 = (bf16[1,2048,256]{2,1,0:T(8,128)(2,1)S(1)}, bf16[1,2048,256]{2,1,0:T(8,128)(2,1)}, u32[]{:S(2)}) copy-start(bf16[1,2048,256]{2,1,0:T(8,128)(2,1)} %param.14) | copy-start | bytes 3145732
  51.3 8.9 %copy-start.8 = (bf16[256,1024]{1,0:T(8,128)(2,1)S(1)}, bf16[256,1024]{1,0:T(8,128)(2,1)}, u32[]{:S(2)}) copy-start(bf16[256,1024]{1,0:T(8,128)(2,1)} %now_w.3) | copy-start | bytes 1572868
  51.3 8.9 %copy-start.9 = (bf16[512,256]{1,0:T(8,128)(2,1)S(1)}, bf16[512,256]{1,0:T(8,128)(2,1)}, u32[]{:S(2)}) copy-start(bf16[512,256]{1,0:T(8,128)(2,1)} %res_w.3) | copy-start | bytes 786436
  51.3 8.9 %copy-start.10 = (bf16[512,256]{1,0:T(8,128)(2,1)S(1)}, bf16[512,256]{1,0:T(8,128)(2,1)}, u32[]{:S(2)}) copy-start(bf16[512,256]{1,0:T(8,128)(2,1)} %skip_w.3) | copy-start | bytes 786436
  51.9 12.1 %collective-permute-start.4 = (bf16[2,8,3200]{2,1,0:T(8,128)(2,1)S(1)}, bf16[2,8,3200]{2,1,0:T(8,128)(2,1)S(1)}, u32[]{:S(2)}, u32[]{:S(2)}) collective-permute-start(bf16[2,8,3200]{2,1,0:T(8,128)(2,1)S(1)} %get-tuple-element.62), channel_id=1, source_target_pairs={{0,4},{1,5},{2,6},{3,7},{4,8},{5,9},{6,10},{7,11},{8,12},{9,13},{1... | collective-permute-start | bytes 307208 | tf_op jit(solution)/shard_map/ppermute | solution.py:189
  56.3 10.4 %collective-permute-start.5 = (bf16[2,8,3200]{2,1,0:T(8,128)(2,1)S(1)}, bf16[2,8,3200]{2,1,0:T(8,128)(2,1)S(1)}, u32[]{:S(2)}, u32[]{:S(2)}) collective-permute-start(bf16[2,8,3200]{2,1,0:T(8,128)(2,1)S(1)} %get-tuple-element.63), channel_id=1, source_target_pairs={{0,8},{1,9},{2,10},{3,11},{4,12},{5,13},{6,14},{7,15},{8,0},{9,1},... | collective-permute-start | bytes 307208 | tf_op jit(solution)/shard_map/ppermute | solution.py:189
  57.3 11.4 %collective-permute-start.6 = (bf16[2,8,3200]{2,1,0:T(8,128)(2,1)S(1)}, bf16[2,8,3200]{2,1,0:T(8,128)(2,1)S(1)}, u32[]{:S(2)}, u32[]{:S(2)}) collective-permute-start(bf16[2,8,3200]{2,1,0:T(8,128)(2,1)S(1)} %get-tuple-element.64), channel_id=1, source_target_pairs={{0,12},{1,13},{2,14},{3,15},{4,0},{5,1},{6,2},{7,3},{8,4},{9,5},{1... | collective-permute-start | bytes 307208 | tf_op jit(solution)/shard_map/ppermute | solution.py:189
  69.3 9.5 %collective-permute-start.8 = (bf16[8,3200]{1,0:T(8,128)(2,1)S(1)}, bf16[8,3200]{1,0:T(8,128)(2,1)S(1)}, u32[]{:S(2)}, u32[]{:S(2)}) collective-permute-start(bf16[8,3200]{1,0:T(8,128)(2,1)S(1)} %get-tuple-element.74.own), channel_id=1, source_target_pairs={{0,32},{1,33},{2,34},{3,35},{4,36},{5,37},{6,38},{7,39},{8,40},{9,... | collective-permute-start | bytes 153608 | tf_op jit(solution)/shard_map/ppermute | solution.py:205
  73.3 5.6 %collective-permute-start.9 = (bf16[8,3200]{1,0:T(8,128)(2,1)S(1)}, bf16[8,3200]{1,0:T(8,128)(2,1)S(1)}, u32[]{:S(2)}, u32[]{:S(2)}) collective-permute-start(bf16[8,3200]{1,0:T(8,128)(2,1)S(1)} %get-tuple-element.75), channel_id=1, source_target_pairs={{0,48},{1,49},{2,50},{3,51},{4,52},{5,53},{6,54},{7,55},{8,56},{9,... | collective-permute-start | bytes 153608 | tf_op jit(solution)/shard_map/ppermute | solution.py:205
  73.3 5.6 %collective-permute-start.7 = (bf16[8,3200]{1,0:T(8,128)(2,1)S(1)}, bf16[8,3200]{1,0:T(8,128)(2,1)S(1)}, u32[]{:S(2)}, u32[]{:S(2)}) collective-permute-start(bf16[8,3200]{1,0:T(8,128)(2,1)S(1)} %get-tuple-element.75), channel_id=1, source_target_pairs={{0,16},{1,17},{2,18},{3,19},{4,20},{5,21},{6,22},{7,23},{8,24},{9,... | collective-permute-start | bytes 153608 | tf_op jit(solution)/shard_map/ppermute | solution.py:205
  75.4 1.6 %copy-start = (f32[2048,256]{1,0:T(8,128)S(1)}, f32[2048,256]{1,0:T(8,128)}, u32[]{:S(2)}) copy-start(f32[2048,256]{1,0:T(8,128)} %get-tuple-element.76.part) | copy-start | bytes 6291460
  77.0 8.5 %copy-start.1 = (f32[2048,256]{1,0:T(8,128)S(1)}, f32[2048,256]{1,0:T(8,128)}, u32[]{:S(2)}) copy-start(f32[2048,256]{1,0:T(8,128)} %get-tuple-element.76.part) | copy-start | bytes 6291460
  78.9 8.3 %collective-permute-start.13 = (bf16[8,3200]{1,0:T(8,128)(2,1)S(1)}, bf16[8,3200]{1,0:T(8,128)(2,1)S(1)}, u32[]{:S(2)}, u32[]{:S(2)}) collective-permute-start(bf16[8,3200]{1,0:T(8,128)(2,1)S(1)} %by_x.1.own), channel_id=1, source_target_pairs={{0,192},{32,224},{64,0},{96,32},{128,64},{160,96},{192,128},{224,1... | collective-permute-start | bytes 153608 | tf_op jit(solution)/shard_map/ppermute | solution.py:189
  83.8 5.6 %collective-permute-start.12 = (bf16[8,3200]{1,0:T(8,128)(2,1)S(1)}, bf16[8,3200]{1,0:T(8,128)(2,1)S(1)}, u32[]{:S(2)}, u32[]{:S(2)}) collective-permute-start(bf16[8,3200]{1,0:T(8,128)(2,1)S(1)} %by_x.1.own), channel_id=1, source_target_pairs={{0,128},{32,160},{64,192},{96,224},{128,0},{160,32},{192,64},{224,... | collective-permute-start | bytes 153608 | tf_op jit(solution)/shard_map/ppermute | solution.py:189
  84.4 5.5 %collective-permute-start.11 = (bf16[8,3200]{1,0:T(8,128)(2,1)S(1)}, bf16[8,3200]{1,0:T(8,128)(2,1)S(1)}, u32[]{:S(2)}, u32[]{:S(2)}) collective-permute-start(bf16[8,3200]{1,0:T(8,128)(2,1)S(1)} %by_x.1.own), channel_id=1, source_target_pairs={{0,64},{32,96},{64,128},{96,160},{128,192},{160,224},{192,0},{224,... | collective-permute-start | bytes 153608 | tf_op jit(solution)/shard_map/ppermute | solution.py:189

commit v6 on v3

--- a/solution.py
+++ b/solution.py
@@ -318,11 +318,10 @@
     same, other = step(
         by_z_kernel, "by_z", (place, own, one, two, three), [(block_shape, BF16)] * 2
     )
-    (mine,) = step(
-        by_x_kernel, "by_x", (same, along_x(other, 1), along_x(same, 2), along_x(other, 3)), [(block_shape, BF16)]
-    )
+    xs = along_x(other, 1), along_x(same, 2), along_x(other, 3)
+    *xs, grad_in = lax.optimization_barrier((*xs, grad_in))
+    (mine,) = step(by_x_kernel, "by_x", (same, *xs), [(block_shape, BF16)])
     others = [along_y(mine, k) for k in (1, 2, 3)]
-    *others, grad_in = lax.optimization_barrier((*others, grad_in))
     g_now, g_past, g_res, g_skip, g_bias = step(
         owner_kernel,
         "owner",

time: 89.6 us -> 89.5 us (level)
  the two profiles are of different devices: /device:TPU:64 before, /device:TPU:6 now
where the time goes in v6:
time: 89.5 us; the launch traced here: 89.2 us
  starting transfers between devices  40 us (45%)
  Pallas kernels  27.6 us (31%)
  waiting for transfers between devices  20.5 us (23%)
    pallas_call x11, Pallas kernels, call(): pl.pallas_call(body, out_shape=[kind(s, t) for s, t, *_ in outs for kind...  23.9 us
    ppermute x9, starting transfers between devices, exchange(): lax.ppermute(value, axis, [(i, partner(i)) for i in range(lax.axis_size(a...  19.7 us
    ppermute x4, starting transfers between devices, shift(): lax.ppermute(value, 'tm', [(s, s + steps) for s in range(max(0, -steps),...  13.6 us
    ppermute x4, waiting for transfers between devices, shift(): lax.ppermute(value, 'tm', [(s, s + steps) for s in range(max(0, -steps),...  10.7 us
    ppermute x9, waiting for transfers between devices, exchange(): lax.ppermute(value, axis, [(i, partner(i)) for i in range(lax.axis_size(a...  9.37 us
    ppermute x3, starting transfers between devices, along_x(): lax.ppermute(value, ('tm', 'dp'), [(i, target(i)) for i in range(256)])  6.72 us
    pallas_call x2, Pallas kernels, copy_rows(): pl.pallas_call(functools.partial(copy_rows_kernel, base), out_shape=jax.S...  3.69 us
  transfers between devices with their start and end apart: 16, of which 11 were waited for; matrix products, arithmetic and copies ran while one was open for 0% of the time, Pallas kernels for 27%

profile of v6, /device:TPU:6, one launch (start us, length us, event | category | flops | bytes accessed | tf_op | source)
XLA Modules:
  0.0 89.2 jit_solution(14759301406575712323)
XLA Ops:
  0.6 1.8 %copy_rows.3 = bf16[1024,256]{1,0:T(8,128)(2,1)} custom-call(bf16[2048,256]{1,0:T(8,128)(2,1)} %bitcast.13), custom_call_target="tpu_custom_call" | custom-call | bytes 1048576 | tf_op jit(solution)/shard_map/copy_rows/pallas_call | solution.py:189
  2.5 4.3 %collective-permute-start.1 = (bf16[1024,256]{1,0:T(8,128)(2,1)}, bf16[1024,256]{1,0:T(8,128)(2,1)S(1)}, u32[]{:S(2)}, u32[]{:S(2)}) collective-permute-start(bf16[1024,256]{1,0:T(8,128)(2,1)} %copy_rows.3), channel_id=1, source_target_pairs={{0,32},{32,64},{64,96},{96,128},{128,160},{160,192},{192,224},{1,3... | collective-permute-start | bytes 1572872 | tf_op jit(solution)/shard_map/ppermute | solution.py:202
  6.8 1.8 %copy_rows.2 = bf16[1024,256]{1,0:T(8,128)(2,1)} custom-call(bf16[2048,256]{1,0:T(8,128)(2,1)} %bitcast.14), custom_call_target="tpu_custom_call" | custom-call | bytes 1048576 | tf_op jit(solution)/shard_map/copy_rows/pallas_call | solution.py:189
  8.7 4.0 %collective-permute-start = (bf16[1024,256]{1,0:T(8,128)(2,1)}, bf16[1024,256]{1,0:T(8,128)(2,1)S(1)}, u32[]{:S(2)}, u32[]{:S(2)}) collective-permute-start(bf16[1024,256]{1,0:T(8,128)(2,1)} %copy_rows.2), channel_id=1, source_target_pairs={{0,32},{32,64},{64,96},{96,128},{128,160},{160,192},{192,224},{1,3... | collective-permute-start | bytes 1572872 | tf_op jit(solution)/shard_map/ppermute | solution.py:202
  12.8 0.1 stack.23.place
  12.9 0.0 copy-start
  12.9 0.0 copy-start.1
  12.9 0.0 copy-start.2
  12.9 0.0 copy-start.3
  12.9 0.0 copy-start.4
  12.9 0.0 copy-start.5
  12.9 0.0 copy-start.6
  12.9 5.0 %before.1 = (f32[2048,1024]{1,0:T(8,128)S(1)}, f32[2048,512]{1,0:T(8,128)S(1)}) custom-call(bf16[2048,256]{1,0:T(8,128)(2,1)} %bitcast.15, bf16[2048,256]{1,0:T(8,128)(2,1)} %bitcast.19, bf16[2048,256]{1,0:T(8,128)(2,1)} %bitcast.23, bf16[256,1024]{1,0:T(8,128)(2,1)} %now_w.5, f32[1,1024]{1,0:T(1,128)} %bitcast.29, bf16[512,256]{1,0:T(8,128)(2,1)} %res_w.5, ...), custom_call_target="tpu_custom_call" | custom-call | flops 2147483648 | bytes 4194304 | tf_op jit(solution)/shard_map/before/pallas_call | solution.py:163
  18.0 2.9 %collective-permute-done.1.d = bf16[1024,256]{1,0:T(8,128)(2,1)S(1)} collective-permute-done((bf16[1024,256]{1,0:T(8,128)(2,1)}, bf16[1024,256]{1,0:T(8,128)(2,1)S(1)}, u32[]{:S(2)}, u32[]{:S(2)}) %collective-permute-start.1) | collective-permute-done | bytes 524320 | tf_op jit(solution)/shard_map/ppermute | solution.py:202
  20.9 0.0 copy-done
  20.9 0.0 copy-done.1
  20.9 0.0 copy-done.2
  20.9 0.0 copy-done.3
  20.9 0.0 copy-done.4
  20.9 0.0 copy-done.5
  20.9 0.0 copy-done.6
  21.0 6.0 %first.1 = (bf16[2048,256]{1,0:T(8,128)(2,1)}, bf16[2048,256]{1,0:T(8,128)(2,1)}, f32[1024,256]{1,0:T(8,128)}, bf16[1024,256]{1,0:T(8,128)(2,1)S(1)}, f32[512,10...) custom-call(bf16[2048,256]{1,0:T(8,128)(2,1)S(1)} %bitcast.16, ...), custom_call_target="tpu_custom_call" | custom-call | flops 3758096384 | bytes 7340032 | tf_op jit(solution)/shard_map/first/pallas_call | solution.py:163
  27.0 1.9 %collective-permute-start.4 = (bf16[1024,256]{1,0:T(8,128)(2,1)S(1)}, bf16[1024,256]{1,0:T(8,128)(2,1)S(1)}, u32[]{:S(2)}, u32[]{:S(2)}) collective-permute-start(bf16[1024,256]{1,0:T(8,128)(2,1)S(1)} %get-tuple-element.67), channel_id=1, source_target_pairs={{32,0},{64,32},{96,64},{128,96},{160,128},{192,160},{224,192},{33,... | collective-permute-start | bytes 1572872 | tf_op jit(solution)/shard_map/ppermute | solution.py:202
  28.9 2.1 %collective-permute-done.d = bf16[1024,256]{1,0:T(8,128)(2,1)S(1)} collective-permute-done((bf16[1024,256]{1,0:T(8,128)(2,1)}, bf16[1024,256]{1,0:T(8,128)(2,1)S(1)}, u32[]{:S(2)}, u32[]{:S(2)}) %collective-permute-start) | collective-permute-done | bytes 524320 | tf_op jit(solution)/shard_map/ppermute | solution.py:202
  31.0 4.1 %last.1 = (bf16[1024,512]{1,0:T(8,128)(2,1)S(1)}, bf16[1024,1024]{1,0:T(8,128)(2,1)S(1)}, bf16[4,2,8,3200]{3,2,1,0:T(8,128)(2,1)S(1)}, bf16[4,2,8,3200]{3,2,1,0:...) custom-call(s32[5]{0:T(128)S(1)} %stack.23.place, ...), custom_call_target="tpu_custom_call", output_to_operand_aliasing={{5}: (8, {}), {6}: (9, {}), {7}: (10, {})} | custom-call | flops 1048576 | bytes 2048 | tf_op jit(solution)/shard_map/last/pallas_call | solution.py:163
  35.1 0.1 collective-permute-start.2
  35.2 0.5 collective-permute-start.3
  35.7 1.2 %collective-permute-done.2.came0 = bf16[4,2,8,3200]{3,2,1,0:T(8,128)(2,1)S(1)} collective-permute-done((bf16[4,2,8,3200]{3,2,1,0:T(8,128)(2,1)S(1)}, bf16[4,2,8,3200]{3,2,1,0:T(8,128)(2,1)S(1)}, u32[]{:S(2)}, u32[]{:S(2)}) %collective-permute-start.2) | collective-permute-done | bytes 409632 | tf_op jit(solution)/shard_map/ppermute | solution.py:208
  37.0 0.6 collective-permute-done.3.came1
  37.5 5.7 %collective-permute-done.4.came = bf16[1024,256]{1,0:T(8,128)(2,1)S(1)} collective-permute-done((bf16[1024,256]{1,0:T(8,128)(2,1)S(1)}, bf16[1024,256]{1,0:T(8,128)(2,1)S(1)}, u32[]{:S(2)}, u32[]{:S(2)}) %collective-permute-start.4) | collective-permute-done | bytes 524320 | tf_op jit(solution)/shard_map/ppermute | solution.py:202
  43.2 0.7 by_core.1
  43.9 0.1 copy-done.9
  44.0 1.9 %collective-permute-start.5 = (bf16[4,2,8,3200]{3,2,1,0:T(8,128)(2,1)S(1)}, bf16[4,2,8,3200]{3,2,1,0:T(8,128)(2,1)S(1)}, u32[]{:S(2)}, u32[]{:S(2)}) collective-permute-start(bf16[4,2,8,3200]{3,2,1,0:T(8,128)(2,1)S(1)} %get-tuple-element.70), channel_id=1, source_target_pairs={{0,2},{1,3},{2,0},{3,1},{4,6},{5,7},{6,4},{7,5},{8,10},{9,11},{10,... | collective-permute-start | bytes 1228808 | tf_op jit(solution)/shard_map/ppermute | solution.py:208
  46.0 2.9 %after.1 = (bf16[2048,256]{1,0:T(8,128)(2,1)}, bf16[2048,256]{1,0:T(8,128)(2,1)}, f32[1024,256]{1,0:T(8,128)}, bf16[1024,256]{1,0:T(8,128)(2,1)}) custom-call(bf16[1024,512]{1,0:T(8,128)(2,1)S(1)} %get-tuple-element.71.gated, bf16[1024,1024]{1,0:T(8,128)(2,1)S(1)} %get-tuple-element.72.dz, ...), custom_call_target="tpu_custom_call", output_to_operand_aliasing={{0}: (8, {}), {1}: (9, {})} | custom-call | flops 1610612736 | bytes 3145728 | tf_op jit(solution)/shard_map/after/pallas_call | solution.py:163
  48.9 3.3 %collective-permute-start.12 = (bf16[1024,256]{1,0:T(8,128)(2,1)}, bf16[1024,256]{1,0:T(8,128)(2,1)}, u32[]{:S(2)}, u32[]{:S(2)}) collective-permute-start(bf16[1024,256]{1,0:T(8,128)(2,1)} %get-tuple-element.91), channel_id=1, source_target_pairs={{32,0},{64,32},{96,64},{128,96},{160,128},{192,160},{224,192},{33,... | collective-permute-start | bytes 1572872 | tf_op jit(solution)/shard_map/ppermute | solution.py:202
  52.2 0.6 collective-permute-done.5.came
  52.8 0.6 by_pair.1
  53.4 0.0 copy-start.7
  53.5 3.3 %collective-permute-start.6 = (bf16[2,8,3200]{2,1,0:T(8,128)(2,1)S(1)}, bf16[2,8,3200]{2,1,0:T(8,128)(2,1)S(1)}, u32[]{:S(2)}, u32[]{:S(2)}) collective-permute-start(bf16[2,8,3200]{2,1,0:T(8,128)(2,1)S(1)} %get-tuple-element.79), channel_id=1, source_target_pairs={{0,4},{1,5},{2,6},{3,7},{4,8},{5,9},{6,10},{7,11},{8,12},{9,13},{1... | collective-permute-start | bytes 307208 | tf_op jit(solution)/shard_map/ppermute | solution.py:208
  56.8 5.2 %collective-permute-start.7 = (bf16[2,8,3200]{2,1,0:T(8,128)(2,1)S(1)}, bf16[2,8,3200]{2,1,0:T(8,128)(2,1)S(1)}, u32[]{:S(2)}, u32[]{:S(2)}) collective-permute-start(bf16[2,8,3200]{2,1,0:T(8,128)(2,1)S(1)} %get-tuple-element.80), channel_id=1, source_target_pairs={{0,8},{1,9},{2,10},{3,11},{4,12},{5,13},{6,14},{7,15},{8,0},{9,1},... | collective-permute-start | bytes 307208 | tf_op jit(solution)/shard_map/ppermute | solution.py:208
  62.0 2.7 %collective-permute-start.8 = (bf16[2,8,3200]{2,1,0:T(8,128)(2,1)S(1)}, bf16[2,8,3200]{2,1,0:T(8,128)(2,1)S(1)}, u32[]{:S(2)}, u32[]{:S(2)}) collective-permute-start(bf16[2,8,3200]{2,1,0:T(8,128)(2,1)S(1)} %get-tuple-element.81), channel_id=1, source_target_pairs={{0,12},{1,13},{2,14},{3,15},{4,0},{5,1},{6,2},{7,3},{8,4},{9,5},{1... | collective-permute-start | bytes 307208 | tf_op jit(solution)/shard_map/ppermute | solution.py:208
  64.7 0.0 copy-done.8
  64.7 0.0 copy-done.10
  64.7 0.8 finish.2.refs_0_
  65.5 0.0 collective-permute-done.6.one
  65.5 2.2 %collective-permute-done.7.two = bf16[2,8,3200]{2,1,0:T(8,128)(2,1)S(1)} collective-permute-done((bf16[2,8,3200]{2,1,0:T(8,128)(2,1)S(1)}, bf16[2,8,3200]{2,1,0:T(8,128)(2,1)S(1)}, u32[]{:S(2)}, u32[]{:S(2)}) %collective-permute-start.7) | collective-permute-done | bytes 102432 | tf_op jit(solution)/shard_map/ppermute | solution.py:208
  67.7 0.7 collective-permute-done.8.three
  68.4 0.6 by_z.1
  69.1 0.8 collective-permute-start.11
  69.8 2.5 %collective-permute-start.9 = (bf16[8,3200]{1,0:T(8,128)(2,1)S(1)}, bf16[8,3200]{1,0:T(8,128)(2,1)S(1)}, u32[]{:S(2)}, u32[]{:S(2)}) collective-permute-start(bf16[8,3200]{1,0:T(8,128)(2,1)S(1)} %get-tuple-element.88), channel_id=1, source_target_pairs={{0,16},{1,17},{2,18},{3,19},{4,20},{5,21},{6,22},{7,23},{8,24},{9,... | collective-permute-start | bytes 153608 | tf_op jit(solution)/shard_map/ppermute | solution.py:224
  72.4 3.4 %collective-permute-start.10 = (bf16[8,3200]{1,0:T(8,128)(2,1)S(1)}, bf16[8,3200]{1,0:T(8,128)(2,1)S(1)}, u32[]{:S(2)}, u32[]{:S(2)}) collective-permute-start(bf16[8,3200]{1,0:T(8,128)(2,1)S(1)} %get-tuple-element.89.own), channel_id=1, source_target_pairs={{0,32},{1,33},{2,34},{3,35},{4,36},{5,37},{6,38},{7,39},{8,40},{9,... | collective-permute-start | bytes 153608 | tf_op jit(solution)/shard_map/ppermute | solution.py:224
  75.8 0.0 collective-permute-done.12.came
  75.8 0.0 copy-done.7
  75.8 1.8 %finish.3 = bf16[2048,256]{1,0:T(8,128)(2,1)} custom-call(f32[1024,256]{1,0:T(8,128)S(1)} %copy-done.7, bf16[1024,256]{1,0:T(8,128)(2,1)} %collective-permute-done.12.came, bf16[2048,256]{1,0:T(8,128)(2,1)} %finish.2.refs_0_), custom_call_target="tpu_custom_call", output_to_operand_aliasing={{}: (2, {})} | custom-call | flops 268435456 | bytes 524288 | tf_op jit(solution)/shard_map/finish/pallas_call | solution.py:163
  77.6 0.0 collective-permute-done.11.three
  77.6 0.0 collective-permute-done.9.one
  77.6 0.4 collective-permute-done.10.two
  78.0 2.2 %collective-permute-start.15 = (bf16[8,3200]{1,0:T(8,128)(2,1)S(1)}, bf16[8,3200]{1,0:T(8,128)(2,1)S(1)}, u32[]{:S(2)}, u32[]{:S(2)}) collective-permute-start(bf16[8,3200]{1,0:T(8,128)(2,1)S(1)} %by_x.1.own), channel_id=1, source_target_pairs={{0,192},{32,224},{64,0},{96,32},{128,64},{160,96},{192,128},{224,1... | collective-permute-start | bytes 153608 | tf_op jit(solution)/shard_map/ppermute | solution.py:208
  80.2 2.4 %collective-permute-start.14 = (bf16[8,3200]{1,0:T(8,128)(2,1)S(1)}, bf16[8,3200]{1,0:T(8,128)(2,1)S(1)}, u32[]{:S(2)}, u32[]{:S(2)}) collective-permute-start(bf16[8,3200]{1,0:T(8,128)(2,1)S(1)} %by_x.1.own), channel_id=1, source_target_pairs={{0,128},{32,160},{64,192},{96,224},{128,0},{160,32},{192,64},{224,... | collective-permute-start | bytes 153608 | tf_op jit(solution)/shard_map/ppermute | solution.py:208
  82.6 1.3 %collective-permute-start.13 = (bf16[8,3200]{1,0:T(8,128)(2,1)S(1)}, bf16[8,3200]{1,0:T(8,128)(2,1)S(1)}, u32[]{:S(2)}, u32[]{:S(2)}) collective-permute-start(bf16[8,3200]{1,0:T(8,128)(2,1)S(1)} %by_x.1.own), channel_id=1, source_target_pairs={{0,64},{32,96},{64,128},{96,160},{128,192},{160,224},{192,0},{224,... | collective-permute-start | bytes 153608 | tf_op jit(solution)/shard_map/ppermute | solution.py:208
  84.0 0.0 collective-permute-done.15.three
  84.0 1.9 %collective-permute-done.14.two = bf16[8,3200]{1,0:T(8,128)(2,1)S(1)} collective-permute-done((bf16[8,3200]{1,0:T(8,128)(2,1)S(1)}, bf16[8,3200]{1,0:T(8,128)(2,1)S(1)}, u32[]{:S(2)}, u32[]{:S(2)}) %collective-permute-start.14) | collective-permute-done | bytes 51232 | tf_op jit(solution)/shard_map/ppermute | solution.py:208
  85.8 2.1 %collective-permute-done.13.one = bf16[8,3200]{1,0:T(8,128)(2,1)S(1)} collective-permute-done((bf16[8,3200]{1,0:T(8,128)(2,1)S(1)}, bf16[8,3200]{1,0:T(8,128)(2,1)S(1)}, u32[]{:S(2)}, u32[]{:S(2)}) %collective-permute-start.13) | collective-permute-done | bytes 51232 | tf_op jit(solution)/shard_map/ppermute | solution.py:208
  88.0 1.2 %owner.1 = (f32[8,1024]{1,0:T(8,128)}, f32[8,1024]{1,0:T(8,128)}, f32[16,256]{1,0:T(8,128)}, f32[16,256]{1,0:T(8,128)}, f32[1,32]{1,0:T(1,128)}) custom-call(s32[5]{0:T(128)S(1)} %stack.23.place, bf16[8,3200]{1,0:T(8,128)(2,1)S(1)} %by_x.1.own, bf16[8,3200]{1,0:T(8,128)(2,1)S(1)} %collective-permute-done.13.one, ...), custom_call_target="tpu_custom_call" | custom-call | flops 1048576 | bytes 2048 | tf_op jit(solution)/shard_map/owner/pallas_call | solution.py:163
  (4 shorter events, 0.0 us)
Async XLA Ops:
  2.5 18.4 %collective-permute-start.1 = (bf16[1024,256]{1,0:T(8,128)(2,1)}, bf16[1024,256]{1,0:T(8,128)(2,1)S(1)}, u32[]{:S(2)}, u32[]{:S(2)}) collective-permute-start(bf16[1024,256]{1,0:T(8,128)(2,1)} %copy_rows.3), channel_id=1, source_target_pairs={{0,32},{32,64},{64,96},{96,128},{128,160},{160,192},{192,224},{1,3... | collective-permute-start | bytes 1572872 | tf_op jit(solution)/shard_map/ppermute | solution.py:202
  8.7 22.3 %collective-permute-start = (bf16[1024,256]{1,0:T(8,128)(2,1)}, bf16[1024,256]{1,0:T(8,128)(2,1)S(1)}, u32[]{:S(2)}, u32[]{:S(2)}) collective-permute-start(bf16[1024,256]{1,0:T(8,128)(2,1)} %copy_rows.2), channel_id=1, source_target_pairs={{0,32},{32,64},{64,96},{96,128},{128,160},{160,192},{192,224},{1,3... | collective-permute-start | bytes 1572872 | tf_op jit(solution)/shard_map/ppermute | solution.py:202
  12.9 8.0 %copy-start = (bf16[1,2048,256]{2,1,0:T(8,128)(2,1)S(1)}, bf16[1,2048,256]{2,1,0:T(8,128)(2,1)}, u32[]{:S(2)}) copy-start(bf16[1,2048,256]{2,1,0:T(8,128)(2,1)} %param.8) | copy-start | bytes 3145732
  12.9 8.0 %copy-start.1 = (bf16[1,2048,256]{2,1,0:T(8,128)(2,1)S(1)}, bf16[1,2048,256]{2,1,0:T(8,128)(2,1)}, u32[]{:S(2)}) copy-start(bf16[1,2048,256]{2,1,0:T(8,128)(2,1)} %param.14) | copy-start | bytes 3145732
  12.9 8.0 %copy-start.2 = (bf16[256,1024]{1,0:T(8,128)(2,1)S(1)}, bf16[256,1024]{1,0:T(8,128)(2,1)}, u32[]{:S(2)}) copy-start(bf16[256,1024]{1,0:T(8,128)(2,1)} %past_w.5) | copy-start | bytes 1572868
  12.9 8.0 %copy-start.3 = (bf16[1,2048,256]{2,1,0:T(8,128)(2,1)S(1)}, bf16[1,2048,256]{2,1,0:T(8,128)(2,1)}, u32[]{:S(2)}) copy-start(bf16[1,2048,256]{2,1,0:T(8,128)(2,1)} %param.15) | copy-start | bytes 3145732
  12.9 8.0 %copy-start.4 = (bf16[256,1024]{1,0:T(8,128)(2,1)S(1)}, bf16[256,1024]{1,0:T(8,128)(2,1)}, u32[]{:S(2)}) copy-start(bf16[256,1024]{1,0:T(8,128)(2,1)} %now_w.5) | copy-start | bytes 1572868
  12.9 8.0 %copy-start.5 = (bf16[512,256]{1,0:T(8,128)(2,1)S(1)}, bf16[512,256]{1,0:T(8,128)(2,1)}, u32[]{:S(2)}) copy-start(bf16[512,256]{1,0:T(8,128)(2,1)} %res_w.5) | copy-start | bytes 786436
  12.9 8.0 %copy-start.6 = (bf16[512,256]{1,0:T(8,128)(2,1)S(1)}, bf16[512,256]{1,0:T(8,128)(2,1)}, u32[]{:S(2)}) copy-start(bf16[512,256]{1,0:T(8,128)(2,1)} %skip_w.5) | copy-start | bytes 786436
  27.0 16.2 %collective-permute-start.4 = (bf16[1024,256]{1,0:T(8,128)(2,1)S(1)}, bf16[1024,256]{1,0:T(8,128)(2,1)S(1)}, u32[]{:S(2)}, u32[]{:S(2)}) collective-permute-start(bf16[1024,256]{1,0:T(8,128)(2,1)S(1)} %get-tuple-element.67), channel_id=1, source_target_pairs={{32,0},{64,32},{96,64},{128,96},{160,128},{192,160},{224,192},{33,... | collective-permute-start | bytes 1572872 | tf_op jit(solution)/shard_map/ppermute | solution.py:202
  35.1 1.8 %collective-permute-start.2 = (bf16[4,2,8,3200]{3,2,1,0:T(8,128)(2,1)S(1)}, bf16[4,2,8,3200]{3,2,1,0:T(8,128)(2,1)S(1)}, u32[]{:S(2)}, u32[]{:S(2)}) collective-permute-start(bf16[4,2,8,3200]{3,2,1,0:T(8,128)(2,1)S(1)} %get-tuple-element.65), channel_id=1, source_target_pairs={{0,1},{1,0},{2,3},{3,2},{4,5},{5,4},{6,7},{7,6},{8,9},{9,8},{10,11... | collective-permute-start | bytes 1228808 | tf_op jit(solution)/shard_map/ppermute | solution.py:208
  35.2 2.3 %collective-permute-start.3 = (bf16[4,2,8,3200]{3,2,1,0:T(8,128)(2,1)S(1)}, bf16[4,2,8,3200]{3,2,1,0:T(8,128)(2,1)S(1)}, u32[]{:S(2)}, u32[]{:S(2)}) collective-permute-start(bf16[4,2,8,3200]{3,2,1,0:T(8,128)(2,1)S(1)} %get-tuple-element.66), channel_id=1, source_target_pairs={{0,1},{1,0},{2,3},{3,2},{4,5},{5,4},{6,7},{7,6},{8,9},{9,8},{10,11... | collective-permute-start | bytes 1228808 | tf_op jit(solution)/shard_map/ppermute | solution.py:208
  43.2 0.8 copy-start.9
  44.0 8.8 %collective-permute-start.5 = (bf16[4,2,8,3200]{3,2,1,0:T(8,128)(2,1)S(1)}, bf16[4,2,8,3200]{3,2,1,0:T(8,128)(2,1)S(1)}, u32[]{:S(2)}, u32[]{:S(2)}) collective-permute-start(bf16[4,2,8,3200]{3,2,1,0:T(8,128)(2,1)S(1)} %get-tuple-element.70), channel_id=1, source_target_pairs={{0,2},{1,3},{2,0},{3,1},{4,6},{5,7},{6,4},{7,5},{8,10},{9,11},{10,... | collective-permute-start | bytes 1228808 | tf_op jit(solution)/shard_map/ppermute | solution.py:208
  48.9 26.9 %collective-permute-start.12 = (bf16[1024,256]{1,0:T(8,128)(2,1)}, bf16[1024,256]{1,0:T(8,128)(2,1)}, u32[]{:S(2)}, u32[]{:S(2)}) collective-permute-start(bf16[1024,256]{1,0:T(8,128)(2,1)} %get-tuple-element.91), channel_id=1, source_target_pairs={{32,0},{64,32},{96,64},{128,96},{160,128},{192,160},{224,192},{33,... | collective-permute-start | bytes 1572872 | tf_op jit(solution)/shard_map/ppermute | solution.py:202
  52.8 11.9 %copy-start.8 = (f32[1024,256]{1,0:T(8,128)S(1)}, f32[1024,256]{1,0:T(8,128)}, u32[]{:S(2)}) copy-start(f32[1024,256]{1,0:T(8,128)} %get-tuple-element.82.part) | copy-start | bytes 3145732
  52.8 11.9 %copy-start.10 = (bf16[1024,256]{1,0:T(8,128)(2,1)S(1)}, bf16[1024,256]{1,0:T(8,128)(2,1)}, u32[]{:S(2)}) copy-start(bf16[1024,256]{1,0:T(8,128)(2,1)} %copy-done.9) | copy-start | bytes 1572868
  53.4 22.3 %copy-start.7 = (f32[1024,256]{1,0:T(8,128)S(1)}, f32[1024,256]{1,0:T(8,128)}, u32[]{:S(2)}) copy-start(f32[1024,256]{1,0:T(8,128)} %get-tuple-element.90.part) | copy-start | bytes 3145732
  53.5 12.1 %collective-permute-start.6 = (bf16[2,8,3200]{2,1,0:T(8,128)(2,1)S(1)}, bf16[2,8,3200]{2,1,0:T(8,128)(2,1)S(1)}, u32[]{:S(2)}, u32[]{:S(2)}) collective-permute-start(bf16[2,8,3200]{2,1,0:T(8,128)(2,1)S(1)} %get-tuple-element.79), channel_id=1, source_target_pairs={{0,4},{1,5},{2,6},{3,7},{4,8},{5,9},{6,10},{7,11},{8,12},{9,13},{1... | collective-permute-start | bytes 307208 | tf_op jit(solution)/shard_map/ppermute | solution.py:208
  56.8 10.9 %collective-permute-start.7 = (bf16[2,8,3200]{2,1,0:T(8,128)(2,1)S(1)}, bf16[2,8,3200]{2,1,0:T(8,128)(2,1)S(1)}, u32[]{:S(2)}, u32[]{:S(2)}) collective-permute-start(bf16[2,8,3200]{2,1,0:T(8,128)(2,1)S(1)} %get-tuple-element.80), channel_id=1, source_target_pairs={{0,8},{1,9},{2,10},{3,11},{4,12},{5,13},{6,14},{7,15},{8,0},{9,1},... | collective-permute-start | bytes 307208 | tf_op jit(solution)/shard_map/ppermute | solution.py:208
  62.0 6.4 %collective-permute-start.8 = (bf16[2,8,3200]{2,1,0:T(8,128)(2,1)S(1)}, bf16[2,8,3200]{2,1,0:T(8,128)(2,1)S(1)}, u32[]{:S(2)}, u32[]{:S(2)}) collective-permute-start(bf16[2,8,3200]{2,1,0:T(8,128)(2,1)S(1)} %get-tuple-element.81), channel_id=1, source_target_pairs={{0,12},{1,13},{2,14},{3,15},{4,0},{5,1},{6,2},{7,3},{8,4},{9,5},{1... | collective-permute-start | bytes 307208 | tf_op jit(solution)/shard_map/ppermute | solution.py:208
  69.1 8.5 %collective-permute-start.11 = (bf16[8,3200]{1,0:T(8,128)(2,1)S(1)}, bf16[8,3200]{1,0:T(8,128)(2,1)S(1)}, u32[]{:S(2)}, u32[]{:S(2)}) collective-permute-start(bf16[8,3200]{1,0:T(8,128)(2,1)S(1)} %get-tuple-element.88), channel_id=1, source_target_pairs={{0,48},{1,49},{2,50},{3,51},{4,52},{5,53},{6,54},{7,55},{8,56},{9,... | collective-permute-start | bytes 153608 | tf_op jit(solution)/shard_map/ppermute | solution.py:224
  69.8 7.7 %collective-permute-start.9 = (bf16[8,3200]{1,0:T(8,128)(2,1)S(1)}, bf16[8,3200]{1,0:T(8,128)(2,1)S(1)}, u32[]{:S(2)}, u32[]{:S(2)}) collective-permute-start(bf16[8,3200]{1,0:T(8,128)(2,1)S(1)} %get-tuple-element.88), channel_id=1, source_target_pairs={{0,16},{1,17},{2,18},{3,19},{4,20},{5,21},{6,22},{7,23},{8,24},{9,... | collective-permute-start | bytes 153608 | tf_op jit(solution)/shard_map/ppermute | solution.py:224
  72.4 5.6 %collective-permute-start.10 = (bf16[8,3200]{1,0:T(8,128)(2,1)S(1)}, bf16[8,3200]{1,0:T(8,128)(2,1)S(1)}, u32[]{:S(2)}, u32[]{:S(2)}) collective-permute-start(bf16[8,3200]{1,0:T(8,128)(2,1)S(1)} %get-tuple-element.89.own), channel_id=1, source_target_pairs={{0,32},{1,33},{2,34},{3,35},{4,36},{5,37},{6,38},{7,39},{8,40},{9,... | collective-permute-start | bytes 153608 | tf_op jit(solution)/shard_map/ppermute | solution.py:224
  78.0 5.9 %collective-permute-start.15 = (bf16[8,3200]{1,0:T(8,128)(2,1)S(1)}, bf16[8,3200]{1,0:T(8,128)(2,1)S(1)}, u32[]{:S(2)}, u32[]{:S(2)}) collective-permute-start(bf16[8,3200]{1,0:T(8,128)(2,1)S(1)} %by_x.1.own), channel_id=1, source_target_pairs={{0,192},{32,224},{64,0},{96,32},{128,64},{160,96},{192,128},{224,1... | collective-permute-start | bytes 153608 | tf_op jit(solution)/shard_map/ppermute | solution.py:208
  80.2 5.6 %collective-permute-start.14 = (bf16[8,3200]{1,0:T(8,128)(2,1)S(1)}, bf16[8,3200]{1,0:T(8,128)(2,1)S(1)}, u32[]{:S(2)}, u32[]{:S(2)}) collective-permute-start(bf16[8,3200]{1,0:T(8,128)(2,1)S(1)} %by_x.1.own), channel_id=1, source_target_pairs={{0,128},{32,160},{64,192},{96,224},{128,0},{160,32},{192,64},{224,... | collective-permute-start | bytes 153608 | tf_op jit(solution)/shard_map/ppermute | solution.py:208
  82.6 5.3 %collective-permute-start.13 = (bf16[8,3200]{1,0:T(8,128)(2,1)S(1)}, bf16[8,3200]{1,0:T(8,128)(2,1)S(1)}, u32[]{:S(2)}, u32[]{:S(2)}) collective-permute-start(bf16[8,3200]{1,0:T(8,128)(2,1)S(1)} %by_x.1.own), channel_id=1, source_target_pairs={{0,64},{32,96},{64,128},{96,160},{128,192},{160,224},{192,0},{224,... | collective-permute-start | bytes 153608 | tf_op jit(solution)/shard_map/ppermute | solution.py:208
